TPU v7x, 256 devices: a whole 4x4x8 slice. The times are simulated.
256 devices in a mesh: seq: 32 (over z, x_hi, core), chan: 8 (over y, x_lo).
Axes of the slice: x: 4 (x_hi: 2, x_lo: 2; x = x_hi * 2 + x_lo), y: 4, z: 8, core: 2. Of those that a mesh axis runs over, the one named last changes fastest.
Arguments:
- inputs: bfloat16 [131072, 2048], P('seq', 'chan'), may hold values from -6 to 6
- twiddle: float32 [256, 512], P('seq'), may hold values from -4 to 4
- right_factor: bfloat16 [512, 512], replicated, may hold values from -0.25 to 0.25
- left_factor: bfloat16 [256, 256], replicated, may hold values from -0.375 to 0.375
- blocks: bfloat16 [2048, 512], P('chan'), may hold values from -0.25 to 0.25
- block_mixer: float32 [512, 4, 4], replicated, may hold values from -3 to 3
- out_grad: bfloat16 [131072, 2048], P('seq', 'chan'), may hold values from -6 to 6
Outputs:
- output: bfloat16 [131072, 2048], P('seq', 'chan')
- input_grad: bfloat16 [131072, 2048], P('seq', 'chan')
All inputs are finite; a program needn't handle non-finite values.
Results may differ from a plain program's by a relative error of at most 0.0076.
Values may be sent and summed in bfloat16 or wider, within the bound.
No kernel may reach another device: no remote copies, remote signals or barrier semaphores. Data moves between devices by JAX's collectives and lax.ppermute only.
A program may use at most 128 MiB of HBM per device.

v0:
```python
import jax
import jax.numpy as jnp
from jax import lax
from jax.sharding import PartitionSpec as P


def seq_pass(values, left_matrix):
    mixed_cols = jnp.einsum(
        "ia,ajc->ijc",
        left_matrix,
        lax.all_to_all(values, "seq", split_axis=1, concat_axis=0, tiled=True),
        preferred_element_type=jnp.float32,
    ).astype(jnp.bfloat16)
    return lax.all_to_all(mixed_cols, "seq", split_axis=0, concat_axis=1, tiled=True)


def send_back(values):
    return (
        lax.all_to_all(values[0], "chan", split_axis=2, concat_axis=1, tiled=True),
        lax.all_to_all(values[1], "chan", split_axis=2, concat_axis=1, tiled=True),
    )


def gate_of(values, rows_all, block_mixer):
    row_count, length, full_width = values.shape
    block_width = rows_all.shape[1]
    block_count = full_width // block_width
    block_table = rows_all.reshape(block_count, block_width, block_width)
    split = values.reshape(row_count, length, block_count, block_width)
    middle = jnp.einsum(
        "nbpq,pkq->nbpk", split, block_table, preferred_element_type=jnp.float32
    ).astype(jnp.bfloat16)
    gate = jnp.einsum(
        "nbpk,kop->nbok", middle.astype(jnp.float32), block_mixer, precision=lax.Precision.HIGHEST
    )
    return gate.reshape(row_count, length, full_width).astype(jnp.bfloat16)


def grad_of(values, rows_all, block_mixer):
    row_count, length, full_width = values.shape
    block_width = rows_all.shape[1]
    block_count = full_width // block_width
    block_table = rows_all.reshape(block_count, block_width, block_width)
    split = values.reshape(row_count, length, block_count, block_width).astype(jnp.float32)
    grad_middle = jnp.einsum(
        "nbok,kop->nbpk", split, block_mixer, precision=lax.Precision.HIGHEST
    ).astype(jnp.bfloat16)
    chan_grad = jnp.einsum(
        "nbpk,pkq->nbpq", grad_middle, block_table, preferred_element_type=jnp.float32
    )
    return chan_grad.reshape(row_count, length, full_width).astype(jnp.bfloat16)


def local(inputs, twiddle, right_factor, left_factor, blocks, block_mixer, out_grad):
    outer_rows, inner_len = twiddle.shape
    local_chan = inputs.shape[1]
    values = inputs.reshape(outer_rows, inner_len, local_chan)
    grad_values = out_grad.reshape(outer_rows, inner_len, local_chan)
    rows_all = lax.all_gather(blocks, "chan", axis=0, tiled=True)
    first_section = jnp.einsum(
        "jb,abc->ajc", right_factor, values, preferred_element_type=jnp.float32
    )
    twisted = (first_section * twiddle[:, :, None]).astype(jnp.bfloat16)
    mixed = seq_pass(twisted, left_factor)
    mixed_wide = mixed.astype(jnp.float32)
    grad_wide = grad_values.astype(jnp.float32)
    grad_gate = (grad_wide * mixed_wide).astype(jnp.bfloat16)
    gate, chan_grad = send_back(
        (
            gate_of(
                lax.all_to_all(values, "chan", split_axis=1, concat_axis=2, tiled=True),
                rows_all,
                block_mixer,
            ),
            grad_of(
                lax.all_to_all(grad_gate, "chan", split_axis=1, concat_axis=2, tiled=True),
                rows_all,
                block_mixer,
            ),
        )
    )
    gate_wide = gate.astype(jnp.float32)
    output = (gate_wide * mixed_wide).astype(jnp.bfloat16)
    grad_mixed = (grad_wide * gate_wide).astype(jnp.bfloat16)
    grad_twisted = seq_pass(grad_mixed, left_factor.T)
    grad_first = (grad_twisted.astype(jnp.float32) * twiddle[:, :, None]).astype(jnp.bfloat16)
    seq_grad = jnp.einsum(
        "jb,ajc->abc", right_factor, grad_first, preferred_element_type=jnp.float32
    )
    input_grad = (seq_grad + chan_grad.astype(jnp.float32)).astype(jnp.bfloat16)
    total_rows = outer_rows * inner_len
    return (output.reshape(total_rows, local_chan), input_grad.reshape(total_rows, local_chan))


def solution(mesh):
    return jax.shard_map(
        local,
        mesh=mesh,
        in_specs=(
            P("seq", "chan"),
            P("seq", None),
            P(),
            P(),
            P("chan", None),
            P(),
            P("seq", "chan"),
        ),
        out_specs=(P("seq", "chan"), P("seq", "chan")),
        check_vma=False,
    )
```

profile of v0, /device:TPU:1, one launch (start us, length us, event | category | flops | bytes accessed | tf_op | source)
XLA Modules:
  0.0 430.2 jit_solution(8274621310463001034)
XLA Ops:
  7.2 4.2 copy.132
  11.3 6.1 %all-to-all-start = ((bf16[8,512,256]{2,0,1:T(8,128)(2,1)}), bf16[8,512,256]{2,0,1:T(8,128)(2,1)S(1)}, u32[]{:S(2)}, u32[]{:S(2)}) async-start(bf16[8,512,256]{2,0,1:T(8,128)(2,1)} %copy.132), calls=%async_computation | async-start | bytes 4194304 | tf_op jit(solution)/shard_map/all_to_all | solution.py:71
  18.2 4.2 fusion.19
  22.4 4.5 %copy.143 = bf16[8,512,256]{2,0,1:T(8,128)(2,1)} copy(bf16[8,512,256]{1,2,0:T(8,128)(2,1)} %fusion.19) | data formatting | bytes 4194304 | tf_op jit(solution)/shard_map/convert_element_type | solution.py:63
  26.9 21.5 %all-to-all-done = bf16[8,512,256]{2,0,1:T(8,128)(2,1)S(1)} async-done(((bf16[8,512,256]{2,0,1:T(8,128)(2,1)}), bf16[8,512,256]{2,0,1:T(8,128)(2,1)S(1)}, u32[]{:S(2)}, u32[]{:S(2)}) %all-to-all-start) | async-done | bytes 2097184 | tf_op jit(solution)/shard_map/all_to_all | solution.py:71
  48.4 17.2 %all-to-all-start.2 = ((bf16[8,512,256]{2,0,1:T(8,128)(2,1)}), bf16[8,512,256]{2,0,1:T(8,128)(2,1)}, u32[]{:S(2)}, u32[]{:S(2)}) async-start(bf16[8,512,256]{2,0,1:T(8,128)(2,1)} %copy.143), calls=%async_computation.2 | async-start | bytes 4194304 | tf_op jit(solution)/shard_map/all_to_all | solution.py:11
  74.4 30.2 %all-gather.2.cloned.1.call-done = bf16[2048,512]{1,0:T(8,128)(2,1)} async-done(((bf16[256,512]{1,0:T(8,128)(2,1)}), bf16[2048,512]{1,0:T(8,128)(2,1)}) %all-gather.2.cloned.1.call-update) | async-done | bytes 2097168 | tf_op jit(solution)/shard_map/all_gather | solution.py:59
  108.4 5.5 %copy.136 = bf16[8,64,4,512]{1,2,0,3:T(4,128)(2,1)} copy(bf16[8,64,4,512]{3,1,0,2:T(8,128)(2,1)S(1)} %convert_bitcast_fusion.5) | data formatting | bytes 4194304 | tf_op jit(solution)/shard_map/convert_element_type | solution.py:32
  113.9 9.6 %fusion.7 = bf16[8,64,4,512]{1,2,0,3:T(4,128)(2,1)S(1)} fusion(bf16[8,64,4,512]{1,2,0,3:T(4,128)(2,1)} %copy.136, f32[512,4,4,1]{1,2,3,0:T(4,128)} %copy.172), kind=kOutput, calls=%fused_computation.19 | convolution fusion | flops 51380224 | bytes 4227072 | tf_op jit(solution)/shard_map/nbpk,kop->nbok/dot_general | solution.py:33
  126.1 7.8 %reshape.82 = bf16[8,2,65536]{2,1,0:T(2,128)(2,1)} reshape(bf16[2048,8,64]{2,1,0:T(8,128)(2,1)} %bitcast.122) | data formatting | bytes 4194304
  142.8 4.5 %copy.147 = bf16[256,16,256]{2,1,0:T(8,128)(2,1)} copy(bf16[256,16,256]{0,2,1:T(8,128)(2,1)} %convert_bitcast_fusion.4) | data formatting | bytes 4194304 | tf_op jit(solution)/shard_map/convert_element_type | solution.py:13
  147.3 16.5 %all-to-all-done.1 = bf16[8,2,65536]{2,1,0:T(2,128)(2,1)S(1)} async-done(((bf16[8,2,65536]{2,1,0:T(2,128)(2,1)}), bf16[8,2,65536]{2,1,0:T(2,128)(2,1)S(1)}, u32[]{:S(2)}, u32[]{:S(2)}) %all-to-all-start.1) | async-done | bytes 2097184 | tf_op jit(solution)/shard_map/all_to_all | solution.py:19
  163.8 13.6 %all-to-all-start.3 = ((bf16[256,16,256]{2,1,0:T(8,128)(2,1)}), bf16[256,16,256]{2,1,0:T(8,128)(2,1)}, u32[]{:S(2)}, u32[]{:S(2)}) async-start(bf16[256,16,256]{2,1,0:T(8,128)(2,1)} %copy.147), calls=%async_computation.3 | async-start | bytes 4194304 | tf_op jit(solution)/shard_map/all_to_all | solution.py:14
  177.3 5.0 %reshape.83 = bf16[2048,8,64]{2,1,0:T(8,128)(2,1)} reshape(bf16[8,2,65536]{2,1,0:T(2,128)(2,1)S(1)} %all-to-all-done.1) | data formatting | bytes 4194304
  182.3 4.5 %copy.140 = bf16[8,64,2048]{2,1,0:T(8,128)(2,1)S(1)} copy(bf16[8,64,2048]{1,0,2:T(8,128)(2,1)} %bitcast.118) | data formatting | bytes 4194304 | tf_op jit(solution)/shard_map/all_to_all | solution.py:19
  190.8 36.7 %all-to-all-done.3 = bf16[256,16,256]{2,1,0:T(8,128)(2,1)} async-done(((bf16[256,16,256]{2,1,0:T(8,128)(2,1)}), bf16[256,16,256]{2,1,0:T(8,128)(2,1)}, u32[]{:S(2)}, u32[]{:S(2)}) %all-to-all-start.3) | async-done | bytes 2097184 | tf_op jit(solution)/shard_map/all_to_all | solution.py:14
  238.1 4.4 %all-to-all-start.6 = ((bf16[8,512,256]{2,0,1:T(8,128)(2,1)}), bf16[8,512,256]{2,0,1:T(8,128)(2,1)}, u32[]{:S(2)}, u32[]{:S(2)}) async-start(bf16[8,512,256]{2,0,1:T(8,128)(2,1)} %copy.158), calls=%async_computation.6 | async-start | bytes 4194304 | tf_op jit(solution)/shard_map/all_to_all | solution.py:76
  245.0 24.1 %all-to-all-done.6 = bf16[8,512,256]{2,0,1:T(8,128)(2,1)} async-done(((bf16[8,512,256]{2,0,1:T(8,128)(2,1)}), bf16[8,512,256]{2,0,1:T(8,128)(2,1)}, u32[]{:S(2)}, u32[]{:S(2)}) %all-to-all-start.6) | async-done | bytes 2097184 | tf_op jit(solution)/shard_map/all_to_all | solution.py:76
  269.0 7.8 %all-to-all-start.4 = ((bf16[8,512,256]{2,0,1:T(8,128)(2,1)}), bf16[8,512,256]{2,0,1:T(8,128)(2,1)}, u32[]{:S(2)}, u32[]{:S(2)}) async-start(bf16[8,512,256]{2,0,1:T(8,128)(2,1)} %copy.150), calls=%async_computation.4 | async-start | bytes 4194304 | tf_op jit(solution)/shard_map/all_to_all | solution.py:11
  284.1 5.9 %copy.160 = bf16[8,64,4,512]{1,2,0,3:T(4,128)(2,1)} copy(bf16[8,64,4,512]{3,2,1,0:T(4,128)(2,1)S(1)} %reshape.60) | data formatting | bytes 4194304 | tf_op jit(solution)/shard_map/reshape | solution.py:44
  290.0 9.3 %fusion.8 = bf16[8,64,4,512]{1,2,0,3:T(4,128)(2,1)S(1)} fusion(bf16[8,64,4,512]{1,2,0,3:T(4,128)(2,1)} %copy.160, f32[512,4,4,1]{1,2,3,0:T(4,128)} %copy.172), kind=kOutput, calls=%fused_computation.20 | convolution fusion | flops 51380224 | bytes 4227072 | tf_op jit(solution)/shard_map/nbok,kop->nbpk/dot_general | solution.py:45
  302.5 4.4 %copy.182 = bf16[8,64,4,512]{1,0,3,2:T(8,128)(2,1)} copy(bf16[8,64,4,512]{3,1,0,2:T(8,128)(2,1)S(1)} %convert_bitcast_fusion.2) | data formatting | bytes 4194304 | tf_op jit(solution)/shard_map/convert_element_type | solution.py:51
  306.8 7.6 %reshape.84 = bf16[8,2,65536]{2,1,0:T(2,128)(2,1)} reshape(bf16[2048,8,64]{2,1,0:T(8,128)(2,1)} %bitcast.119) | data formatting | bytes 4194304
  314.4 12.4 %all-to-all-done.4 = bf16[8,512,256]{2,0,1:T(8,128)(2,1)} async-done(((bf16[8,512,256]{2,0,1:T(8,128)(2,1)}), bf16[8,512,256]{2,0,1:T(8,128)(2,1)}, u32[]{:S(2)}, u32[]{:S(2)}) %all-to-all-start.4) | async-done | bytes 2097184 | tf_op jit(solution)/shard_map/all_to_all | solution.py:11
  335.8 4.6 %copy.154 = bf16[256,16,256]{2,1,0:T(8,128)(2,1)} copy(bf16[256,16,256]{0,2,1:T(8,128)(2,1)} %convert_bitcast_fusion.3) | data formatting | bytes 4194304 | tf_op jit(solution)/shard_map/convert_element_type | solution.py:13
  340.4 16.7 %all-to-all-done.7 = bf16[8,2,65536]{2,1,0:T(2,128)(2,1)S(1)} async-done(((bf16[8,2,65536]{2,1,0:T(2,128)(2,1)}), bf16[8,2,65536]{2,1,0:T(2,128)(2,1)S(1)}, u32[]{:S(2)}, u32[]{:S(2)}) %all-to-all-start.7) | async-done | bytes 2097184 | tf_op jit(solution)/shard_map/all_to_all | solution.py:20
  357.1 7.2 %all-to-all-start.5 = ((bf16[256,16,256]{2,1,0:T(8,128)(2,1)}), bf16[256,16,256]{2,1,0:T(8,128)(2,1)}, u32[]{:S(2)}, u32[]{:S(2)}) async-start(bf16[256,16,256]{2,1,0:T(8,128)(2,1)} %copy.154), calls=%async_computation.5 | async-start | bytes 4194304 | tf_op jit(solution)/shard_map/all_to_all | solution.py:14
  364.3 5.2 %fusion.4 = bf16[4096,256]{1,0:T(8,128)(2,1)} fusion(f32[8,32,16,256]{3,2,1,0:T(8,128)} %copy-done.2, f32[8,8,64,256]{3,2,1,0:T(8,128)} %copy.141), kind=kLoop, calls=%fused_computation.15 | loop fusion | flops 2097152 | bytes 10485760 | tf_op jit(solution)/shard_map/convert_element_type | solution.py:83
  369.6 5.0 %reshape.85 = bf16[2048,8,64]{2,1,0:T(8,128)(2,1)} reshape(bf16[8,2,65536]{2,1,0:T(2,128)(2,1)S(1)} %all-to-all-done.7) | data formatting | bytes 4194304
  374.5 4.5 %copy.165 = bf16[8,64,2048]{2,1,0:T(8,128)(2,1)S(1)} copy(bf16[8,64,2048]{1,0,2:T(8,128)(2,1)} %bitcast.120) | data formatting | bytes 4194304 | tf_op jit(solution)/shard_map/all_to_all | solution.py:20
  383.1 5.3 %copy.167 = f32[8,512,256]{1,2,0:T(8,128)} copy(f32[8,512,256]{2,1,0:T(8,128)} %bitcast.125) | data formatting | bytes 8388608 | tf_op jit(solution)/shard_map/convert_element_type | solution.py:90
  388.4 26.0 %all-to-all-done.5 = bf16[256,16,256]{2,1,0:T(8,128)(2,1)} async-done(((bf16[256,16,256]{2,1,0:T(8,128)(2,1)}), bf16[256,16,256]{2,1,0:T(8,128)(2,1)}, u32[]{:S(2)}, u32[]{:S(2)}) %all-to-all-start.5) | async-done | bytes 2097184 | tf_op jit(solution)/shard_map/all_to_all | solution.py:14
  (53 shorter events, 73.9 us)
Async XLA Ops:
  7.2 11.0 %copy-start = (bf16[512,512]{1,0:T(8,128)(2,1)S(1)}, bf16[512,512]{1,0:T(8,128)(2,1)}, u32[]{:S(2)}) copy-start(bf16[512,512]{1,0:T(8,128)(2,1)} %param.9) | copy-start | bytes 1572868
  11.3 6.8 %copy-start.8 = (f32[8,512]{1,0:T(8,128)S(1)}, f32[8,512]{1,0:T(8,128)}, u32[]{:S(2)}) copy-start(f32[8,512]{1,0:T(8,128)} %param.8) | copy-start | bytes 49156
  11.3 37.0 %all-to-all-start = ((bf16[8,512,256]{2,0,1:T(8,128)(2,1)}), bf16[8,512,256]{2,0,1:T(8,128)(2,1)S(1)}, u32[]{:S(2)}, u32[]{:S(2)}) async-start(bf16[8,512,256]{2,0,1:T(8,128)(2,1)} %copy.132), calls=%async_computation | async-start | bytes 4194304 | tf_op jit(solution)/shard_map/all_to_all | solution.py:71
  17.4 87.2 %all-gather.2.cloned.1.call-start = ((), (), s32[]{:S(2)}) async-start(), calls=%async_computation.8 | async-start | bytes 2359296 | tf_op jit(solution)/shard_map/all_gather | solution.py:59
  26.9 38.7 %copy-start.7 = (f32[512,4,4]{0,2,1:T(4,128)S(1)}, f32[512,4,4]{0,2,1:T(4,128)}, u32[]{:S(2)}) copy-start(f32[512,4,4]{0,2,1:T(4,128)} %param.12) | copy-start | bytes 98308
  48.4 85.5 %all-to-all-start.2 = ((bf16[8,512,256]{2,0,1:T(8,128)(2,1)}), bf16[8,512,256]{2,0,1:T(8,128)(2,1)}, u32[]{:S(2)}, u32[]{:S(2)}) async-start(bf16[8,512,256]{2,0,1:T(8,128)(2,1)} %copy.143), calls=%async_computation.2 | async-start | bytes 4194304 | tf_op jit(solution)/shard_map/all_to_all | solution.py:11
  133.9 29.9 %all-to-all-start.1 = ((bf16[8,2,65536]{2,1,0:T(2,128)(2,1)}), bf16[8,2,65536]{2,1,0:T(2,128)(2,1)S(1)}, u32[]{:S(2)}, u32[]{:S(2)}) async-start(bf16[8,2,65536]{2,1,0:T(2,128)(2,1)} %reshape.82), calls=%async_computation.1 | async-start | bytes 4194304 | tf_op jit(solution)/shard_map/all_to_all | solution.py:19
  137.5 2.3 copy-start.6
  163.8 63.7 %all-to-all-start.3 = ((bf16[256,16,256]{2,1,0:T(8,128)(2,1)}), bf16[256,16,256]{2,1,0:T(8,128)(2,1)}, u32[]{:S(2)}, u32[]{:S(2)}) async-start(bf16[256,16,256]{2,1,0:T(8,128)(2,1)} %copy.147), calls=%async_computation.3 | async-start | bytes 4194304 | tf_op jit(solution)/shard_map/all_to_all | solution.py:14
  229.6 3.7 copy-start.1
  229.6 4.4 %copy-start.5 = (bf16[4096,256]{1,0:T(8,128)(2,1)S(1)}, bf16[4096,256]{1,0:T(8,128)(2,1)}, u32[]{:S(2)}) copy-start(bf16[4096,256]{1,0:T(8,128)(2,1)} %param.13) | copy-start | bytes 6291460
  230.1 5.4 %copy-start.2 = (f32[8,32,16,256]{3,2,1,0:T(8,128)}, f32[8,32,16,256]{3,2,1,0:T(8,128)S(1)}, u32[]{:S(2)}) copy-start(f32[8,32,16,256]{3,2,1,0:T(8,128)S(1)} %copy.148) | copy-start | bytes 12582916
  238.1 31.0 %all-to-all-start.6 = ((bf16[8,512,256]{2,0,1:T(8,128)(2,1)}), bf16[8,512,256]{2,0,1:T(8,128)(2,1)}, u32[]{:S(2)}, u32[]{:S(2)}) async-start(bf16[8,512,256]{2,0,1:T(8,128)(2,1)} %copy.158), calls=%async_computation.6 | async-start | bytes 4194304 | tf_op jit(solution)/shard_map/all_to_all | solution.py:76
  269.0 57.8 %all-to-all-start.4 = ((bf16[8,512,256]{2,0,1:T(8,128)(2,1)}), bf16[8,512,256]{2,0,1:T(8,128)(2,1)}, u32[]{:S(2)}, u32[]{:S(2)}) async-start(bf16[8,512,256]{2,0,1:T(8,128)(2,1)} %copy.150), calls=%async_computation.4 | async-start | bytes 4194304 | tf_op jit(solution)/shard_map/all_to_all | solution.py:11
  290.0 9.4 %copy-start.4 = (bf16[2048,512]{1,0:T(8,128)(2,1)S(1)}, bf16[2048,512]{1,0:T(8,128)(2,1)}, u32[]{:S(2)}) copy-start(bf16[2048,512]{1,0:T(8,128)(2,1)} %all-gather.2.cloned.1.call-done) | copy-start | bytes 6291460
  326.8 30.3 %all-to-all-start.7 = ((bf16[8,2,65536]{2,1,0:T(2,128)(2,1)}), bf16[8,2,65536]{2,1,0:T(2,128)(2,1)S(1)}, u32[]{:S(2)}, u32[]{:S(2)}) async-start(bf16[8,2,65536]{2,1,0:T(2,128)(2,1)} %reshape.84), calls=%async_computation.7 | async-start | bytes 4194304 | tf_op jit(solution)/shard_map/all_to_all | solution.py:20
  357.1 57.4 %all-to-all-start.5 = ((bf16[256,16,256]{2,1,0:T(8,128)(2,1)}), bf16[256,16,256]{2,1,0:T(8,128)(2,1)}, u32[]{:S(2)}, u32[]{:S(2)}) async-start(bf16[256,16,256]{2,1,0:T(8,128)(2,1)} %copy.154), calls=%async_computation.5 | async-start | bytes 4194304 | tf_op jit(solution)/shard_map/all_to_all | solution.py:14
  417.2 2.2 copy-start.3
Sparse Core Ops, SparseCore 0:
  20.0 84.5 all-gather.1
where the time goes:
time: 435 us; the launch traced here: 430 us
  waiting for transfers between devices  185 us (43%)
  local copies, waits for them, and re-layouts  118 us (27%)
  starting transfers between devices  63.8 us (15%)
  matrix products  37.1 us (9%)
  between operations  14.5 us (3%)
  other arithmetic  12.4 us (3%)
    all_to_all x2, waiting for transfers between devices, seq_pass(): lax.all_to_all(mixed_cols, 'seq', split_axis=0, concat_axis=1, tiled=True)  62.7 us
    unnamed x25, local copies, waits for them, and re-layouts  32.8 us
    all_gather x1, waiting for transfers between devices, local(): rows_all = lax.all_gather(blocks, 'chan', axis=0, tiled=True)  30.2 us
    all_to_all x2, starting transfers between devices, seq_pass(): lax.all_to_all(values, 'seq', split_axis=1, concat_axis=0, tiled=True)  25.1 us
    all_to_all x1, waiting for transfers between devices, local(): lax.all_to_all(grad_gate, 'chan', split_axis=1, concat_axis=2, tiled=True)  24.1 us
    all_to_all x1, waiting for transfers between devices, local(): lax.all_to_all(values, 'chan', split_axis=1, concat_axis=2, tiled=True)  21.5 us
    all_to_all x2, starting transfers between devices, seq_pass(): lax.all_to_all(mixed_cols, 'seq', split_axis=0, concat_axis=1, tiled=True)  20.8 us
    all_to_all x1, waiting for transfers between devices, send_back(): lax.all_to_all(values[1], 'chan', split_axis=2, concat_axis=1, tiled=True)  16.7 us
  transfers between devices with their start and end apart: 9, of which 8 were waited for; matrix products, arithmetic and copies ran while one was open for 33% of the time, Pallas kernels for 0%

commit v1 on v0

v1 whole, which is shorter than its diff:
```python
import jax
import jax.numpy as jnp
from jax import lax
from jax.experimental import pallas as pl
from jax.experimental.pallas import tpu as pltpu
from jax.sharding import PartitionSpec as P


F32 = jnp.float32
BF16 = jnp.bfloat16
NY = 4


def _params(mib=48):
    return pltpu.CompilerParams(vmem_limit_bytes=min(mib << 20, 67043328))


def _hbm(shape):
    return pltpu.HBM(shape, BF16)


def _cost(flops, nbytes):
    return pl.CostEstimate(flops=flops, bytes_accessed=nbytes, transcendentals=0)


def _fwd(s, d):
    return lax.rem(s[0] // 2 + d, NY)


def _back(s, d):
    return lax.rem(s[0] // 2 + NY - d, NY)


def _column(row, length):
    return jnp.transpose(jnp.broadcast_to(row, (128, length)))


def right_kernel(x_ref, r_ref, tw_ref, out_ref, scr):
    outer, _, chan = x_ref.shape
    rows = r_ref.shape[0]
    for a in range(outer):
        acc = jnp.dot(r_ref[...], x_ref[a], preferred_element_type=F32)
        col = _column(tw_ref[a : a + 1, :], rows)
        for c in range(chan // 128):
            scr[c, pl.ds(a, rows, stride=outer), :] = acc[:, c * 128 : c * 128 + 128] * col
    for c in range(chan // 128):
        out_ref[:, :, :, c * 128 : c * 128 + 128] = scr[c].reshape(*out_ref.shape[:3], 128).astype(BF16)


def right_pass(x3, right, twiddle, seq):
    outer, inner, chan = x3.shape
    steps = 2
    rows = inner // steps
    per = inner // seq
    return pl.pallas_call(
        right_kernel,
        name="right_pass",
        grid=(steps,),
        in_specs=[
            pl.BlockSpec((outer, inner, chan), lambda g: (0, 0, 0)),
            pl.BlockSpec((rows, inner), lambda g: (g, 0)),
            pl.BlockSpec((outer, rows), lambda g: (0, g)),
        ],
        out_specs=pl.BlockSpec((seq // steps, per, outer, chan), lambda g: (g, 0, 0, 0)),
        out_shape=_hbm((seq, per, outer, chan)),
        scratch_shapes=[pltpu.VMEM((chan // 128, rows * outer, 128), F32)],
        compiler_params=_params(64),
        cost_estimate=_cost(2 * outer * inner * inner * chan, 6 << 20),
    )(x3, right, twiddle)


def left_kernel(l_ref, in_ref, out_ref):
    seq, per, outer, chan = in_ref.shape
    for j in range(per):
        block = in_ref[:, j].astype(F32).reshape(seq * outer, chan).astype(BF16)
        acc = jnp.dot(l_ref[...], block, preferred_element_type=F32)
        out_ref[:, j] = acc.reshape(seq, outer, chan).astype(BF16)


def left_pass(left, wire):
    seq, per, outer, chan = wire.shape
    steps = 4
    full = seq * outer
    block = (seq, per // steps, outer, chan)
    return pl.pallas_call(
        left_kernel,
        name="left_pass",
        grid=(steps,),
        in_specs=[
            pl.BlockSpec((full, full), lambda g: (0, 0)),
            pl.BlockSpec(block, lambda g: (0, g, 0, 0)),
        ],
        out_specs=pl.BlockSpec(block, lambda g: (0, g, 0, 0)),
        out_shape=_hbm(wire.shape),
        compiler_params=_params(),
        cost_estimate=_cost(2 * full * full * per * chan, 4 << 20),
    )(left, wire)


def middle_kernel(s, x_ref, xr_ref, b_ref, bo_ref, *outs):
    d = pl.program_id(0)
    half_outer, rows, chan = x_ref.shape
    half = lax.rem(s[0], 2)
    own = pl.ds(pl.multiple_of(half * chan, 128), chan)
    other = pl.ds(pl.multiple_of((1 - half) * chan, 128), chan)
    dims = (((1,), (1,)), ((), ()))
    x = x_ref[...].reshape(half_outer * rows, chan)
    xr = xr_ref[...].reshape(half_outer * rows, chan)
    values = []
    for ref in (b_ref, bo_ref):
        acc = lax.dot_general(x, ref[:, own], dims, preferred_element_type=F32)
        acc += lax.dot_general(xr, ref[:, other], dims, preferred_element_type=F32)
        values.append(acc.astype(BF16))
    for i in range(NY):

        @pl.when(d == i)
        def _():
            outs[i][0] = values[0]
            outs[i][1] = values[1]


def middle_pass(s, x3, xr, blocks, blocks_other):
    half_outer, inner, chan = xr.shape
    rows = inner // NY
    block = (half_outer, rows, chan)
    part = (2, half_outer * rows, chan)
    whole = pl.BlockSpec(blocks.shape, lambda d, s: (0, 0))
    return pl.pallas_call(
        middle_kernel,
        name="middle_pass",
        grid_spec=pltpu.PrefetchScalarGridSpec(
            num_scalar_prefetch=1,
            grid=(NY,),
            in_specs=[
                pl.BlockSpec(block, lambda d, s: (lax.rem(s[0], 2), _fwd(s, d), 0)),
                pl.BlockSpec(block, lambda d, s: (0, _fwd(s, d), 0)),
                whole,
                whole,
            ],
            out_specs=[pl.BlockSpec(part, lambda d, s: (0, 0, 0))] * NY,
        ),
        out_shape=[jax.ShapeDtypeStruct(part, BF16)] * NY,
        compiler_params=_params(),
        cost_estimate=_cost(8 * half_outer * inner * chan * chan, 5 << 20),
    )(s, x3, xr, blocks, blocks_other)


def _mixed(s, mix_ref, values, e, k, flip):
    y = s[0] // 2
    chan = values[0].shape[-1]
    cols = pl.ds(pl.multiple_of(lax.rem(s[0] + k, 2) * chan, 128), chan)
    to = lax.rem(y + e, NY)
    acc = None
    for d in range(NY):
        frm = lax.rem(y + NY - d, NY)
        row = mix_ref[frm, pl.ds(to, 1), cols] if flip else mix_ref[to, pl.ds(frm, 1), cols]
        term = values[d] * row
        acc = term if acc is None else acc + term
    return acc.astype(BF16)


def mix_kernel(s, mix_ref, *refs):
    ins, outs = refs[:NY], refs[NY:]
    for k in range(2):
        values = [r[k].astype(F32) for r in ins]
        for e in range(NY):
            outs[2 * e + k][...] = _mixed(s, mix_ref, values, e, k, False)


def mix_pass(s, mixer, parts):
    _, total, chan = parts[0].shape
    steps = 2
    out_block = pl.BlockSpec((total // steps, chan), lambda g, s: (g, 0))
    return pl.pallas_call(
        mix_kernel,
        name="mix_pass",
        grid_spec=pltpu.PrefetchScalarGridSpec(
            num_scalar_prefetch=1,
            grid=(steps,),
            in_specs=[pl.BlockSpec(mixer.shape, lambda g, s: (0, 0, 0))]
            + [pl.BlockSpec((2, total // steps, chan), lambda g, s: (0, g, 0))] * NY,
            out_specs=[out_block] * (2 * NY),
        ),
        out_shape=[jax.ShapeDtypeStruct((total, chan), BF16)] * (2 * NY),
        compiler_params=_params(),
        cost_estimate=_cost(4 * NY * NY * total * chan, 4 << 20),
    )(s, mixer, *parts)


def mix_back_kernel(s, mix_ref, *refs):
    ins, outs = refs[: 2 * NY], refs[2 * NY :]
    for k in range(2):
        values = [ins[2 * d + k][...].astype(F32) for d in range(NY)]
        for e in range(NY):
            outs[e][k] = _mixed(s, mix_ref, values, e, k, True)


def mix_back(s, mixer, pieces):
    total, chan = pieces[0].shape
    steps = 2
    in_block = pl.BlockSpec((total // steps, chan), lambda g, s: (g, 0))
    return pl.pallas_call(
        mix_back_kernel,
        name="mix_back",
        grid_spec=pltpu.PrefetchScalarGridSpec(
            num_scalar_prefetch=1,
            grid=(steps,),
            in_specs=[pl.BlockSpec(mixer.shape, lambda g, s: (0, 0, 0))] + [in_block] * (2 * NY),
            out_specs=[pl.BlockSpec((2, total // steps, chan), lambda g, s: (0, g, 0))] * NY,
        ),
        out_shape=[jax.ShapeDtypeStruct((2, total, chan), BF16)] * NY,
        compiler_params=_params(),
        cost_estimate=_cost(4 * NY * NY * total * chan, 4 << 20),
    )(s, mixer, *pieces)


def gate_kernel(s, og_ref, *refs):
    pieces, (gate_ref, wire_ref, scr) = refs[: 2 * NY], refs[2 * NY :]
    d = pl.program_id(0)
    outer, rows, chan = og_ref.shape
    for i in range(NY):

        @pl.when(d == i)
        def _():
            for k in range(2):
                start = lax.rem(s[0] + k, 2) * (outer // 2)
                gate_ref[pl.ds(start, outer // 2)] = pieces[2 * i + k][...].reshape(outer // 2, rows, chan)

    for a in range(outer):
        for c in range(chan // 128):
            cols = slice(c * 128, c * 128 + 128)
            scr[c, pl.ds(a, rows, stride=outer), :] = og_ref[a, :, cols].astype(F32) * gate_ref[a, :, cols].astype(F32)
    for c in range(chan // 128):
        wire_ref[:, :, :, c * 128 : c * 128 + 128] = scr[c].reshape(*wire_ref.shape[:3], 128).astype(BF16)


def gate_pass(s, og3, pieces, seq):
    outer, inner, chan = og3.shape
    rows = inner // NY
    per = inner // seq
    nat = pl.BlockSpec((outer, rows, chan), lambda d, s: (0, _back(s, d), 0))
    return pl.pallas_call(
        gate_kernel,
        name="gate_pass",
        grid_spec=pltpu.PrefetchScalarGridSpec(
            num_scalar_prefetch=1,
            grid=(NY,),
            in_specs=[nat] + [pl.BlockSpec(pieces[0].shape, lambda d, s: (0, 0))] * (2 * NY),
            out_specs=[nat, pl.BlockSpec((seq // NY, per, outer, chan), lambda d, s: (_back(s, d), 0, 0, 0))],
            scratch_shapes=[pltpu.VMEM((chan // 128, rows * outer, 128), F32)],
        ),
        out_shape=[
            jax.ShapeDtypeStruct(og3.shape, BF16),
            jax.ShapeDtypeStruct((seq, per, outer, chan), BF16),
        ],
        compiler_params=_params(),
        cost_estimate=_cost(outer * inner * chan, 8 << 20),
    )(s, og3, *pieces)


def out_kernel(s, wire_ref, gate_ref, og_ref, out_ref, *refs):
    pieces, (scr, tmp) = refs[: 2 * NY], refs[2 * NY :]
    d = pl.program_id(0)
    outer, rows, chan = og_ref.shape
    for c in range(chan // 128):
        scr[c] = wire_ref[:, :, :, c * 128 : c * 128 + 128].astype(F32).reshape(scr.shape[1:])
    for a in range(outer):
        for c in range(chan // 128):
            cols = slice(c * 128, c * 128 + 128)
            m = scr[c, pl.ds(a, rows, stride=outer), :]
            out_ref[a, :, cols] = (gate_ref[a, :, cols].astype(F32) * m).astype(BF16)
            tmp[a, :, cols] = (og_ref[a, :, cols].astype(F32) * m).astype(BF16)
    for i in range(NY):

        @pl.when(d == i)
        def _():
            for k in range(2):
                start = lax.rem(s[0] + k, 2) * (outer // 2)
                pieces[2 * i + k][...] = tmp[pl.ds(start, outer // 2)].reshape(pieces[0].shape)


def out_pass(s, wire, gate3, og3):
    outer, inner, chan = og3.shape
    seq, per = wire.shape[:2]
    rows = inner // NY
    piece = (outer // 2 * rows, chan)
    nat = pl.BlockSpec((outer, rows, chan), lambda d, s: (0, _fwd(s, d), 0))
    res = pl.pallas_call(
        out_kernel,
        name="out_pass",
        grid_spec=pltpu.PrefetchScalarGridSpec(
            num_scalar_prefetch=1,
            grid=(NY,),
            in_specs=[pl.BlockSpec((seq // NY, per, outer, chan), lambda d, s: (_fwd(s, d), 0, 0, 0)), nat, nat],
            out_specs=[nat] + [pl.BlockSpec(piece, lambda d, s: (0, 0))] * (2 * NY),
            scratch_shapes=[
                pltpu.VMEM((chan // 128, rows * outer, 128), F32),
                pltpu.VMEM((outer, rows, chan), BF16),
            ],
        ),
        out_shape=[jax.ShapeDtypeStruct(og3.shape, BF16)] + [jax.ShapeDtypeStruct(piece, BF16)] * (2 * NY),
        compiler_params=_params(),
        cost_estimate=_cost(2 * outer * inner * chan, 10 << 20),
    )(s, wire, gate3, og3)
    return res[0], res[1:]


def chan_kernel(s, b_ref, bo_ref, *refs):
    parts, (own_ref, other_ref) = refs[:NY], refs[NY:]
    d = pl.program_id(0)
    _, _, chan = own_ref.shape
    for i in range(NY):

        @pl.when(d == i)
        def _():
            for k, ref in enumerate((own_ref, other_ref)):
                cols = pl.ds(pl.multiple_of(lax.rem(s[0] + k, 2) * chan, 128), chan)
                acc = jnp.dot(parts[i][0], b_ref[:, cols], preferred_element_type=F32)
                acc += jnp.dot(parts[i][1], bo_ref[:, cols], preferred_element_type=F32)
                ref[...] = acc.astype(BF16).reshape(ref.shape)


def chan_pass(s, blocks, blocks_other, parts, half_outer):
    _, total, chan = parts[0].shape
    rows = total // half_outer
    whole = pl.BlockSpec(blocks.shape, lambda d, s: (0, 0))
    out = pl.BlockSpec((half_outer, rows, chan), lambda d, s: (0, _back(s, d), 0))
    return pl.pallas_call(
        chan_kernel,
        name="chan_pass",
        grid_spec=pltpu.PrefetchScalarGridSpec(
            num_scalar_prefetch=1,
            grid=(NY,),
            in_specs=[whole, whole] + [pl.BlockSpec(parts[0].shape, lambda d, s: (0, 0, 0))] * NY,
            out_specs=[out, out],
        ),
        out_shape=[jax.ShapeDtypeStruct((half_outer, rows * NY, chan), BF16)] * 2,
        compiler_params=_params(),
        cost_estimate=_cost(8 * total * NY * chan * chan, 5 << 20),
    )(s, blocks, blocks_other, *parts)


def tail_kernel(s, wire_ref, rt_ref, tw_ref, own_ref, other_ref, out_ref, scr):
    outer, inner = tw_ref.shape
    chan = out_ref.shape[2]
    a = pl.program_id(0)

    @pl.when(a == 0)
    def _():
        for c in range(chan // 128):
            scr[c] = wire_ref[:, :, :, c * 128 : c * 128 + 128].astype(F32).reshape(scr.shape[1:])

    col = _column(tw_ref[pl.ds(a, 1), :], inner)
    parts = []
    for c in range(chan // 128):
        parts.append((scr[c, pl.ds(a, inner, stride=outer), :] * col).astype(BF16))
    acc = jnp.dot(rt_ref[...], jnp.concatenate(parts, axis=1), preferred_element_type=F32)
    mine = a // (outer // 2) == lax.rem(s[0], 2)

    @pl.when(mine)
    def _():
        out_ref[0] = (acc + own_ref[0].astype(F32)).astype(BF16)

    @pl.when(jnp.logical_not(mine))
    def _():
        out_ref[0] = (acc + other_ref[0].astype(F32)).astype(BF16)


def tail_pass(s, wire, right_t, twiddle, own, other):
    half_outer, inner, chan = own.shape
    outer = 2 * half_outer

    def part(k):
        return lambda a, s: (jnp.clip(a - lax.rem(s[0] + k, 2) * half_outer, 0, half_outer - 1), 0, 0)

    return pl.pallas_call(
        tail_kernel,
        name="tail_pass",
        grid_spec=pltpu.PrefetchScalarGridSpec(
            num_scalar_prefetch=1,
            grid=(outer,),
            in_specs=[
                pl.BlockSpec(wire.shape, lambda a, s: (0, 0, 0, 0)),
                pl.BlockSpec(right_t.shape, lambda a, s: (0, 0)),
                pl.BlockSpec(twiddle.shape, lambda a, s: (0, 0)),
                pl.BlockSpec((1, inner, chan), part(0)),
                pl.BlockSpec((1, inner, chan), part(1)),
            ],
            out_specs=pl.BlockSpec((1, inner, chan), lambda a, s: (a, 0, 0)),
            scratch_shapes=[pltpu.VMEM((chan // 128, outer * inner, 128), F32)],
        ),
        out_shape=jax.ShapeDtypeStruct((outer, inner, chan), BF16),
        compiler_params=_params(),
        cost_estimate=_cost(2 * outer * inner * inner * chan, 7 << 20),
    )(s, wire, right_t, twiddle, own, other)


def seq_swap(wire):
    return lax.all_to_all(wire, "seq", split_axis=0, concat_axis=0, tiled=True)


def body(inputs, twiddle, right_factor, left_factor, blocks, block_mixer, out_grad):
    outer, inner = twiddle.shape
    chan = inputs.shape[1]
    seq = left_factor.shape[0] // outer
    n = 2 * NY

    def send(v, d, k):
        if d == 0 and k == 0:
            return v
        return lax.ppermute(v, "chan", [(c, (((c // 2 + d) % NY) * 2 + c % 2) ^ k) for c in range(n)])

    def around(parts):
        return [send(parts[d], d, 0) for d in range(NY)]

    def across(pieces):
        return [send(p, i // 2, i % 2) for i, p in enumerate(pieces)]

    s = lax.axis_index("chan").reshape(1)
    x3 = inputs.reshape(outer, inner, chan)
    og3 = out_grad.reshape(outer, inner, chan)
    mixer = jnp.transpose(block_mixer, (1, 2, 0))

    half = lax.rem(lax.axis_index("chan"), 2)
    xs = lax.dynamic_slice_in_dim(x3, (1 - half) * (outer // 2), outer // 2, 0)
    xr = send(xs, 0, 1)
    blocks_other = send(blocks, 0, 1)
    twisted = seq_swap(right_pass(x3, right_factor, twiddle, seq))
    middle = middle_pass(s, x3, xr, blocks, blocks_other)
    twisted, _ = lax.optimization_barrier((twisted, middle[0]))
    mixed_wire = left_pass(left_factor, twisted)

    middle = around(middle)
    *middle, _ = lax.optimization_barrier((*middle, mixed_wire))
    mixed = seq_swap(mixed_wire)
    pieces = mix_pass(s, mixer, middle)
    pieces = across(pieces)
    gate3, grad_mixed = gate_pass(s, og3, pieces, seq)

    grad_mixed, mixed = lax.optimization_barrier((grad_mixed, mixed))
    grad_wire = seq_swap(grad_mixed)
    output, pieces = out_pass(s, mixed, gate3, og3)
    pieces = across(pieces)
    grad_middle = mix_back(s, mixer, pieces)
    grad_wire, _ = lax.optimization_barrier((grad_wire, grad_middle[0]))
    grad_wire = left_pass(left_factor.T, grad_wire)

    grad_middle = around(grad_middle)
    grad_twisted = seq_swap(grad_wire)
    own, other = chan_pass(s, blocks, blocks_other, grad_middle, outer // 2)
    other = send(other, 0, 1)
    input_grad = tail_pass(s, grad_twisted, right_factor.T, twiddle, own, other)
    return (output.reshape(inputs.shape), input_grad.reshape(inputs.shape))


def solution(mesh):
    return jax.shard_map(
        body,
        mesh=mesh,
        in_specs=(
            P("seq", "chan"),
            P("seq", None),
            P(),
            P(),
            P("chan", None),
            P(),
            P("seq", "chan"),
        ),
        out_specs=(P("seq", "chan"), P("seq", "chan")),
        check_vma=False,
    )
```

time: 435 us -> 307 us (0.71)
  local copies, waits for them, and re-layouts: 118 us -> 13.9 us
  Pallas kernels: 0 us -> 37.4 us
  matrix products: 37.1 us -> 0 us
  between operations: 14.5 us -> 0.8 us
  other arithmetic: 12.4 us -> 0 us
  starting transfers between devices: 63.8 us -> 74.3 us
  waiting for transfers between devices: 185 us -> 180 us
    ppermute x0 -> x23, waiting for transfers between devices: none -> 180 us  [send(): lax.ppermute(v, 'chan', [(c, (c // 2 + d) % NY * 2 + c % 2 ^ k) for c in...]
    all_to_all x8 -> x4, waiting for transfers between devices: 154 us -> 0.01 us  [seq_swap(): return lax.all_to_all(wire, 'seq', split_axis=0, concat_axis=0, tiled=True)]
    convert_element_type x16 -> x0, local copies, waits for them, and re-layouts: 46.8 us -> none  [the longest x4 11.3 us: local(): input_grad = (seq_grad + chan_grad.astype(jnp.float32)).astype(jnp.bfloat16)]
    pallas_call x0 -> x10, Pallas kernels: none -> 37.4 us  [the longest x1 7.36 us: tail_pass(): pl.pallas_call(tail_kernel, name='tail_pass', grid_spec=pltpu.PrefetchSca...]
    dot_general x7 -> x0, matrix products: 33.6 us -> none  [the longest x1 9.65 us: gate_of(): jnp.einsum('nbpk,kop->nbok', middle.astype(jnp.float32), block_mixer, pre...]
    all_gather x1 -> x0, waiting for transfers between devices: 30.2 us -> none  [local(): rows_all = lax.all_gather(blocks, 'chan', axis=0, tiled=True)]
    ppermute x0 -> x23, starting transfers between devices: none -> 29.8 us  [send(): lax.ppermute(v, 'chan', [(c, (c // 2 + d) % NY * 2 + c % 2 ^ k) for c in...]
    unnamed x25 -> x38, local copies, waits for them, and re-layouts: 32.8 us -> 12.4 us
  transfers between devices with their start and end apart: 9 -> 27, of which waited for: 8 -> 15; matrix products, arithmetic and copies ran while one was open for 33% -> 1% of each run, Pallas kernels for 0% -> 6%
where the time goes in v1:
time: 307 us; the launch traced here: 306 us
  waiting for transfers between devices  180 us (59%)
  starting transfers between devices  74.3 us (24%)
  Pallas kernels  37.4 us (12%)
  local copies, waits for them, and re-layouts  13.9 us (5%)
    ppermute x23, waiting for transfers between devices, send(): lax.ppermute(v, 'chan', [(c, (c // 2 + d) % NY * 2 + c % 2 ^ k) for c in...  180 us
    all_to_all x4, starting transfers between devices, seq_swap(): return lax.all_to_all(wire, 'seq', split_axis=0, concat_axis=0, tiled=True)  44.5 us
    ppermute x23, starting transfers between devices, send(): lax.ppermute(v, 'chan', [(c, (c // 2 + d) % NY * 2 + c % 2 ^ k) for c in...  29.8 us
    unnamed x38, local copies, waits for them, and re-layouts  12.4 us
    pallas_call x1, Pallas kernels, tail_pass(): pl.pallas_call(tail_kernel, name='tail_pass', grid_spec=pltpu.PrefetchSca...  7.36 us
    pallas_call x2, Pallas kernels, left_pass(): pl.pallas_call(left_kernel, name='left_pass', grid=(steps,), in_specs=[pl...  6.96 us
  transfers between devices with their start and end apart: 27, of which 15 were waited for; matrix products, arithmetic and copies ran while one was open for 1% of the time, Pallas kernels for 6%

profile of v1, /device:TPU:1, one launch (start us, length us, event | category | flops | bytes accessed | tf_op | source)
XLA Modules:
  0.0 306.1 jit_solution(3267286388770721293)
XLA Ops:
  0.6 4.6 %right_pass.1 = bf16[32,16,8,256]{3,2,1,0:T(8,128)(2,1)} custom-call(bf16[8,512,256]{2,1,0:T(8,128)(2,1)} %bitcast.8, bf16[512,512]{1,0:T(8,128)(2,1)} %r_ref.1, f32[8,512]{1,0:T(8,128)} %tw_ref.3), custom_call_target="tpu_custom_call" | custom-call | flops 1073741824 | bytes 6291456 | tf_op jit(solution)/shard_map/right_pass/pallas_call | solution.py:55
  5.2 12.7 %all-to-all-start = ((bf16[32,16,8,256]{3,2,1,0:T(8,128)(2,1)}), bf16[32,16,8,256]{3,2,1,0:T(8,128)(2,1)S(1)}, u32[]{:S(2)}, u32[]{:S(2)}) async-start(bf16[32,16,8,256]{3,2,1,0:T(8,128)(2,1)} %right_pass.1), calls=%async_computation | async-start | bytes 4194304 | tf_op jit(solution)/shard_map/all_to_all | solution.py:399
  20.9 48.8 %collective-permute-done.1.bo_ref = bf16[256,512]{1,0:T(8,128)(2,1)S(1)} collective-permute-done((bf16[256,512]{1,0:T(8,128)(2,1)S(1)}, bf16[256,512]{1,0:T(8,128)(2,1)S(1)}, u32[]{:S(2)}, u32[]{:S(2)}) %collective-permute-start.1) | collective-permute-done | bytes 262176 | tf_op jit(solution)/shard_map/ppermute | solution.py:411
  70.7 2.5 middle_pass.1
  75.5 2.6 left_pass.2
  78.1 10.9 %all-to-all-start.1 = ((bf16[32,16,8,256]{3,2,1,0:T(8,128)(2,1)}), bf16[32,16,8,256]{3,2,1,0:T(8,128)(2,1)S(1)}, u32[]{:S(2)}, u32[]{:S(2)}) async-start(bf16[32,16,8,256]{3,2,1,0:T(8,128)(2,1)} %left_pass.2), calls=%async_computation.1 | async-start | bytes 4194304 | tf_op jit(solution)/shard_map/all_to_all | solution.py:399
  90.5 2.6 collective-permute-start.3
  94.1 9.8 %collective-permute-done.2.refs_1_ = bf16[2,512,256]{2,1,0:T(8,128)(2,1)S(1)} collective-permute-done((bf16[2,512,256]{2,1,0:T(8,128)(2,1)}, bf16[2,512,256]{2,1,0:T(8,128)(2,1)S(1)}, u32[]{:S(2)}, u32[]{:S(2)}) %collective-permute-start.2) | collective-permute-done | bytes 524320 | tf_op jit(solution)/shard_map/ppermute | solution.py:411
  103.9 12.4 %collective-permute-done.3.refs_2_ = bf16[2,512,256]{2,1,0:T(8,128)(2,1)S(1)} collective-permute-done((bf16[2,512,256]{2,1,0:T(8,128)(2,1)}, bf16[2,512,256]{2,1,0:T(8,128)(2,1)S(1)}, u32[]{:S(2)}, u32[]{:S(2)}) %collective-permute-start.3) | collective-permute-done | bytes 524320 | tf_op jit(solution)/shard_map/ppermute | solution.py:411
  117.8 2.5 collective-permute-start.10
  123.0 4.0 %collective-permute-done.10.refs_6_ = bf16[512,256]{1,0:T(8,128)(2,1)S(1)} collective-permute-done((bf16[512,256]{1,0:T(8,128)(2,1)S(1)}, bf16[512,256]{1,0:T(8,128)(2,1)S(1)}, u32[]{:S(2)}, u32[]{:S(2)}) %collective-permute-start.10) | collective-permute-done | bytes 262176 | tf_op jit(solution)/shard_map/ppermute | solution.py:411
  127.0 2.5 collective-permute-start.8
  129.5 4.8 %collective-permute-done.11.refs_7_ = bf16[512,256]{1,0:T(8,128)(2,1)S(1)} collective-permute-done((bf16[512,256]{1,0:T(8,128)(2,1)S(1)}, bf16[512,256]{1,0:T(8,128)(2,1)S(1)}, u32[]{:S(2)}, u32[]{:S(2)}) %collective-permute-start.11) | collective-permute-done | bytes 262176 | tf_op jit(solution)/shard_map/ppermute | solution.py:411
  136.2 2.3 collective-permute-done.5.refs_1_
  138.6 7.5 %collective-permute-done.7.refs_3_ = bf16[512,256]{1,0:T(8,128)(2,1)S(1)} collective-permute-done((bf16[512,256]{1,0:T(8,128)(2,1)S(1)}, bf16[512,256]{1,0:T(8,128)(2,1)S(1)}, u32[]{:S(2)}, u32[]{:S(2)}) %collective-permute-start.7) | collective-permute-done | bytes 262176 | tf_op jit(solution)/shard_map/ppermute | solution.py:411
  146.1 6.2 %collective-permute-done.9.refs_5_ = bf16[512,256]{1,0:T(8,128)(2,1)S(1)} collective-permute-done((bf16[512,256]{1,0:T(8,128)(2,1)S(1)}, bf16[512,256]{1,0:T(8,128)(2,1)S(1)}, u32[]{:S(2)}, u32[]{:S(2)}) %collective-permute-start.9) | collective-permute-done | bytes 262176 | tf_op jit(solution)/shard_map/ppermute | solution.py:411
  152.3 4.7 %gate_pass.1 = (bf16[8,512,256]{2,1,0:T(8,128)(2,1)S(1)}, bf16[32,16,8,256]{3,2,1,0:T(8,128)(2,1)}) custom-call(s32[1]{0:T(128)} %bitcast.s, bf16[8,512,256]{2,1,0:T(8,128)(2,1)} %bitcast.15, bf16[512,256]{1,0:T(8,128)(2,1)S(1)} %get-tuple-element.48.refs_0_, bf16[512,256]{1,0:T(8,128)(2,1)S(1)} %collective-permute-done.5.refs_1_, ...), custom_call_target="tpu_custom_call" | custom-call | flops 1048576 | bytes 8388608 | tf_op jit(solution)/shard_map/gate_pass/pallas_call | solution.py:242
  158.4 10.4 %all-to-all-start.2 = ((bf16[32,16,8,256]{3,2,1,0:T(8,128)(2,1)}), bf16[32,16,8,256]{3,2,1,0:T(8,128)(2,1)}, u32[]{:S(2)}, u32[]{:S(2)}) async-start(bf16[32,16,8,256]{3,2,1,0:T(8,128)(2,1)} %get-tuple-element.60), calls=%async_computation.2 | async-start | bytes 4194304 | tf_op jit(solution)/shard_map/all_to_all | solution.py:399
  168.8 5.4 %out_pass.1 = (bf16[8,512,256]{2,1,0:T(8,128)(2,1)}, bf16[512,256]{1,0:T(8,128)(2,1)S(1)}, bf16[512,256]{1,0:T(8,128)(2,1)S(1)}, bf16[512,256]{1,0:T(8,128)(2,1)...) custom-call(s32[1]{0:T(128)} %bitcast.s, ...), custom_call_target="tpu_custom_call" | custom-call | flops 2097152 | bytes 10485760 | tf_op jit(solution)/shard_map/out_pass/pallas_call | solution.py:288
  176.3 3.0 collective-permute-start.15
  179.3 8.7 %collective-permute-done.12.refs_1_ = bf16[512,256]{1,0:T(8,128)(2,1)S(1)} collective-permute-done((bf16[512,256]{1,0:T(8,128)(2,1)S(1)}, bf16[512,256]{1,0:T(8,128)(2,1)S(1)}, u32[]{:S(2)}, u32[]{:S(2)}) %collective-permute-start.12) | collective-permute-done | bytes 262176 | tf_op jit(solution)/shard_map/ppermute | solution.py:411
  191.0 7.2 %collective-permute-done.14.refs_3_ = bf16[512,256]{1,0:T(8,128)(2,1)S(1)} collective-permute-done((bf16[512,256]{1,0:T(8,128)(2,1)}, bf16[512,256]{1,0:T(8,128)(2,1)S(1)}, u32[]{:S(2)}, u32[]{:S(2)}) %collective-permute-start.14) | collective-permute-done | bytes 262176 | tf_op jit(solution)/shard_map/ppermute | solution.py:411
  198.1 12.6 %collective-permute-done.16.refs_5_ = bf16[512,256]{1,0:T(8,128)(2,1)S(1)} collective-permute-done((bf16[512,256]{1,0:T(8,128)(2,1)}, bf16[512,256]{1,0:T(8,128)(2,1)S(1)}, u32[]{:S(2)}, u32[]{:S(2)}) %collective-permute-start.16) | collective-permute-done | bytes 262176 | tf_op jit(solution)/shard_map/ppermute | solution.py:411
  210.7 5.4 %collective-permute-done.18.refs_7_ = bf16[512,256]{1,0:T(8,128)(2,1)S(1)} collective-permute-done((bf16[512,256]{1,0:T(8,128)(2,1)S(1)}, bf16[512,256]{1,0:T(8,128)(2,1)S(1)}, u32[]{:S(2)}, u32[]{:S(2)}) %collective-permute-start.18) | collective-permute-done | bytes 262176 | tf_op jit(solution)/shard_map/ppermute | solution.py:411
  219.9 4.3 %left_pass.3 = bf16[32,16,8,256]{3,2,1,0:T(8,128)(2,1)} custom-call(bf16[256,256]{1,0:T(8,128)(2,1)S(1)} %bitcast.12, bf16[32,16,8,256]{3,2,1,0:T(8,128)(2,1)} %all-to-all-done.2.in_ref), custom_call_target="tpu_custom_call" | custom-call | flops 536870912 | bytes 4194304 | tf_op jit(solution)/shard_map/left_pass/pallas_call | solution.py:85
  224.3 10.5 %all-to-all-start.3 = ((bf16[32,16,8,256]{3,2,1,0:T(8,128)(2,1)}), bf16[32,16,8,256]{3,2,1,0:T(8,128)(2,1)S(1)}, u32[]{:S(2)}, u32[]{:S(2)}) async-start(bf16[32,16,8,256]{3,2,1,0:T(8,128)(2,1)} %left_pass.3), calls=%async_computation.3 | async-start | bytes 4194304 | tf_op jit(solution)/shard_map/all_to_all | solution.py:399
  236.0 2.6 collective-permute-start.20
  240.1 9.4 %collective-permute-done.19.refs_1_ = bf16[2,512,256]{2,1,0:T(8,128)(2,1)S(1)} collective-permute-done((bf16[2,512,256]{2,1,0:T(8,128)(2,1)}, bf16[2,512,256]{2,1,0:T(8,128)(2,1)S(1)}, u32[]{:S(2)}, u32[]{:S(2)}) %collective-permute-start.19) | collective-permute-done | bytes 524320 | tf_op jit(solution)/shard_map/ppermute | solution.py:411
  249.5 12.4 %collective-permute-done.20.refs_2_ = bf16[2,512,256]{2,1,0:T(8,128)(2,1)S(1)} collective-permute-done((bf16[2,512,256]{2,1,0:T(8,128)(2,1)}, bf16[2,512,256]{2,1,0:T(8,128)(2,1)S(1)}, u32[]{:S(2)}, u32[]{:S(2)}) %collective-permute-start.20) | collective-permute-done | bytes 524320 | tf_op jit(solution)/shard_map/ppermute | solution.py:411
  263.7 3.0 chan_pass.1
  269.2 28.3 %collective-permute-done.22.other_ref = bf16[4,512,256]{2,1,0:T(8,128)(2,1)} collective-permute-done((bf16[4,512,256]{2,1,0:T(8,128)(2,1)}, bf16[4,512,256]{2,1,0:T(8,128)(2,1)}, u32[]{:S(2)}, u32[]{:S(2)}) %collective-permute-start.22) | collective-permute-done | bytes 1048608 | tf_op jit(solution)/shard_map/ppermute | solution.py:411
  298.8 7.4 %tail_pass.1 = bf16[8,512,256]{2,1,0:T(8,128)(2,1)} custom-call(s32[1]{0:T(128)} %bitcast.s, bf16[32,16,8,256]{3,2,1,0:T(8,128)(2,1)S(1)} %all-to-all-done.3.wire_ref, bf16[512,512]{1,0:T(8,128)(2,1)S(1)} %bitcast.11, f32[8,512]{1,0:T(8,128)S(1)} %copy-done.6, bf16[4,512,256]{2,1,0:T(8,128)(2,1)S(1)} %copy-done.3, ...), custom_call_target="tpu_custom_call" | custom-call | flops 1073741824 | bytes 7340032 | tf_op jit(solution)/shard_map/tail_pass/pallas_call | solution.py:376
  (71 shorter events, 33.4 us)
Async XLA Ops:
  5.2 14.6 %copy-start.13 = (bf16[256,512]{1,0:T(8,128)(2,1)S(1)}, bf16[256,512]{1,0:T(8,128)(2,1)}, u32[]{:S(2)}) copy-start(bf16[256,512]{1,0:T(8,128)(2,1)} %b_ref.3) | copy-start | bytes 786436
  5.2 70.3 %all-to-all-start = ((bf16[32,16,8,256]{3,2,1,0:T(8,128)(2,1)}), bf16[32,16,8,256]{3,2,1,0:T(8,128)(2,1)S(1)}, u32[]{:S(2)}, u32[]{:S(2)}) async-start(bf16[32,16,8,256]{3,2,1,0:T(8,128)(2,1)} %right_pass.1), calls=%async_computation | async-start | bytes 4194304 | tf_op jit(solution)/shard_map/all_to_all | solution.py:399
  17.9 51.8 %copy-start = (bf16[4096,256]{1,0:T(8,128)(2,1)S(1)}, bf16[4096,256]{1,0:T(8,128)(2,1)}, u32[]{:S(2)}) copy-start(bf16[4096,256]{1,0:T(8,128)(2,1)} %param.7) | copy-start | bytes 6291460
  19.4 56.1 %copy-start.4 = (bf16[256,256]{1,0:T(8,128)(2,1)S(1)}, bf16[256,256]{1,0:T(8,128)(2,1)}, u32[]{:S(2)}) copy-start(bf16[256,256]{1,0:T(8,128)(2,1)} %l_ref.1) | copy-start | bytes 393220
  19.4 50.3 %collective-permute-start = (bf16[4,512,256]{2,1,0:T(8,128)(2,1)S(1)}, bf16[4,512,256]{2,1,0:T(8,128)(2,1)S(1)}, u32[]{:S(2)}, u32[]{:S(2)}) collective-permute-start(bf16[4,512,256]{2,1,0:T(8,128)(2,1)S(1)} %constant_dynamic-slice_fusion), channel_id=1, source_target_pairs={{0,1},{1,0},{2,3},{3,2},{4,5},{5,4},{6,7},{7,6},{8,9},{9,8},{10,11... | collective-permute-start | bytes 3145736 | tf_op jit(solution)/shard_map/ppermute | solution.py:411
  19.8 49.9 %collective-permute-start.1 = (bf16[256,512]{1,0:T(8,128)(2,1)S(1)}, bf16[256,512]{1,0:T(8,128)(2,1)S(1)}, u32[]{:S(2)}, u32[]{:S(2)}) collective-permute-start(bf16[256,512]{1,0:T(8,128)(2,1)S(1)} %copy-done.13), channel_id=1, source_target_pairs={{0,1},{1,0},{2,3},{3,2},{4,5},{5,4},{6,7},{7,6},{8,9},{9,8},{10,11... | collective-permute-start | bytes 786440 | tf_op jit(solution)/shard_map/ppermute | solution.py:411
  78.1 38.2 %copy-start.5 = (f32[512,4,4]{0,2,1:T(4,128)S(1)}, f32[512,4,4]{0,2,1:T(4,128)}, u32[]{:S(2)}) copy-start(f32[512,4,4]{0,2,1:T(4,128)} %param.12) | copy-start | bytes 98308
  78.1 80.2 %all-to-all-start.1 = ((bf16[32,16,8,256]{3,2,1,0:T(8,128)(2,1)}), bf16[32,16,8,256]{3,2,1,0:T(8,128)(2,1)S(1)}, u32[]{:S(2)}, u32[]{:S(2)}) async-start(bf16[32,16,8,256]{3,2,1,0:T(8,128)(2,1)} %left_pass.2), calls=%async_computation.1 | async-start | bytes 4194304 | tf_op jit(solution)/shard_map/all_to_all | solution.py:399
  89.1 14.9 %collective-permute-start.2 = (bf16[2,512,256]{2,1,0:T(8,128)(2,1)}, bf16[2,512,256]{2,1,0:T(8,128)(2,1)S(1)}, u32[]{:S(2)}, u32[]{:S(2)}) collective-permute-start(bf16[2,512,256]{2,1,0:T(8,128)(2,1)} %copy-done.12), channel_id=1, source_target_pairs={{0,2},{1,3},{2,4},{3,5},{4,6},{5,7},{6,0},{7,1},{8,10},{9,11},{10,... | collective-permute-start | bytes 1572872 | tf_op jit(solution)/shard_map/ppermute | solution.py:411
  90.5 25.8 %collective-permute-start.3 = (bf16[2,512,256]{2,1,0:T(8,128)(2,1)}, bf16[2,512,256]{2,1,0:T(8,128)(2,1)S(1)}, u32[]{:S(2)}, u32[]{:S(2)}) collective-permute-start(bf16[2,512,256]{2,1,0:T(8,128)(2,1)} %copy-done.11), channel_id=1, source_target_pairs={{0,4},{1,5},{2,6},{3,7},{4,0},{5,1},{6,2},{7,3},{8,12},{9,13},{10,... | collective-permute-start | bytes 1572872 | tf_op jit(solution)/shard_map/ppermute | solution.py:411
  93.1 23.2 %collective-permute-start.4 = (bf16[2,512,256]{2,1,0:T(8,128)(2,1)S(1)}, bf16[2,512,256]{2,1,0:T(8,128)(2,1)S(1)}, u32[]{:S(2)}, u32[]{:S(2)}) collective-permute-start(bf16[2,512,256]{2,1,0:T(8,128)(2,1)S(1)} %get-tuple-element.42), channel_id=1, source_target_pairs={{0,6},{1,7},{2,0},{3,1},{4,2},{5,3},{6,4},{7,5},{8,14},{9,15},{10,... | collective-permute-start | bytes 1572872 | tf_op jit(solution)/shard_map/ppermute | solution.py:411
  117.8 9.2 %collective-permute-start.10 = (bf16[512,256]{1,0:T(8,128)(2,1)S(1)}, bf16[512,256]{1,0:T(8,128)(2,1)S(1)}, u32[]{:S(2)}, u32[]{:S(2)}) collective-permute-start(bf16[512,256]{1,0:T(8,128)(2,1)S(1)} %get-tuple-element.54), channel_id=1, source_target_pairs={{0,6},{1,7},{2,0},{3,1},{4,2},{5,3},{6,4},{7,5},{8,14},{9,15},{10,... | collective-permute-start | bytes 786440 | tf_op jit(solution)/shard_map/ppermute | solution.py:411
  120.3 14.0 %collective-permute-start.11 = (bf16[512,256]{1,0:T(8,128)(2,1)S(1)}, bf16[512,256]{1,0:T(8,128)(2,1)S(1)}, u32[]{:S(2)}, u32[]{:S(2)}) collective-permute-start(bf16[512,256]{1,0:T(8,128)(2,1)S(1)} %get-tuple-element.55), channel_id=1, source_target_pairs={{0,7},{1,6},{2,1},{3,0},{4,3},{5,2},{6,5},{7,4},{8,15},{9,14},{10,... | collective-permute-start | bytes 786440 | tf_op jit(solution)/shard_map/ppermute | solution.py:411
  120.3 18.2 %collective-permute-start.5 = (bf16[512,256]{1,0:T(8,128)(2,1)S(1)}, bf16[512,256]{1,0:T(8,128)(2,1)S(1)}, u32[]{:S(2)}, u32[]{:S(2)}) collective-permute-start(bf16[512,256]{1,0:T(8,128)(2,1)S(1)} %get-tuple-element.49), channel_id=1, source_target_pairs={{0,1},{1,0},{2,3},{3,2},{4,5},{5,4},{6,7},{7,6},{8,9},{9,8},{10,11... | collective-permute-start | bytes 786440 | tf_op jit(solution)/shard_map/ppermute | solution.py:411
  121.6 17.0 %collective-permute-start.6 = (bf16[512,256]{1,0:T(8,128)(2,1)S(1)}, bf16[512,256]{1,0:T(8,128)(2,1)S(1)}, u32[]{:S(2)}, u32[]{:S(2)}) collective-permute-start(bf16[512,256]{1,0:T(8,128)(2,1)S(1)} %get-tuple-element.50), channel_id=1, source_target_pairs={{0,2},{1,3},{2,4},{3,5},{4,6},{5,7},{6,0},{7,1},{8,10},{9,11},{10,... | collective-permute-start | bytes 786440 | tf_op jit(solution)/shard_map/ppermute | solution.py:411
  123.0 23.1 %collective-permute-start.7 = (bf16[512,256]{1,0:T(8,128)(2,1)S(1)}, bf16[512,256]{1,0:T(8,128)(2,1)S(1)}, u32[]{:S(2)}, u32[]{:S(2)}) collective-permute-start(bf16[512,256]{1,0:T(8,128)(2,1)S(1)} %get-tuple-element.51), channel_id=1, source_target_pairs={{0,3},{1,2},{2,5},{3,4},{4,7},{5,6},{6,1},{7,0},{8,11},{9,10},{10,... | collective-permute-start | bytes 786440 | tf_op jit(solution)/shard_map/ppermute | solution.py:411
  127.0 19.1 %collective-permute-start.8 = (bf16[512,256]{1,0:T(8,128)(2,1)S(1)}, bf16[512,256]{1,0:T(8,128)(2,1)S(1)}, u32[]{:S(2)}, u32[]{:S(2)}) collective-permute-start(bf16[512,256]{1,0:T(8,128)(2,1)S(1)} %get-tuple-element.52), channel_id=1, source_target_pairs={{0,4},{1,5},{2,6},{3,7},{4,0},{5,1},{6,2},{7,3},{8,12},{9,13},{10,... | collective-permute-start | bytes 786440 | tf_op jit(solution)/shard_map/ppermute | solution.py:411
  134.3 18.0 %collective-permute-start.9 = (bf16[512,256]{1,0:T(8,128)(2,1)S(1)}, bf16[512,256]{1,0:T(8,128)(2,1)S(1)}, u32[]{:S(2)}, u32[]{:S(2)}) collective-permute-start(bf16[512,256]{1,0:T(8,128)(2,1)S(1)} %get-tuple-element.53), channel_id=1, source_target_pairs={{0,5},{1,4},{2,7},{3,6},{4,1},{5,0},{6,3},{7,2},{8,13},{9,12},{10,... | collective-permute-start | bytes 786440 | tf_op jit(solution)/shard_map/ppermute | solution.py:411
  158.4 61.6 %all-to-all-start.2 = ((bf16[32,16,8,256]{3,2,1,0:T(8,128)(2,1)}), bf16[32,16,8,256]{3,2,1,0:T(8,128)(2,1)}, u32[]{:S(2)}, u32[]{:S(2)}) async-start(bf16[32,16,8,256]{3,2,1,0:T(8,128)(2,1)} %get-tuple-element.60), calls=%async_computation.2 | async-start | bytes 4194304 | tf_op jit(solution)/shard_map/all_to_all | solution.py:399
  174.2 13.7 %collective-permute-start.12 = (bf16[512,256]{1,0:T(8,128)(2,1)S(1)}, bf16[512,256]{1,0:T(8,128)(2,1)S(1)}, u32[]{:S(2)}, u32[]{:S(2)}) collective-permute-start(bf16[512,256]{1,0:T(8,128)(2,1)S(1)} %get-tuple-element.62), channel_id=1, source_target_pairs={{0,1},{1,0},{2,3},{3,2},{4,5},{5,4},{6,7},{7,6},{8,9},{9,8},{10,11... | collective-permute-start | bytes 786440 | tf_op jit(solution)/shard_map/ppermute | solution.py:411
  174.3 15.9 %collective-permute-start.13 = (bf16[512,256]{1,0:T(8,128)(2,1)S(1)}, bf16[512,256]{1,0:T(8,128)(2,1)S(1)}, u32[]{:S(2)}, u32[]{:S(2)}) collective-permute-start(bf16[512,256]{1,0:T(8,128)(2,1)S(1)} %get-tuple-element.63), channel_id=1, source_target_pairs={{0,2},{1,3},{2,4},{3,5},{4,6},{5,7},{6,0},{7,1},{8,10},{9,11},{10,... | collective-permute-start | bytes 786440 | tf_op jit(solution)/shard_map/ppermute | solution.py:411
  174.3 23.8 %collective-permute-start.14 = (bf16[512,256]{1,0:T(8,128)(2,1)}, bf16[512,256]{1,0:T(8,128)(2,1)S(1)}, u32[]{:S(2)}, u32[]{:S(2)}) collective-permute-start(bf16[512,256]{1,0:T(8,128)(2,1)} %get-tuple-element.64), channel_id=1, source_target_pairs={{0,3},{1,2},{2,5},{3,4},{4,7},{5,6},{6,1},{7,0},{8,11},{9,10},{10,... | collective-permute-start | bytes 786440 | tf_op jit(solution)/shard_map/ppermute | solution.py:411
  176.3 21.8 %collective-permute-start.15 = (bf16[512,256]{1,0:T(8,128)(2,1)}, bf16[512,256]{1,0:T(8,128)(2,1)S(1)}, u32[]{:S(2)}, u32[]{:S(2)}) collective-permute-start(bf16[512,256]{1,0:T(8,128)(2,1)} %get-tuple-element.65), channel_id=1, source_target_pairs={{0,4},{1,5},{2,6},{3,7},{4,0},{5,1},{6,2},{7,3},{8,12},{9,13},{10,... | collective-permute-start | bytes 786440 | tf_op jit(solution)/shard_map/ppermute | solution.py:411
  179.3 31.4 %collective-permute-start.16 = (bf16[512,256]{1,0:T(8,128)(2,1)}, bf16[512,256]{1,0:T(8,128)(2,1)S(1)}, u32[]{:S(2)}, u32[]{:S(2)}) collective-permute-start(bf16[512,256]{1,0:T(8,128)(2,1)} %get-tuple-element.66), channel_id=1, source_target_pairs={{0,5},{1,4},{2,7},{3,6},{4,1},{5,0},{6,3},{7,2},{8,13},{9,12},{10,... | collective-permute-start | bytes 786440 | tf_op jit(solution)/shard_map/ppermute | solution.py:411
  188.0 22.7 %collective-permute-start.17 = (bf16[512,256]{1,0:T(8,128)(2,1)S(1)}, bf16[512,256]{1,0:T(8,128)(2,1)S(1)}, u32[]{:S(2)}, u32[]{:S(2)}) collective-permute-start(bf16[512,256]{1,0:T(8,128)(2,1)S(1)} %get-tuple-element.67), channel_id=1, source_target_pairs={{0,6},{1,7},{2,0},{3,1},{4,2},{5,3},{6,4},{7,5},{8,14},{9,15},{10,... | collective-permute-start | bytes 786440 | tf_op jit(solution)/shard_map/ppermute | solution.py:411
  190.1 26.0 %collective-permute-start.18 = (bf16[512,256]{1,0:T(8,128)(2,1)S(1)}, bf16[512,256]{1,0:T(8,128)(2,1)S(1)}, u32[]{:S(2)}, u32[]{:S(2)}) collective-permute-start(bf16[512,256]{1,0:T(8,128)(2,1)S(1)} %get-tuple-element.68), channel_id=1, source_target_pairs={{0,7},{1,6},{2,1},{3,0},{4,3},{5,2},{6,5},{7,4},{8,15},{9,14},{10,... | collective-permute-start | bytes 786440 | tf_op jit(solution)/shard_map/ppermute | solution.py:411
  224.3 73.3 %all-to-all-start.3 = ((bf16[32,16,8,256]{3,2,1,0:T(8,128)(2,1)}), bf16[32,16,8,256]{3,2,1,0:T(8,128)(2,1)S(1)}, u32[]{:S(2)}, u32[]{:S(2)}) async-start(bf16[32,16,8,256]{3,2,1,0:T(8,128)(2,1)} %left_pass.3), calls=%async_computation.3 | async-start | bytes 4194304 | tf_op jit(solution)/shard_map/all_to_all | solution.py:399
  234.7 14.7 %collective-permute-start.19 = (bf16[2,512,256]{2,1,0:T(8,128)(2,1)}, bf16[2,512,256]{2,1,0:T(8,128)(2,1)S(1)}, u32[]{:S(2)}, u32[]{:S(2)}) collective-permute-start(bf16[2,512,256]{2,1,0:T(8,128)(2,1)} %copy-done.10), channel_id=1, source_target_pairs={{0,2},{1,3},{2,4},{3,5},{4,6},{5,7},{6,0},{7,1},{8,10},{9,11},{10,... | collective-permute-start | bytes 1572872 | tf_op jit(solution)/shard_map/ppermute | solution.py:411
  236.0 25.8 %collective-permute-start.20 = (bf16[2,512,256]{2,1,0:T(8,128)(2,1)}, bf16[2,512,256]{2,1,0:T(8,128)(2,1)S(1)}, u32[]{:S(2)}, u32[]{:S(2)}) collective-permute-start(bf16[2,512,256]{2,1,0:T(8,128)(2,1)} %copy-done.9), channel_id=1, source_target_pairs={{0,4},{1,5},{2,6},{3,7},{4,0},{5,1},{6,2},{7,3},{8,12},{9,13},{10,... | collective-permute-start | bytes 1572872 | tf_op jit(solution)/shard_map/ppermute | solution.py:411
  238.6 58.9 %copy-start.6 = (f32[8,512]{1,0:T(8,128)S(1)}, f32[8,512]{1,0:T(8,128)}, u32[]{:S(2)}) copy-start(f32[8,512]{1,0:T(8,128)} %tw_ref.3) | copy-start | bytes 49156
  238.6 23.2 %collective-permute-start.21 = (bf16[2,512,256]{2,1,0:T(8,128)(2,1)S(1)}, bf16[2,512,256]{2,1,0:T(8,128)(2,1)S(1)}, u32[]{:S(2)}, u32[]{:S(2)}) collective-permute-start(bf16[2,512,256]{2,1,0:T(8,128)(2,1)S(1)} %copy-done.8), channel_id=1, source_target_pairs={{0,6},{1,7},{2,0},{3,1},{4,2},{5,3},{6,4},{7,5},{8,14},{9,15},{10,... | collective-permute-start | bytes 1572872 | tf_op jit(solution)/shard_map/ppermute | solution.py:411
  267.7 29.9 %collective-permute-start.22 = (bf16[4,512,256]{2,1,0:T(8,128)(2,1)}, bf16[4,512,256]{2,1,0:T(8,128)(2,1)}, u32[]{:S(2)}, u32[]{:S(2)}) collective-permute-start(bf16[4,512,256]{2,1,0:T(8,128)(2,1)} %get-tuple-element.75), channel_id=1, source_target_pairs={{0,1},{1,0},{2,3},{3,2},{4,5},{5,4},{6,7},{7,6},{8,9},{9,8},{10,11... | collective-permute-start | bytes 3145736 | tf_op jit(solution)/shard_map/ppermute | solution.py:411
  (13 other events, 25.4 us)

commit v2 on v1

--- a/solution.py
+++ b/solution.py
@@ -11,7 +11,7 @@
 NY = 4
 
 
-def _params(mib=48):
+def _params(mib=32):
     return pltpu.CompilerParams(vmem_limit_bytes=min(mib << 20, 67043328))
 
 
@@ -139,7 +139,7 @@
             ],
             out_specs=[pl.BlockSpec(part, lambda d, s: (0, 0, 0))] * NY,
         ),
-        out_shape=[jax.ShapeDtypeStruct(part, BF16)] * NY,
+        out_shape=[_hbm(part)] * NY,
         compiler_params=_params(),
         cost_estimate=_cost(8 * half_outer * inner * chan * chan, 5 << 20),
     )(s, x3, xr, blocks, blocks_other)
@@ -181,7 +181,7 @@
             + [pl.BlockSpec((2, total // steps, chan), lambda g, s: (0, g, 0))] * NY,
             out_specs=[out_block] * (2 * NY),
         ),
-        out_shape=[jax.ShapeDtypeStruct((total, chan), BF16)] * (2 * NY),
+        out_shape=[_hbm((total, chan))] * (2 * NY),
         compiler_params=_params(),
         cost_estimate=_cost(4 * NY * NY * total * chan, 4 << 20),
     )(s, mixer, *parts)
@@ -208,7 +208,7 @@
             in_specs=[pl.BlockSpec(mixer.shape, lambda g, s: (0, 0, 0))] + [in_block] * (2 * NY),
             out_specs=[pl.BlockSpec((2, total // steps, chan), lambda g, s: (0, g, 0))] * NY,
         ),
-        out_shape=[jax.ShapeDtypeStruct((2, total, chan), BF16)] * NY,
+        out_shape=[_hbm((2, total, chan))] * NY,
         compiler_params=_params(),
         cost_estimate=_cost(4 * NY * NY * total * chan, 4 << 20),
     )(s, mixer, *pieces)
@@ -250,8 +250,8 @@
             scratch_shapes=[pltpu.VMEM((chan // 128, rows * outer, 128), F32)],
         ),
         out_shape=[
-            jax.ShapeDtypeStruct(og3.shape, BF16),
-            jax.ShapeDtypeStruct((seq, per, outer, chan), BF16),
+            _hbm(og3.shape),
+            _hbm((seq, per, outer, chan)),
         ],
         compiler_params=_params(),
         cost_estimate=_cost(outer * inner * chan, 8 << 20),
@@ -298,51 +298,46 @@
                 pltpu.VMEM((outer, rows, chan), BF16),
             ],
         ),
-        out_shape=[jax.ShapeDtypeStruct(og3.shape, BF16)] + [jax.ShapeDtypeStruct(piece, BF16)] * (2 * NY),
+        out_shape=[_hbm(og3.shape)] + [_hbm(piece)] * (2 * NY),
         compiler_params=_params(),
         cost_estimate=_cost(2 * outer * inner * chan, 10 << 20),
     )(s, wire, gate3, og3)
     return res[0], res[1:]
 
 
-def chan_kernel(s, b_ref, bo_ref, *refs):
-    parts, (own_ref, other_ref) = refs[:NY], refs[NY:]
-    d = pl.program_id(0)
-    _, _, chan = own_ref.shape
-    for i in range(NY):
-
-        @pl.when(d == i)
-        def _():
-            for k, ref in enumerate((own_ref, other_ref)):
-                cols = pl.ds(pl.multiple_of(lax.rem(s[0] + k, 2) * chan, 128), chan)
-                acc = jnp.dot(parts[i][0], b_ref[:, cols], preferred_element_type=F32)
-                acc += jnp.dot(parts[i][1], bo_ref[:, cols], preferred_element_type=F32)
-                ref[...] = acc.astype(BF16).reshape(ref.shape)
-
-
-def chan_pass(s, blocks, blocks_other, parts, half_outer):
-    _, total, chan = parts[0].shape
-    rows = total // half_outer
-    whole = pl.BlockSpec(blocks.shape, lambda d, s: (0, 0))
-    out = pl.BlockSpec((half_outer, rows, chan), lambda d, s: (0, _back(s, d), 0))
+def chan_kernel(s, b_ref, bo_ref, part_ref, own_ref, other_ref):
+    chan = own_ref.shape[1]
+    for k, ref in enumerate((own_ref, other_ref)):
+        cols = pl.ds(pl.multiple_of(lax.rem(s[0] + k, 2) * chan, 128), chan)
+        acc = jnp.dot(part_ref[0], b_ref[:, cols], preferred_element_type=F32)
+        acc += jnp.dot(part_ref[1], bo_ref[:, cols], preferred_element_type=F32)
+        ref[...] = acc.astype(BF16)
+
+
+def chan_pass(s, blocks, blocks_other, part):
+    _, total, chan = part.shape
+    whole = pl.BlockSpec(blocks.shape, lambda i, s: (0, 0))
+    out = pl.BlockSpec((total, chan), lambda i, s: (0, 0))
     return pl.pallas_call(
         chan_kernel,
         name="chan_pass",
         grid_spec=pltpu.PrefetchScalarGridSpec(
             num_scalar_prefetch=1,
-            grid=(NY,),
-            in_specs=[whole, whole] + [pl.BlockSpec(parts[0].shape, lambda d, s: (0, 0, 0))] * NY,
+            grid=(1,),
+            in_specs=[whole, whole, pl.BlockSpec(part.shape, lambda i, s: (0, 0, 0))],
             out_specs=[out, out],
         ),
-        out_shape=[jax.ShapeDtypeStruct((half_outer, rows * NY, chan), BF16)] * 2,
-        compiler_params=_params(),
-        cost_estimate=_cost(8 * total * NY * chan * chan, 5 << 20),
-    )(s, blocks, blocks_other, *parts)
-
-
-def tail_kernel(s, wire_ref, rt_ref, tw_ref, own_ref, other_ref, out_ref, scr):
+        out_shape=[_hbm((total, chan))] * 2,
+        compiler_params=_params(),
+        cost_estimate=_cost(8 * total * chan * chan, 2 << 20),
+    )(s, blocks, blocks_other, part)
+
+
+def tail_kernel(s, wire_ref, rt_ref, tw_ref, *refs):
+    own, other, (out_ref, scr, total_ref) = refs[:NY], refs[NY : 2 * NY], refs[2 * NY :]
     outer, inner = tw_ref.shape
     chan = out_ref.shape[2]
+    rows = inner // NY
     a = pl.program_id(0)
 
     @pl.when(a == 0)
@@ -354,24 +349,26 @@
     parts = []
     for c in range(chan // 128):
         parts.append((scr[c, pl.ds(a, inner, stride=outer), :] * col).astype(BF16))
-    acc = jnp.dot(rt_ref[...], jnp.concatenate(parts, axis=1), preferred_element_type=F32)
+    total_ref[...] = jnp.dot(rt_ref[...], jnp.concatenate(parts, axis=1), preferred_element_type=F32)
     mine = a // (outer // 2) == lax.rem(s[0], 2)
 
-    @pl.when(mine)
-    def _():
-        out_ref[0] = (acc + own_ref[0].astype(F32)).astype(BF16)
-
-    @pl.when(jnp.logical_not(mine))
-    def _():
-        out_ref[0] = (acc + other_ref[0].astype(F32)).astype(BF16)
+    def finish(refs):
+        for d in range(NY):
+            at = pl.ds(pl.multiple_of(_back(s, d) * rows, rows), rows)
+            out_ref[0, at, :] = (total_ref[at, :] + refs[d][...].astype(F32)).astype(BF16)
+
+    pl.when(mine)(lambda: finish(own))
+    pl.when(jnp.logical_not(mine))(lambda: finish(other))
 
 
 def tail_pass(s, wire, right_t, twiddle, own, other):
-    half_outer, inner, chan = own.shape
-    outer = 2 * half_outer
+    outer, inner = twiddle.shape
+    chan = wire.shape[3]
+    half_outer, rows = outer // 2, inner // NY
 
     def part(k):
-        return lambda a, s: (jnp.clip(a - lax.rem(s[0] + k, 2) * half_outer, 0, half_outer - 1), 0, 0)
+        block = (rows, chan)
+        return pl.BlockSpec(block, lambda a, s: (jnp.clip(a - lax.rem(s[0] + k, 2) * half_outer, 0, half_outer - 1), 0))
 
     return pl.pallas_call(
         tail_kernel,
@@ -383,16 +380,16 @@
                 pl.BlockSpec(wire.shape, lambda a, s: (0, 0, 0, 0)),
                 pl.BlockSpec(right_t.shape, lambda a, s: (0, 0)),
                 pl.BlockSpec(twiddle.shape, lambda a, s: (0, 0)),
-                pl.BlockSpec((1, inner, chan), part(0)),
-                pl.BlockSpec((1, inner, chan), part(1)),
-            ],
+            ]
+            + [part(0)] * NY
+            + [part(1)] * NY,
             out_specs=pl.BlockSpec((1, inner, chan), lambda a, s: (a, 0, 0)),
-            scratch_shapes=[pltpu.VMEM((chan // 128, outer * inner, 128), F32)],
+            scratch_shapes=[pltpu.VMEM((chan // 128, outer * inner, 128), F32), pltpu.VMEM((inner, chan), F32)],
         ),
         out_shape=jax.ShapeDtypeStruct((outer, inner, chan), BF16),
-        compiler_params=_params(),
+        compiler_params=_params(64),
         cost_estimate=_cost(2 * outer * inner * inner * chan, 7 << 20),
-    )(s, wire, right_t, twiddle, own, other)
+    )(s, wire, right_t, twiddle, *own, *other)
 
 
 def seq_swap(wire):
@@ -427,13 +424,12 @@
     blocks_other = send(blocks, 0, 1)
     twisted = seq_swap(right_pass(x3, right_factor, twiddle, seq))
     middle = middle_pass(s, x3, xr, blocks, blocks_other)
-    twisted, _ = lax.optimization_barrier((twisted, middle[0]))
+    middle = around(middle)
+    pieces = mix_pass(s, mixer, middle)
+    twisted, _ = lax.optimization_barrier((twisted, pieces[0]))
     mixed_wire = left_pass(left_factor, twisted)
 
-    middle = around(middle)
-    *middle, _ = lax.optimization_barrier((*middle, mixed_wire))
     mixed = seq_swap(mixed_wire)
-    pieces = mix_pass(s, mixer, middle)
     pieces = across(pieces)
     gate3, grad_mixed = gate_pass(s, og3, pieces, seq)
 
@@ -447,8 +443,12 @@
 
     grad_middle = around(grad_middle)
     grad_twisted = seq_swap(grad_wire)
-    own, other = chan_pass(s, blocks, blocks_other, grad_middle, outer // 2)
-    other = send(other, 0, 1)
+    own, other = [], []
+    for d in (0, 1, 3, 2):
+        mine, away = chan_pass(s, blocks, blocks_other, grad_middle[d])
+        own.append(mine)
+        other.append(send(away, 0, 1))
+    own, other = ([v[i] for i in (0, 1, 3, 2)] for v in (own, other))
     input_grad = tail_pass(s, grad_twisted, right_factor.T, twiddle, own, other)
     return (output.reshape(inputs.shape), input_grad.reshape(inputs.shape))
 

time: 307 us -> 307 us (level)
  local copies, waits for them, and re-layouts: 13.9 us -> 6.16 us
  Pallas kernels: 37.4 us -> 43 us
    unnamed x38 -> x28, local copies, waits for them, and re-layouts: 12.4 us -> 4.72 us
    ppermute x23 -> x26, waiting for transfers between devices: 180 us -> 181 us  [send(): lax.ppermute(v, 'chan', [(c, (c // 2 + d) % NY * 2 + c % 2 ^ k) for c in...]
    ppermute x23 -> x26, starting transfers between devices: 29.8 us -> 28.8 us  [send(): lax.ppermute(v, 'chan', [(c, (c // 2 + d) % NY * 2 + c % 2 ^ k) for c in...]
  transfers between devices with their start and end apart: 27 -> 30, of which waited for: 15 -> 17; matrix products, arithmetic and copies ran while one was open for 1% -> 1% of each run, Pallas kernels for 6% -> 7%
where the time goes in v2:
time: 307 us; the launch traced here: 306 us
  waiting for transfers between devices  182 us (59%)
  starting transfers between devices  74 us (24%)
  Pallas kernels  43 us (14%)
  local copies, waits for them, and re-layouts  6.16 us (2%)
    ppermute x26, waiting for transfers between devices, send(): lax.ppermute(v, 'chan', [(c, (c // 2 + d) % NY * 2 + c % 2 ^ k) for c in...  181 us
    all_to_all x4, starting transfers between devices, seq_swap(): return lax.all_to_all(wire, 'seq', split_axis=0, concat_axis=0, tiled=True)  45.2 us
    ppermute x26, starting transfers between devices, send(): lax.ppermute(v, 'chan', [(c, (c // 2 + d) % NY * 2 + c % 2 ^ k) for c in...  28.8 us
    pallas_call x1, Pallas kernels, tail_pass(): pl.pallas_call(tail_kernel, name='tail_pass', grid_spec=pltpu.PrefetchSca...  9.07 us
    pallas_call x2, Pallas kernels, left_pass(): pl.pallas_call(left_kernel, name='left_pass', grid=(steps,), in_specs=[pl...  6.98 us
  transfers between devices with their start and end apart: 30, of which 17 were waited for; matrix products, arithmetic and copies ran while one was open for 1% of the time, Pallas kernels for 7%

profile of v2, /device:TPU:1, one launch (start us, length us, event | category | flops | bytes accessed | tf_op | source)
XLA Modules:
  0.0 305.7 jit_solution(4577080712417335420)
XLA Ops:
  0.6 4.6 %right_pass.1 = bf16[32,16,8,256]{3,2,1,0:T(8,128)(2,1)} custom-call(bf16[8,512,256]{2,1,0:T(8,128)(2,1)} %bitcast.10, bf16[512,512]{1,0:T(8,128)(2,1)} %r_ref.1, f32[8,512]{1,0:T(8,128)} %tw_ref.3), custom_call_target="tpu_custom_call" | custom-call | flops 1073741824 | bytes 6291456 | tf_op jit(solution)/shard_map/right_pass/pallas_call | solution.py:55
  5.2 12.7 %all-to-all-start = ((bf16[32,16,8,256]{3,2,1,0:T(8,128)(2,1)}), bf16[32,16,8,256]{3,2,1,0:T(8,128)(2,1)S(1)}, u32[]{:S(2)}, u32[]{:S(2)}) async-start(bf16[32,16,8,256]{3,2,1,0:T(8,128)(2,1)} %right_pass.1), calls=%async_computation | async-start | bytes 4194304 | tf_op jit(solution)/shard_map/all_to_all | solution.py:396
  20.9 48.8 %collective-permute-done.1.bo_ref = bf16[256,512]{1,0:T(8,128)(2,1)S(1)} collective-permute-done((bf16[256,512]{1,0:T(8,128)(2,1)S(1)}, bf16[256,512]{1,0:T(8,128)(2,1)S(1)}, u32[]{:S(2)}, u32[]{:S(2)}) %collective-permute-start.1) | collective-permute-done | bytes 262176 | tf_op jit(solution)/shard_map/ppermute | solution.py:408
  69.7 3.9 %middle_pass.1 = (bf16[2,512,256]{2,1,0:T(8,128)(2,1)}, bf16[2,512,256]{2,1,0:T(8,128)(2,1)}, bf16[2,512,256]{2,1,0:T(8,128)(2,1)}, bf16[2,512,256]{2,1,0:T(8,128)(2,1)}) custom-call(s32[1]{0:T(128)} %bitcast.s, bf16[8,512,256]{2,1,0:T(8,128)(2,1)S(1)} %bitcast.12, bf16[4,512,256]{2,1,0:T(8,128)(2,1)S(1)} %collective-permute-done.xr_ref, ...), custom_call_target="tpu_custom_call" | custom-call | flops 1073741824 | bytes 5242880 | tf_op jit(solution)/shard_map/middle_pass/pallas_call | solution.py:128
  74.9 2.6 collective-permute-start.3
  78.6 9.2 %collective-permute-done.2.refs_1_ = bf16[2,512,256]{2,1,0:T(8,128)(2,1)S(1)} collective-permute-done((bf16[2,512,256]{2,1,0:T(8,128)(2,1)}, bf16[2,512,256]{2,1,0:T(8,128)(2,1)S(1)}, u32[]{:S(2)}, u32[]{:S(2)}) %collective-permute-start.2) | collective-permute-done | bytes 524320 | tf_op jit(solution)/shard_map/ppermute | solution.py:408
  87.8 12.4 %collective-permute-done.3.refs_2_ = bf16[2,512,256]{2,1,0:T(8,128)(2,1)S(1)} collective-permute-done((bf16[2,512,256]{2,1,0:T(8,128)(2,1)}, bf16[2,512,256]{2,1,0:T(8,128)(2,1)S(1)}, u32[]{:S(2)}, u32[]{:S(2)}) %collective-permute-start.3) | collective-permute-done | bytes 524320 | tf_op jit(solution)/shard_map/ppermute | solution.py:408
  103.5 2.6 left_pass.2
  106.2 11.8 %all-to-all-start.1 = ((bf16[32,16,8,256]{3,2,1,0:T(8,128)(2,1)}), bf16[32,16,8,256]{3,2,1,0:T(8,128)(2,1)}, u32[]{:S(2)}, u32[]{:S(2)}) async-start(bf16[32,16,8,256]{3,2,1,0:T(8,128)(2,1)} %left_pass.2), calls=%async_computation.1 | async-start | bytes 4194304 | tf_op jit(solution)/shard_map/all_to_all | solution.py:396
  122.5 5.8 %collective-permute-done.10.refs_6_ = bf16[512,256]{1,0:T(8,128)(2,1)S(1)} collective-permute-done((bf16[512,256]{1,0:T(8,128)(2,1)}, bf16[512,256]{1,0:T(8,128)(2,1)S(1)}, u32[]{:S(2)}, u32[]{:S(2)}) %collective-permute-start.10) | collective-permute-done | bytes 262176 | tf_op jit(solution)/shard_map/ppermute | solution.py:408
  128.3 2.7 collective-permute-start.8
  131.0 4.5 %collective-permute-done.11.refs_7_ = bf16[512,256]{1,0:T(8,128)(2,1)S(1)} collective-permute-done((bf16[512,256]{1,0:T(8,128)(2,1)}, bf16[512,256]{1,0:T(8,128)(2,1)S(1)}, u32[]{:S(2)}, u32[]{:S(2)}) %collective-permute-start.11) | collective-permute-done | bytes 262176 | tf_op jit(solution)/shard_map/ppermute | solution.py:408
  135.5 3.4 %collective-permute-start.9 = (bf16[512,256]{1,0:T(8,128)(2,1)S(1)}, bf16[512,256]{1,0:T(8,128)(2,1)S(1)}, u32[]{:S(2)}, u32[]{:S(2)}) collective-permute-start(bf16[512,256]{1,0:T(8,128)(2,1)S(1)} %copy-done.12), channel_id=1, source_target_pairs={{0,5},{1,4},{2,7},{3,6},{4,1},{5,0},{6,3},{7,2},{8,13},{9,12},{10,... | collective-permute-start | bytes 786440 | tf_op jit(solution)/shard_map/ppermute | solution.py:408
  138.9 4.4 %collective-permute-done.5.refs_1_ = bf16[512,256]{1,0:T(8,128)(2,1)S(1)} collective-permute-done((bf16[512,256]{1,0:T(8,128)(2,1)}, bf16[512,256]{1,0:T(8,128)(2,1)S(1)}, u32[]{:S(2)}, u32[]{:S(2)}) %collective-permute-start.5) | collective-permute-done | bytes 262176 | tf_op jit(solution)/shard_map/ppermute | solution.py:408
  143.3 11.4 %collective-permute-done.7.refs_3_ = bf16[512,256]{1,0:T(8,128)(2,1)S(1)} collective-permute-done((bf16[512,256]{1,0:T(8,128)(2,1)}, bf16[512,256]{1,0:T(8,128)(2,1)S(1)}, u32[]{:S(2)}, u32[]{:S(2)}) %collective-permute-start.7) | collective-permute-done | bytes 262176 | tf_op jit(solution)/shard_map/ppermute | solution.py:408
  154.7 11.1 %collective-permute-done.9.refs_5_ = bf16[512,256]{1,0:T(8,128)(2,1)S(1)} collective-permute-done((bf16[512,256]{1,0:T(8,128)(2,1)S(1)}, bf16[512,256]{1,0:T(8,128)(2,1)S(1)}, u32[]{:S(2)}, u32[]{:S(2)}) %collective-permute-start.9) | collective-permute-done | bytes 262176 | tf_op jit(solution)/shard_map/ppermute | solution.py:408
  165.9 3.6 %gate_pass.1 = (bf16[8,512,256]{2,1,0:T(8,128)(2,1)}, bf16[32,16,8,256]{3,2,1,0:T(8,128)(2,1)}) custom-call(s32[1]{0:T(128)} %bitcast.s, bf16[8,512,256]{2,1,0:T(8,128)(2,1)S(1)} %bitcast.8, bf16[512,256]{1,0:T(8,128)(2,1)S(1)} %copy-done.7, bf16[512,256]{1,0:T(8,128)(2,1)S(1)} %collective-permute-done.5.refs_1_, ...), custom_call_target="tpu_custom_call" | custom-call | flops 1048576 | bytes 8388608 | tf_op jit(solution)/shard_map/gate_pass/pallas_call | solution.py:242
  169.4 10.9 %all-to-all-start.2 = ((bf16[32,16,8,256]{3,2,1,0:T(8,128)(2,1)}), bf16[32,16,8,256]{3,2,1,0:T(8,128)(2,1)}, u32[]{:S(2)}, u32[]{:S(2)}) async-start(bf16[32,16,8,256]{3,2,1,0:T(8,128)(2,1)} %get-tuple-element.58), calls=%async_computation.2 | async-start | bytes 4194304 | tf_op jit(solution)/shard_map/all_to_all | solution.py:396
  181.9 5.5 %out_pass.1 = (bf16[8,512,256]{2,1,0:T(8,128)(2,1)}, bf16[512,256]{1,0:T(8,128)(2,1)}, bf16[512,256]{1,0:T(8,128)(2,1)}, bf16[512,256]{1,0:T(8,128)(2,1)}, bf16[...) custom-call(s32[1]{0:T(128)} %bitcast.s, ...), custom_call_target="tpu_custom_call" | custom-call | flops 2097152 | bytes 10485760 | tf_op jit(solution)/shard_map/out_pass/pallas_call | solution.py:288
  189.1 3.4 %collective-permute-start.15 = (bf16[512,256]{1,0:T(8,128)(2,1)}, bf16[512,256]{1,0:T(8,128)(2,1)S(1)}, u32[]{:S(2)}, u32[]{:S(2)}) collective-permute-start(bf16[512,256]{1,0:T(8,128)(2,1)} %get-tuple-element.63), channel_id=1, source_target_pairs={{0,4},{1,5},{2,6},{3,7},{4,0},{5,1},{6,2},{7,3},{8,12},{9,13},{10,... | collective-permute-start | bytes 786440 | tf_op jit(solution)/shard_map/ppermute | solution.py:408
  192.5 10.6 %collective-permute-done.12.refs_1_ = bf16[512,256]{1,0:T(8,128)(2,1)S(1)} collective-permute-done((bf16[512,256]{1,0:T(8,128)(2,1)}, bf16[512,256]{1,0:T(8,128)(2,1)S(1)}, u32[]{:S(2)}, u32[]{:S(2)}) %collective-permute-start.12) | collective-permute-done | bytes 262176 | tf_op jit(solution)/shard_map/ppermute | solution.py:408
  204.3 6.2 %collective-permute-done.14.refs_3_ = bf16[512,256]{1,0:T(8,128)(2,1)S(1)} collective-permute-done((bf16[512,256]{1,0:T(8,128)(2,1)}, bf16[512,256]{1,0:T(8,128)(2,1)S(1)}, u32[]{:S(2)}, u32[]{:S(2)}) %collective-permute-start.14) | collective-permute-done | bytes 262176 | tf_op jit(solution)/shard_map/ppermute | solution.py:408
  210.5 13.7 %collective-permute-done.16.refs_5_ = bf16[512,256]{1,0:T(8,128)(2,1)S(1)} collective-permute-done((bf16[512,256]{1,0:T(8,128)(2,1)}, bf16[512,256]{1,0:T(8,128)(2,1)S(1)}, u32[]{:S(2)}, u32[]{:S(2)}) %collective-permute-start.16) | collective-permute-done | bytes 262176 | tf_op jit(solution)/shard_map/ppermute | solution.py:408
  224.2 5.0 %collective-permute-done.18.refs_7_ = bf16[512,256]{1,0:T(8,128)(2,1)S(1)} collective-permute-done((bf16[512,256]{1,0:T(8,128)(2,1)}, bf16[512,256]{1,0:T(8,128)(2,1)S(1)}, u32[]{:S(2)}, u32[]{:S(2)}) %collective-permute-start.18) | collective-permute-done | bytes 262176 | tf_op jit(solution)/shard_map/ppermute | solution.py:408
  232.4 4.3 %left_pass.3 = bf16[32,16,8,256]{3,2,1,0:T(8,128)(2,1)} custom-call(bf16[256,256]{1,0:T(8,128)(2,1)S(1)} %bitcast.13, bf16[32,16,8,256]{3,2,1,0:T(8,128)(2,1)} %all-to-all-done.2.in_ref), custom_call_target="tpu_custom_call" | custom-call | flops 536870912 | bytes 4194304 | tf_op jit(solution)/shard_map/left_pass/pallas_call | solution.py:85
  236.7 9.8 %all-to-all-start.3 = ((bf16[32,16,8,256]{3,2,1,0:T(8,128)(2,1)}), bf16[32,16,8,256]{3,2,1,0:T(8,128)(2,1)}, u32[]{:S(2)}, u32[]{:S(2)}) async-start(bf16[32,16,8,256]{3,2,1,0:T(8,128)(2,1)} %left_pass.3), calls=%async_computation.3 | async-start | bytes 4194304 | tf_op jit(solution)/shard_map/all_to_all | solution.py:396
  246.6 3.4 %collective-permute-start.20 = (bf16[2,512,256]{2,1,0:T(8,128)(2,1)}, bf16[2,512,256]{2,1,0:T(8,128)(2,1)S(1)}, u32[]{:S(2)}, u32[]{:S(2)}) collective-permute-start(bf16[2,512,256]{2,1,0:T(8,128)(2,1)} %get-tuple-element.72), channel_id=1, source_target_pairs={{0,4},{1,5},{2,6},{3,7},{4,0},{5,1},{6,2},{7,3},{8,12},{9,13},{10,... | collective-permute-start | bytes 1572872 | tf_op jit(solution)/shard_map/ppermute | solution.py:408
  251.8 9.5 %collective-permute-done.19.part_ref = bf16[2,512,256]{2,1,0:T(8,128)(2,1)S(1)} collective-permute-done((bf16[2,512,256]{2,1,0:T(8,128)(2,1)}, bf16[2,512,256]{2,1,0:T(8,128)(2,1)S(1)}, u32[]{:S(2)}, u32[]{:S(2)}) %collective-permute-start.19) | collective-permute-done | bytes 524320 | tf_op jit(solution)/shard_map/ppermute | solution.py:408
  262.5 10.8 %collective-permute-done.20.part_ref = bf16[2,512,256]{2,1,0:T(8,128)(2,1)S(1)} collective-permute-done((bf16[2,512,256]{2,1,0:T(8,128)(2,1)}, bf16[2,512,256]{2,1,0:T(8,128)(2,1)S(1)}, u32[]{:S(2)}, u32[]{:S(2)}) %collective-permute-start.20) | collective-permute-done | bytes 524320 | tf_op jit(solution)/shard_map/ppermute | solution.py:408
  278.2 12.0 %collective-permute-done.24.refs_6_ = bf16[512,256]{1,0:T(8,128)(2,1)} collective-permute-done((bf16[512,256]{1,0:T(8,128)(2,1)}, bf16[512,256]{1,0:T(8,128)(2,1)}, u32[]{:S(2)}, u32[]{:S(2)}) %collective-permute-start.24) | collective-permute-done | bytes 262176 | tf_op jit(solution)/shard_map/ppermute | solution.py:408
  290.2 5.7 %collective-permute-done.25.refs_7_ = bf16[512,256]{1,0:T(8,128)(2,1)} collective-permute-done((bf16[512,256]{1,0:T(8,128)(2,1)}, bf16[512,256]{1,0:T(8,128)(2,1)}, u32[]{:S(2)}, u32[]{:S(2)}) %collective-permute-start.25) | collective-permute-done | bytes 262176 | tf_op jit(solution)/shard_map/ppermute | solution.py:408
  296.6 9.1 %tail_pass.1 = bf16[8,512,256]{2,1,0:T(8,128)(2,1)} custom-call(s32[1]{0:T(128)} %bitcast.s, bf16[32,16,8,256]{3,2,1,0:T(8,128)(2,1)} %all-to-all-done.3.wire_ref, bf16[512,512]{1,0:T(8,128)(2,1)} %bitcast.17, f32[8,512]{1,0:T(8,128)} %tw_ref.3, bf16[512,256]{1,0:T(8,128)(2,1)} %get-tuple-element.69.refs_0_, bf16[512,256]{1,0:T(8,128)(2,1)} %get-tuple-element.71.refs_1_, ...), custom_call_target="tpu_custom_call" | custom-call | flops 1073741824 | bytes 7340032 | tf_op jit(solution)/shard_map/tail_pass/pallas_call | solution.py:373
  (70 shorter events, 29.6 us)
Async XLA Ops:
  5.2 98.3 %all-to-all-start = ((bf16[32,16,8,256]{3,2,1,0:T(8,128)(2,1)}), bf16[32,16,8,256]{3,2,1,0:T(8,128)(2,1)S(1)}, u32[]{:S(2)}, u32[]{:S(2)}) async-start(bf16[32,16,8,256]{3,2,1,0:T(8,128)(2,1)} %right_pass.1), calls=%async_computation | async-start | bytes 4194304 | tf_op jit(solution)/shard_map/all_to_all | solution.py:396
  19.4 80.8 %copy-start.9 = (f32[512,4,4]{0,2,1:T(4,128)S(1)}, f32[512,4,4]{0,2,1:T(4,128)}, u32[]{:S(2)}) copy-start(f32[512,4,4]{0,2,1:T(4,128)} %param.12) | copy-start | bytes 98308
  19.4 50.3 %collective-permute-start = (bf16[4,512,256]{2,1,0:T(8,128)(2,1)S(1)}, bf16[4,512,256]{2,1,0:T(8,128)(2,1)S(1)}, u32[]{:S(2)}, u32[]{:S(2)}) collective-permute-start(bf16[4,512,256]{2,1,0:T(8,128)(2,1)S(1)} %constant_dynamic-slice_fusion), channel_id=1, source_target_pairs={{0,1},{1,0},{2,3},{3,2},{4,5},{5,4},{6,7},{7,6},{8,9},{9,8},{10,11... | collective-permute-start | bytes 3145736 | tf_op jit(solution)/shard_map/ppermute | solution.py:408
  19.8 49.9 %collective-permute-start.1 = (bf16[256,512]{1,0:T(8,128)(2,1)S(1)}, bf16[256,512]{1,0:T(8,128)(2,1)S(1)}, u32[]{:S(2)}, u32[]{:S(2)}) collective-permute-start(bf16[256,512]{1,0:T(8,128)(2,1)S(1)} %copy-done.2), channel_id=1, source_target_pairs={{0,1},{1,0},{2,3},{3,2},{4,5},{5,4},{6,7},{7,6},{8,9},{9,8},{10,11... | collective-permute-start | bytes 786440 | tf_op jit(solution)/shard_map/ppermute | solution.py:408
  73.6 14.2 %collective-permute-start.2 = (bf16[2,512,256]{2,1,0:T(8,128)(2,1)}, bf16[2,512,256]{2,1,0:T(8,128)(2,1)S(1)}, u32[]{:S(2)}, u32[]{:S(2)}) collective-permute-start(bf16[2,512,256]{2,1,0:T(8,128)(2,1)} %get-tuple-element.42), channel_id=1, source_target_pairs={{0,2},{1,3},{2,4},{3,5},{4,6},{5,7},{6,0},{7,1},{8,10},{9,11},{10,... | collective-permute-start | bytes 1572872 | tf_op jit(solution)/shard_map/ppermute | solution.py:408
  74.9 25.3 %collective-permute-start.3 = (bf16[2,512,256]{2,1,0:T(8,128)(2,1)}, bf16[2,512,256]{2,1,0:T(8,128)(2,1)S(1)}, u32[]{:S(2)}, u32[]{:S(2)}) collective-permute-start(bf16[2,512,256]{2,1,0:T(8,128)(2,1)} %get-tuple-element.43), channel_id=1, source_target_pairs={{0,4},{1,5},{2,6},{3,7},{4,0},{5,1},{6,2},{7,3},{8,12},{9,13},{10,... | collective-permute-start | bytes 1572872 | tf_op jit(solution)/shard_map/ppermute | solution.py:408
  77.5 22.6 %collective-permute-start.4 = (bf16[2,512,256]{2,1,0:T(8,128)(2,1)}, bf16[2,512,256]{2,1,0:T(8,128)(2,1)S(1)}, u32[]{:S(2)}, u32[]{:S(2)}) collective-permute-start(bf16[2,512,256]{2,1,0:T(8,128)(2,1)} %get-tuple-element.44), channel_id=1, source_target_pairs={{0,6},{1,7},{2,0},{3,1},{4,2},{5,3},{6,4},{7,5},{8,14},{9,15},{10,... | collective-permute-start | bytes 1572872 | tf_op jit(solution)/shard_map/ppermute | solution.py:408
  106.2 59.7 %copy-start.7 = (bf16[512,256]{1,0:T(8,128)(2,1)S(1)}, bf16[512,256]{1,0:T(8,128)(2,1)}, u32[]{:S(2)}) copy-start(bf16[512,256]{1,0:T(8,128)(2,1)} %get-tuple-element.45.refs_0_) | copy-start | bytes 786436
  106.2 63.2 %all-to-all-start.1 = ((bf16[32,16,8,256]{3,2,1,0:T(8,128)(2,1)}), bf16[32,16,8,256]{3,2,1,0:T(8,128)(2,1)}, u32[]{:S(2)}, u32[]{:S(2)}) async-start(bf16[32,16,8,256]{3,2,1,0:T(8,128)(2,1)} %left_pass.2), calls=%async_computation.1 | async-start | bytes 4194304 | tf_op jit(solution)/shard_map/all_to_all | solution.py:396
  118.0 10.3 %collective-permute-start.10 = (bf16[512,256]{1,0:T(8,128)(2,1)}, bf16[512,256]{1,0:T(8,128)(2,1)S(1)}, u32[]{:S(2)}, u32[]{:S(2)}) collective-permute-start(bf16[512,256]{1,0:T(8,128)(2,1)} %get-tuple-element.51), channel_id=1, source_target_pairs={{0,6},{1,7},{2,0},{3,1},{4,2},{5,3},{6,4},{7,5},{8,14},{9,15},{10,... | collective-permute-start | bytes 786440 | tf_op jit(solution)/shard_map/ppermute | solution.py:408
  119.9 15.6 %collective-permute-start.11 = (bf16[512,256]{1,0:T(8,128)(2,1)}, bf16[512,256]{1,0:T(8,128)(2,1)S(1)}, u32[]{:S(2)}, u32[]{:S(2)}) collective-permute-start(bf16[512,256]{1,0:T(8,128)(2,1)} %get-tuple-element.52), channel_id=1, source_target_pairs={{0,7},{1,6},{2,1},{3,0},{4,3},{5,2},{6,5},{7,4},{8,15},{9,14},{10,... | collective-permute-start | bytes 786440 | tf_op jit(solution)/shard_map/ppermute | solution.py:408
  120.5 22.8 %collective-permute-start.5 = (bf16[512,256]{1,0:T(8,128)(2,1)}, bf16[512,256]{1,0:T(8,128)(2,1)S(1)}, u32[]{:S(2)}, u32[]{:S(2)}) collective-permute-start(bf16[512,256]{1,0:T(8,128)(2,1)} %get-tuple-element.46), channel_id=1, source_target_pairs={{0,1},{1,0},{2,3},{3,2},{4,5},{5,4},{6,7},{7,6},{8,9},{9,8},{10,11... | collective-permute-start | bytes 786440 | tf_op jit(solution)/shard_map/ppermute | solution.py:408
  121.9 21.5 %collective-permute-start.6 = (bf16[512,256]{1,0:T(8,128)(2,1)}, bf16[512,256]{1,0:T(8,128)(2,1)S(1)}, u32[]{:S(2)}, u32[]{:S(2)}) collective-permute-start(bf16[512,256]{1,0:T(8,128)(2,1)} %get-tuple-element.47), channel_id=1, source_target_pairs={{0,2},{1,3},{2,4},{3,5},{4,6},{5,7},{6,0},{7,1},{8,10},{9,11},{10,... | collective-permute-start | bytes 786440 | tf_op jit(solution)/shard_map/ppermute | solution.py:408
  122.5 32.2 %collective-permute-start.7 = (bf16[512,256]{1,0:T(8,128)(2,1)}, bf16[512,256]{1,0:T(8,128)(2,1)S(1)}, u32[]{:S(2)}, u32[]{:S(2)}) collective-permute-start(bf16[512,256]{1,0:T(8,128)(2,1)} %get-tuple-element.48), channel_id=1, source_target_pairs={{0,3},{1,2},{2,5},{3,4},{4,7},{5,6},{6,1},{7,0},{8,11},{9,10},{10,... | collective-permute-start | bytes 786440 | tf_op jit(solution)/shard_map/ppermute | solution.py:408
  128.3 26.4 %collective-permute-start.8 = (bf16[512,256]{1,0:T(8,128)(2,1)}, bf16[512,256]{1,0:T(8,128)(2,1)S(1)}, u32[]{:S(2)}, u32[]{:S(2)}) collective-permute-start(bf16[512,256]{1,0:T(8,128)(2,1)} %get-tuple-element.49), channel_id=1, source_target_pairs={{0,4},{1,5},{2,6},{3,7},{4,0},{5,1},{6,2},{7,3},{8,12},{9,13},{10,... | collective-permute-start | bytes 786440 | tf_op jit(solution)/shard_map/ppermute | solution.py:408
  135.5 30.3 %collective-permute-start.9 = (bf16[512,256]{1,0:T(8,128)(2,1)S(1)}, bf16[512,256]{1,0:T(8,128)(2,1)S(1)}, u32[]{:S(2)}, u32[]{:S(2)}) collective-permute-start(bf16[512,256]{1,0:T(8,128)(2,1)S(1)} %copy-done.12), channel_id=1, source_target_pairs={{0,5},{1,4},{2,7},{3,6},{4,1},{5,0},{6,3},{7,2},{8,13},{9,12},{10,... | collective-permute-start | bytes 786440 | tf_op jit(solution)/shard_map/ppermute | solution.py:408
  169.4 63.0 %all-to-all-start.2 = ((bf16[32,16,8,256]{3,2,1,0:T(8,128)(2,1)}), bf16[32,16,8,256]{3,2,1,0:T(8,128)(2,1)}, u32[]{:S(2)}, u32[]{:S(2)}) async-start(bf16[32,16,8,256]{3,2,1,0:T(8,128)(2,1)} %get-tuple-element.58), calls=%async_computation.2 | async-start | bytes 4194304 | tf_op jit(solution)/shard_map/all_to_all | solution.py:396
  187.4 15.7 %collective-permute-start.12 = (bf16[512,256]{1,0:T(8,128)(2,1)}, bf16[512,256]{1,0:T(8,128)(2,1)S(1)}, u32[]{:S(2)}, u32[]{:S(2)}) collective-permute-start(bf16[512,256]{1,0:T(8,128)(2,1)} %get-tuple-element.60), channel_id=1, source_target_pairs={{0,1},{1,0},{2,3},{3,2},{4,5},{5,4},{6,7},{7,6},{8,9},{9,8},{10,11... | collective-permute-start | bytes 786440 | tf_op jit(solution)/shard_map/ppermute | solution.py:408
  187.6 16.5 %collective-permute-start.13 = (bf16[512,256]{1,0:T(8,128)(2,1)}, bf16[512,256]{1,0:T(8,128)(2,1)S(1)}, u32[]{:S(2)}, u32[]{:S(2)}) collective-permute-start(bf16[512,256]{1,0:T(8,128)(2,1)} %get-tuple-element.61), channel_id=1, source_target_pairs={{0,2},{1,3},{2,4},{3,5},{4,6},{5,7},{6,0},{7,1},{8,10},{9,11},{10,... | collective-permute-start | bytes 786440 | tf_op jit(solution)/shard_map/ppermute | solution.py:408
  187.7 22.8 %collective-permute-start.14 = (bf16[512,256]{1,0:T(8,128)(2,1)}, bf16[512,256]{1,0:T(8,128)(2,1)S(1)}, u32[]{:S(2)}, u32[]{:S(2)}) collective-permute-start(bf16[512,256]{1,0:T(8,128)(2,1)} %get-tuple-element.62), channel_id=1, source_target_pairs={{0,3},{1,2},{2,5},{3,4},{4,7},{5,6},{6,1},{7,0},{8,11},{9,10},{10,... | collective-permute-start | bytes 786440 | tf_op jit(solution)/shard_map/ppermute | solution.py:408
  189.1 21.4 %collective-permute-start.15 = (bf16[512,256]{1,0:T(8,128)(2,1)}, bf16[512,256]{1,0:T(8,128)(2,1)S(1)}, u32[]{:S(2)}, u32[]{:S(2)}) collective-permute-start(bf16[512,256]{1,0:T(8,128)(2,1)} %get-tuple-element.63), channel_id=1, source_target_pairs={{0,4},{1,5},{2,6},{3,7},{4,0},{5,1},{6,2},{7,3},{8,12},{9,13},{10,... | collective-permute-start | bytes 786440 | tf_op jit(solution)/shard_map/ppermute | solution.py:408
  192.5 31.7 %collective-permute-start.16 = (bf16[512,256]{1,0:T(8,128)(2,1)}, bf16[512,256]{1,0:T(8,128)(2,1)S(1)}, u32[]{:S(2)}, u32[]{:S(2)}) collective-permute-start(bf16[512,256]{1,0:T(8,128)(2,1)} %get-tuple-element.64), channel_id=1, source_target_pairs={{0,5},{1,4},{2,7},{3,6},{4,1},{5,0},{6,3},{7,2},{8,13},{9,12},{10,... | collective-permute-start | bytes 786440 | tf_op jit(solution)/shard_map/ppermute | solution.py:408
  203.1 21.1 %collective-permute-start.17 = (bf16[512,256]{1,0:T(8,128)(2,1)}, bf16[512,256]{1,0:T(8,128)(2,1)S(1)}, u32[]{:S(2)}, u32[]{:S(2)}) collective-permute-start(bf16[512,256]{1,0:T(8,128)(2,1)} %get-tuple-element.65), channel_id=1, source_target_pairs={{0,6},{1,7},{2,0},{3,1},{4,2},{5,3},{6,4},{7,5},{8,14},{9,15},{10,... | collective-permute-start | bytes 786440 | tf_op jit(solution)/shard_map/ppermute | solution.py:408
  204.2 25.0 %collective-permute-start.18 = (bf16[512,256]{1,0:T(8,128)(2,1)}, bf16[512,256]{1,0:T(8,128)(2,1)S(1)}, u32[]{:S(2)}, u32[]{:S(2)}) collective-permute-start(bf16[512,256]{1,0:T(8,128)(2,1)} %get-tuple-element.66), channel_id=1, source_target_pairs={{0,7},{1,6},{2,1},{3,0},{4,3},{5,2},{6,5},{7,4},{8,15},{9,14},{10,... | collective-permute-start | bytes 786440 | tf_op jit(solution)/shard_map/ppermute | solution.py:408
  236.7 59.9 %all-to-all-start.3 = ((bf16[32,16,8,256]{3,2,1,0:T(8,128)(2,1)}), bf16[32,16,8,256]{3,2,1,0:T(8,128)(2,1)}, u32[]{:S(2)}, u32[]{:S(2)}) async-start(bf16[32,16,8,256]{3,2,1,0:T(8,128)(2,1)} %left_pass.3), calls=%async_computation.3 | async-start | bytes 4194304 | tf_op jit(solution)/shard_map/all_to_all | solution.py:396
  246.5 14.8 %collective-permute-start.19 = (bf16[2,512,256]{2,1,0:T(8,128)(2,1)}, bf16[2,512,256]{2,1,0:T(8,128)(2,1)S(1)}, u32[]{:S(2)}, u32[]{:S(2)}) collective-permute-start(bf16[2,512,256]{2,1,0:T(8,128)(2,1)} %get-tuple-element.70), channel_id=1, source_target_pairs={{0,2},{1,3},{2,4},{3,5},{4,6},{5,7},{6,0},{7,1},{8,10},{9,11},{10,... | collective-permute-start | bytes 1572872 | tf_op jit(solution)/shard_map/ppermute | solution.py:408
  246.6 26.7 %collective-permute-start.20 = (bf16[2,512,256]{2,1,0:T(8,128)(2,1)}, bf16[2,512,256]{2,1,0:T(8,128)(2,1)S(1)}, u32[]{:S(2)}, u32[]{:S(2)}) collective-permute-start(bf16[2,512,256]{2,1,0:T(8,128)(2,1)} %get-tuple-element.72), channel_id=1, source_target_pairs={{0,4},{1,5},{2,6},{3,7},{4,0},{5,1},{6,2},{7,3},{8,12},{9,13},{10,... | collective-permute-start | bytes 1572872 | tf_op jit(solution)/shard_map/ppermute | solution.py:408
  250.0 24.6 %collective-permute-start.21 = (bf16[2,512,256]{2,1,0:T(8,128)(2,1)S(1)}, bf16[2,512,256]{2,1,0:T(8,128)(2,1)S(1)}, u32[]{:S(2)}, u32[]{:S(2)}) collective-permute-start(bf16[2,512,256]{2,1,0:T(8,128)(2,1)S(1)} %copy-done.11), channel_id=1, source_target_pairs={{0,6},{1,7},{2,0},{3,1},{4,2},{5,3},{6,4},{7,5},{8,14},{9,15},{10,... | collective-permute-start | bytes 1572872 | tf_op jit(solution)/shard_map/ppermute | solution.py:408
  251.7 26.5 %collective-permute-start.22 = (bf16[512,256]{1,0:T(8,128)(2,1)}, bf16[512,256]{1,0:T(8,128)(2,1)}, u32[]{:S(2)}, u32[]{:S(2)}) collective-permute-start(bf16[512,256]{1,0:T(8,128)(2,1)} %get-tuple-element.76), channel_id=1, source_target_pairs={{0,1},{1,0},{2,3},{3,2},{4,5},{5,4},{6,7},{7,6},{8,9},{9,8},{10,11... | collective-permute-start | bytes 786440 | tf_op jit(solution)/shard_map/ppermute | solution.py:408
  262.5 15.7 %collective-permute-start.23 = (bf16[512,256]{1,0:T(8,128)(2,1)}, bf16[512,256]{1,0:T(8,128)(2,1)}, u32[]{:S(2)}, u32[]{:S(2)}) collective-permute-start(bf16[512,256]{1,0:T(8,128)(2,1)} %get-tuple-element.77), channel_id=1, source_target_pairs={{0,1},{1,0},{2,3},{3,2},{4,5},{5,4},{6,7},{7,6},{8,9},{9,8},{10,11... | collective-permute-start | bytes 786440 | tf_op jit(solution)/shard_map/ppermute | solution.py:408
  274.5 15.7 %collective-permute-start.24 = (bf16[512,256]{1,0:T(8,128)(2,1)}, bf16[512,256]{1,0:T(8,128)(2,1)}, u32[]{:S(2)}, u32[]{:S(2)}) collective-permute-start(bf16[512,256]{1,0:T(8,128)(2,1)} %get-tuple-element.78), channel_id=1, source_target_pairs={{0,1},{1,0},{2,3},{3,2},{4,5},{5,4},{6,7},{7,6},{8,9},{9,8},{10,11... | collective-permute-start | bytes 786440 | tf_op jit(solution)/shard_map/ppermute | solution.py:408
  275.8 20.0 %collective-permute-start.25 = (bf16[512,256]{1,0:T(8,128)(2,1)}, bf16[512,256]{1,0:T(8,128)(2,1)}, u32[]{:S(2)}, u32[]{:S(2)}) collective-permute-start(bf16[512,256]{1,0:T(8,128)(2,1)} %get-tuple-element.79), channel_id=1, source_target_pairs={{0,1},{1,0},{2,3},{3,2},{4,5},{5,4},{6,7},{7,6},{8,9},{9,8},{10,11... | collective-permute-start | bytes 786440 | tf_op jit(solution)/shard_map/ppermute | solution.py:408
  (11 other events, 247.1 us)

commit v3 on v2

v3 whole, which is shorter than its diff:
```python
import functools

import jax
import jax.numpy as jnp
from jax import lax
from jax.experimental import pallas as pl
from jax.experimental.pallas import tpu as pltpu
from jax.sharding import PartitionSpec as P


F32 = jnp.float32
BF16 = jnp.bfloat16
NY = 4


def _params(mib=32):
    return pltpu.CompilerParams(vmem_limit_bytes=min(mib << 20, 67043328))


def _hbm(shape):
    return pltpu.HBM(shape, BF16)


def _cost(flops, nbytes):
    return pl.CostEstimate(flops=flops, bytes_accessed=nbytes, transcendentals=0)


def _fwd(s, d):
    return lax.rem(s[0] // 2 + d, NY)


def _back(s, d):
    return lax.rem(s[0] // 2 + NY - d, NY)


def _column(row, length):
    return jnp.transpose(jnp.broadcast_to(row, (128, length)))


def right_kernel(x_ref, r_ref, tw_ref, out_ref, scr):
    outer, _, chan = x_ref.shape
    rows = r_ref.shape[0]
    for a in range(outer):
        acc = jnp.dot(r_ref[...], x_ref[a], preferred_element_type=F32)
        col = _column(tw_ref[a : a + 1, :], rows)
        for c in range(chan // 128):
            scr[c, pl.ds(a, rows, stride=outer), :] = acc[:, c * 128 : c * 128 + 128] * col
    for c in range(chan // 128):
        out_ref[:, :, :, c * 128 : c * 128 + 128] = scr[c].reshape(*out_ref.shape[:3], 128).astype(BF16)


def right_pass(x3, right, twiddle, seq):
    outer, inner, chan = x3.shape
    steps = 2
    rows = inner // steps
    per = inner // seq
    return pl.pallas_call(
        right_kernel,
        name="right_pass",
        grid=(steps,),
        in_specs=[
            pl.BlockSpec((outer, inner, chan), lambda g: (0, 0, 0)),
            pl.BlockSpec((rows, inner), lambda g: (g, 0)),
            pl.BlockSpec((outer, rows), lambda g: (0, g)),
        ],
        out_specs=pl.BlockSpec((seq // steps, per, outer, chan), lambda g: (g, 0, 0, 0)),
        out_shape=_hbm((seq, per, outer, chan)),
        scratch_shapes=[pltpu.VMEM((chan // 128, rows * outer, 128), F32)],
        compiler_params=_params(64),
        cost_estimate=_cost(2 * outer * inner * inner * chan, 6 << 20),
    )(x3, right, twiddle)


def left_kernel(l_ref, in_ref, out_ref):
    seq, per, outer, chan = in_ref.shape
    for j in range(per):
        block = in_ref[:, j].astype(F32).reshape(seq * outer, chan).astype(BF16)
        acc = jnp.dot(l_ref[...], block, preferred_element_type=F32)
        out_ref[:, j] = acc.reshape(seq, outer, chan).astype(BF16)


def left_pass(left, wire):
    seq, per, outer, chan = wire.shape
    steps = 4
    full = seq * outer
    block = (seq, per // steps, outer, chan)
    return pl.pallas_call(
        left_kernel,
        name="left_pass",
        grid=(steps,),
        in_specs=[
            pl.BlockSpec((full, full), lambda g: (0, 0)),
            pl.BlockSpec(block, lambda g: (0, g, 0, 0)),
        ],
        out_specs=pl.BlockSpec(block, lambda g: (0, g, 0, 0)),
        out_shape=_hbm(wire.shape),
        compiler_params=_params(),
        cost_estimate=_cost(2 * full * full * per * chan, 4 << 20),
    )(left, wire)


def middle_kernel(s, x_ref, xp_ref, b_ref, *outs):
    d = pl.program_id(0)
    outer, rows, chan = x_ref.shape
    half = lax.rem(s[0], 2)
    own = b_ref[:, pl.ds(pl.multiple_of(half * chan, 128), chan)]
    other = b_ref[:, pl.ds(pl.multiple_of((1 - half) * chan, 128), chan)]
    dims = (((1,), (1,)), ((), ()))
    acc = lax.dot_general(x_ref[...].reshape(outer * rows, chan), own, dims, preferred_element_type=F32)
    acc += lax.dot_general(xp_ref[...].reshape(outer * rows, chan), other, dims, preferred_element_type=F32)
    value = acc.astype(BF16).reshape(outer, rows, chan)
    for i in range(NY):

        @pl.when(d == i)
        def _():
            outs[i][...] = value


def middle_pass(s, x3, xp3, blocks):
    outer, inner, chan = x3.shape
    rows = inner // NY
    block = (outer, rows, chan)
    return pl.pallas_call(
        middle_kernel,
        name="middle_pass",
        grid_spec=pltpu.PrefetchScalarGridSpec(
            num_scalar_prefetch=1,
            grid=(NY,),
            in_specs=[
                pl.BlockSpec(block, lambda d, s: (0, _fwd(s, d), 0)),
                pl.BlockSpec(block, lambda d, s: (0, _fwd(s, d), 0)),
                pl.BlockSpec(blocks.shape, lambda d, s: (0, 0)),
            ],
            out_specs=[pl.BlockSpec(block, lambda d, s: (0, 0, 0))] * NY,
        ),
        out_shape=[_hbm(block)] * NY,
        compiler_params=_params(),
        cost_estimate=_cost(4 * outer * inner * chan * chan, 6 << 20),
    )(s, x3, xp3, blocks)


def mix_kernel(flip, s, mix_ref, *refs):
    ins, outs = refs[:NY], refs[NY:]
    y = s[0] // 2
    values = [r[...].astype(F32) for r in ins]
    for e in range(NY):
        to = lax.rem(y + e, NY)
        acc = None
        for d in range(NY):
            frm = lax.rem(y + NY - d, NY)
            row = mix_ref[frm, pl.ds(to, 1), :] if flip else mix_ref[to, pl.ds(frm, 1), :]
            term = values[d] * row
            acc = term if acc is None else acc + term
        outs[e][...] = acc.astype(BF16)


def mix_pass(s, mixer, parts, flip):
    outer, rows, chan = parts[0].shape
    total = outer * rows
    steps = 4
    block = pl.BlockSpec((total // steps, chan), lambda g, s: (g, 0))
    outs = pl.pallas_call(
        functools.partial(mix_kernel, flip),
        name="mix_back" if flip else "mix_pass",
        grid_spec=pltpu.PrefetchScalarGridSpec(
            num_scalar_prefetch=1,
            grid=(steps,),
            in_specs=[pl.BlockSpec((NY, NY, chan), lambda g, s: (0, 0, lax.rem(s[0], 2)))] + [block] * NY,
            out_specs=[block] * NY,
        ),
        out_shape=[_hbm((total, chan))] * NY,
        compiler_params=_params(),
        cost_estimate=_cost(2 * NY * NY * total * chan, 4 << 20),
    )(s, mixer, *[p.reshape(total, chan) for p in parts])
    return [o.reshape(outer, rows, chan) for o in outs]


def gate_kernel(s, og_ref, g0, g1, g2, g3, gate_ref, wire_ref, scr):
    d = pl.program_id(0)
    outer, rows, chan = og_ref.shape
    for i, g_ref in enumerate((g0, g1, g2, g3)):

        @pl.when(d == i)
        def _():
            for a in range(outer):
                g = g_ref[a]
                gate_ref[a] = g
                for c in range(chan // 128):
                    cols = slice(c * 128, c * 128 + 128)
                    scr[c, pl.ds(a, rows, stride=outer), :] = og_ref[a, :, cols].astype(F32) * g[:, cols].astype(F32)

    for c in range(chan // 128):
        wire_ref[:, :, :, c * 128 : c * 128 + 128] = scr[c].reshape(*wire_ref.shape[:3], 128).astype(BF16)


def gate_pass(s, og3, parts, seq):
    outer, inner, chan = og3.shape
    rows = inner // NY
    per = inner // seq
    block = (outer, rows, chan)
    nat = pl.BlockSpec(block, lambda d, s: (0, _back(s, d), 0))
    return pl.pallas_call(
        gate_kernel,
        name="gate_pass",
        grid_spec=pltpu.PrefetchScalarGridSpec(
            num_scalar_prefetch=1,
            grid=(NY,),
            in_specs=[nat] + [pl.BlockSpec(block, lambda d, s: (0, 0, 0))] * NY,
            out_specs=[nat, pl.BlockSpec((seq // NY, per, outer, chan), lambda d, s: (_back(s, d), 0, 0, 0))],
            scratch_shapes=[pltpu.VMEM((chan // 128, rows * outer, 128), F32)],
        ),
        out_shape=[
            _hbm(og3.shape),
            _hbm((seq, per, outer, chan)),
        ],
        compiler_params=_params(),
        cost_estimate=_cost(outer * inner * chan, 8 << 20),
    )(s, og3, *parts)


def out_kernel(s, wire_ref, gate_ref, og_ref, out_ref, o0, o1, o2, o3, scr):
    d = pl.program_id(0)
    outer, rows, chan = og_ref.shape
    for c in range(chan // 128):
        scr[c] = wire_ref[:, :, :, c * 128 : c * 128 + 128].astype(F32).reshape(scr.shape[1:])
    for i, gg_ref in enumerate((o0, o1, o2, o3)):

        @pl.when(d == i)
        def _():
            for a in range(outer):
                for c in range(chan // 128):
                    cols = slice(c * 128, c * 128 + 128)
                    m = scr[c, pl.ds(a, rows, stride=outer), :]
                    out_ref[a, :, cols] = (gate_ref[a, :, cols].astype(F32) * m).astype(BF16)
                    gg_ref[a, :, cols] = (og_ref[a, :, cols].astype(F32) * m).astype(BF16)


def out_pass(s, wire, gate3, og3):
    outer, inner, chan = og3.shape
    seq, per = wire.shape[:2]
    rows = inner // NY
    block = (outer, rows, chan)
    nat = pl.BlockSpec(block, lambda d, s: (0, _fwd(s, d), 0))
    res = pl.pallas_call(
        out_kernel,
        name="out_pass",
        grid_spec=pltpu.PrefetchScalarGridSpec(
            num_scalar_prefetch=1,
            grid=(NY,),
            in_specs=[pl.BlockSpec((seq // NY, per, outer, chan), lambda d, s: (_fwd(s, d), 0, 0, 0)), nat, nat],
            out_specs=[nat] + [pl.BlockSpec(block, lambda d, s: (0, 0, 0))] * NY,
            scratch_shapes=[pltpu.VMEM((chan // 128, rows * outer, 128), F32)],
        ),
        out_shape=[_hbm(og3.shape)] + [_hbm(block)] * NY,
        compiler_params=_params(),
        cost_estimate=_cost(2 * outer * inner * chan, 10 << 20),
    )(s, wire, gate3, og3)
    return res[0], res[1:]


def chan_kernel(s, b_ref, bo_ref, own_ref, other_ref, out_ref):
    chan = out_ref.shape[1]
    cols = pl.ds(pl.multiple_of(lax.rem(s[0], 2) * chan, 128), chan)
    acc = jnp.dot(own_ref[...], b_ref[:, cols], preferred_element_type=F32)
    acc += jnp.dot(other_ref[...], bo_ref[:, cols], preferred_element_type=F32)
    out_ref[...] = acc.astype(BF16)


def chan_pass(s, blocks, blocks_other, own, other):
    outer, rows, chan = own.shape
    total = outer * rows
    steps = 2
    whole = pl.BlockSpec(blocks.shape, lambda i, s: (0, 0))
    tile = pl.BlockSpec((total // steps, chan), lambda i, s: (i, 0))
    return pl.pallas_call(
        chan_kernel,
        name="chan_pass",
        grid_spec=pltpu.PrefetchScalarGridSpec(
            num_scalar_prefetch=1,
            grid=(steps,),
            in_specs=[whole, whole, tile, tile],
            out_specs=tile,
        ),
        out_shape=_hbm((total, chan)),
        compiler_params=_params(),
        cost_estimate=_cost(4 * total * chan * chan, 2 << 20),
    )(s, blocks, blocks_other, own.reshape(total, chan), other.reshape(total, chan))


def tail_kernel(s, wire_ref, rt_ref, tw_ref, *refs):
    parts, (out_ref, scr, total_ref) = refs[:NY], refs[NY:]
    outer, inner = tw_ref.shape
    chan = out_ref.shape[2]
    rows = inner // NY
    a = pl.program_id(0)

    @pl.when(a == 0)
    def _():
        for c in range(chan // 128):
            scr[c] = wire_ref[:, :, :, c * 128 : c * 128 + 128].astype(F32).reshape(scr.shape[1:])

    col = _column(tw_ref[pl.ds(a, 1), :], inner)
    grad = [(scr[c, pl.ds(a, inner, stride=outer), :] * col).astype(BF16) for c in range(chan // 128)]
    total_ref[...] = jnp.dot(rt_ref[...], jnp.concatenate(grad, axis=1), preferred_element_type=F32)
    for d in range(NY):
        at = pl.ds(pl.multiple_of(_back(s, d) * rows, rows), rows)
        out_ref[0, at, :] = (total_ref[at, :] + parts[d][...].astype(F32)).astype(BF16)


def tail_pass(s, wire, right_t, twiddle, parts):
    outer, inner = twiddle.shape
    chan = wire.shape[3]
    part = pl.BlockSpec((inner // NY, chan), lambda a, s: (a, 0))
    return pl.pallas_call(
        tail_kernel,
        name="tail_pass",
        grid_spec=pltpu.PrefetchScalarGridSpec(
            num_scalar_prefetch=1,
            grid=(outer,),
            in_specs=[
                pl.BlockSpec(wire.shape, lambda a, s: (0, 0, 0, 0)),
                pl.BlockSpec(right_t.shape, lambda a, s: (0, 0)),
                pl.BlockSpec(twiddle.shape, lambda a, s: (0, 0)),
            ]
            + [part] * NY,
            out_specs=pl.BlockSpec((1, inner, chan), lambda a, s: (a, 0, 0)),
            scratch_shapes=[pltpu.VMEM((chan // 128, outer * inner, 128), F32), pltpu.VMEM((inner, chan), F32)],
        ),
        out_shape=jax.ShapeDtypeStruct((outer, inner, chan), BF16),
        compiler_params=_params(64),
        cost_estimate=_cost(2 * outer * inner * inner * chan, 7 << 20),
    )(s, wire, right_t, twiddle, *parts)


def seq_swap(wire):
    return lax.all_to_all(wire, "seq", split_axis=0, concat_axis=0, tiled=True)


def body(inputs, twiddle, right_factor, left_factor, blocks, block_mixer, out_grad):
    outer, inner = twiddle.shape
    chan = inputs.shape[1]
    seq = left_factor.shape[0] // outer
    n = 2 * NY

    def to_pair(v):
        return lax.ppermute(v, "chan", [(c, c ^ 1) for c in range(n)])

    def around(parts):
        return [parts[0]] + [
            lax.ppermute(parts[d], "chan", [(c, (c + 2 * d) % n) for c in range(n)]) for d in range(1, NY)
        ]

    s = lax.axis_index("chan").reshape(1)
    x3 = inputs.reshape(outer, inner, chan)
    og3 = out_grad.reshape(outer, inner, chan)
    mixer = jnp.transpose(block_mixer, (1, 2, 0))

    xp3 = to_pair(inputs).reshape(x3.shape)
    twisted = seq_swap(right_pass(x3, right_factor, twiddle, seq))
    middle = middle_pass(s, x3, xp3, blocks)
    middle = around(middle)
    mixed_wire = left_pass(left_factor, twisted)

    mixed = seq_swap(mixed_wire)
    pieces = around(mix_pass(s, mixer, middle, False))
    gate3, grad_mixed = gate_pass(s, og3, pieces, seq)

    grad_mixed, mixed = lax.optimization_barrier((grad_mixed, mixed))
    grad_wire = seq_swap(grad_mixed)
    output, pieces = out_pass(s, mixed, gate3, og3)
    grad_middle = mix_pass(s, mixer, around(pieces), True)
    grad_wire = left_pass(left_factor.T, grad_wire)
    blocks_other = to_pair(blocks)

    grad_middle = around(grad_middle)
    grad_twisted = seq_swap(grad_wire)
    parts = [None] * NY
    for d in (0, 1, 3, 2):
        parts[d] = chan_pass(s, blocks, blocks_other, grad_middle[d], to_pair(grad_middle[d]))
    input_grad = tail_pass(s, grad_twisted, right_factor.T, twiddle, parts)
    return (output.reshape(inputs.shape), input_grad.reshape(inputs.shape))


def solution(mesh):
    return jax.shard_map(
        body,
        mesh=mesh,
        in_specs=(
            P("seq", "chan"),
            P("seq", None),
            P(),
            P(),
            P("chan", None),
            P(),
            P("seq", "chan"),
        ),
        out_specs=(P("seq", "chan"), P("seq", "chan")),
        check_vma=False,
    )
```

time: 307 us -> 407 us (1.33)
  blocking collectives: 0 us -> 63.2 us
  waiting for transfers between devices: 182 us -> 243 us
  starting transfers between devices: 74 us -> 43.3 us
    all_to_all x0 -> x1, blocking collectives: none -> 63.2 us  [seq_swap(): return lax.all_to_all(wire, 'seq', split_axis=0, concat_axis=0, tiled=True)]
    all_to_all x4 -> x3, waiting for transfers between devices: 0.73 us -> 50 us  [seq_swap(): return lax.all_to_all(wire, 'seq', split_axis=0, concat_axis=0, tiled=True)]
    all_to_all x4 -> x3, starting transfers between devices: 45.2 us -> 23.8 us  [seq_swap(): return lax.all_to_all(wire, 'seq', split_axis=0, concat_axis=0, tiled=True)]
    ppermute x26 -> x18, waiting for transfers between devices: 181 us -> 193 us  [the longest x6 101 us: to_pair(): return lax.ppermute(v, 'chan', [(c, c ^ 1) for c in range(n)])]
    ppermute x26 -> x18, starting transfers between devices: 28.8 us -> 19.5 us  [the longest x12 16.2 us: around(): lax.ppermute(parts[d], 'chan', [(c, (c + 2 * d) % n) for c in range(n)])]
  transfers between devices with their start and end apart: 30 -> 21, of which waited for: 17 -> 12; matrix products, arithmetic and copies ran while one was open for 1% -> 1% of each run, Pallas kernels for 7% -> 6%
where the time goes in v3:
time: 407 us; the launch traced here: 404 us
  waiting for transfers between devices  243 us (60%)
  blocking collectives  63.2 us (16%)
  Pallas kernels  46.3 us (11%)
  starting transfers between devices  43.3 us (11%)
  local copies, waits for them, and re-layouts  7.93 us (2%)
    ppermute x6, waiting for transfers between devices, to_pair(): return lax.ppermute(v, 'chan', [(c, c ^ 1) for c in range(n)])  101 us
    ppermute x12, waiting for transfers between devices, around(): lax.ppermute(parts[d], 'chan', [(c, (c + 2 * d) % n) for c in range(n)])  91.8 us
    all_to_all x1, blocking collectives, seq_swap(): return lax.all_to_all(wire, 'seq', split_axis=0, concat_axis=0, tiled=True)  63.2 us
    all_to_all x3, waiting for transfers between devices, seq_swap(): return lax.all_to_all(wire, 'seq', split_axis=0, concat_axis=0, tiled=True)  50 us
    all_to_all x3, starting transfers between devices, seq_swap(): return lax.all_to_all(wire, 'seq', split_axis=0, concat_axis=0, tiled=True)  23.8 us
    ppermute x12, starting transfers between devices, around(): lax.ppermute(parts[d], 'chan', [(c, (c + 2 * d) % n) for c in range(n)])  16.2 us
    pallas_call x1, Pallas kernels, tail_pass(): pl.pallas_call(tail_kernel, name='tail_pass', grid_spec=pltpu.PrefetchSca...  8.95 us
  transfers between devices with their start and end apart: 21, of which 12 were waited for; matrix products, arithmetic and copies ran while one was open for 1% of the time, Pallas kernels for 6%

profile of v3, /device:TPU:1, one launch (start us, length us, event | category | flops | bytes accessed | tf_op | source)
XLA Modules:
  0.0 404.3 jit_solution(17557764322704991126)
XLA Ops:
  0.6 4.6 %right_pass.1 = bf16[32,16,8,256]{3,2,1,0:T(8,128)(2,1)} custom-call(bf16[8,512,256]{2,1,0:T(8,128)(2,1)} %bitcast.34, bf16[512,512]{1,0:T(8,128)(2,1)} %r_ref.1, f32[8,512]{1,0:T(8,128)} %tw_ref.3), custom_call_target="tpu_custom_call" | custom-call | flops 1073741824 | bytes 6291456 | tf_op jit(solution)/shard_map/right_pass/pallas_call | solution.py:57
  5.2 63.2 %all_to_all.20.in_ref = bf16[32,16,8,256]{3,2,1,0:T(8,128)(2,1)S(1)} all-to-all(bf16[32,16,8,256]{3,2,1,0:T(8,128)(2,1)} %right_pass.1), channel_id=1, replica_groups=mesh['seq'=32,'chan'=8] {'seq'}, dimensions={0} | all-to-all | bytes 4194304 | tf_op jit(solution)/shard_map/all_to_all | solution.py:336
  68.4 2.6 left_pass.2
  71.1 6.0 %all-to-all-start.1 = ((bf16[32,16,8,256]{3,2,1,0:T(8,128)(2,1)}), bf16[32,16,8,256]{3,2,1,0:T(8,128)(2,1)}, u32[]{:S(2)}, u32[]{:S(2)}) async-start(bf16[32,16,8,256]{3,2,1,0:T(8,128)(2,1)} %left_pass.2), calls=%async_computation.1 | async-start | bytes 4194304 | tf_op jit(solution)/shard_map/all_to_all | solution.py:336
  77.5 68.2 %collective-permute-done = bf16[4096,256]{1,0:T(8,128)(2,1)} collective-permute-done((bf16[4096,256]{1,0:T(8,128)(2,1)S(1)}, bf16[4096,256]{1,0:T(8,128)(2,1)}, u32[]{:S(2)}, u32[]{:S(2)}) %collective-permute-start) | collective-permute-done | bytes 2097184 | tf_op jit(solution)/shard_map/ppermute | solution.py:346
  145.7 5.3 %middle_pass.1 = (bf16[8,128,256]{2,1,0:T(8,128)(2,1)}, bf16[8,128,256]{2,1,0:T(8,128)(2,1)}, bf16[8,128,256]{2,1,0:T(8,128)(2,1)}, bf16[8,128,256]{2,1,0:T(8,128)(2,1)}) custom-call(s32[1]{0:T(128)} %bitcast.s, bf16[8,512,256]{2,1,0:T(8,128)(2,1)S(1)} %bitcast.35, bf16[8,512,256]{2,1,0:T(8,128)(2,1)} %bitcast.4.xp_ref, bf16[256,512]{1,0:T(8,128)(2,1)S(1)} %copy-done.2), custom_call_target="tpu_custom_call" | custom-call | flops 1073741824 | bytes 6291456 | tf_op jit(solution)/shard_map/middle_pass/pallas_call | solution.py:123
  152.3 2.6 collective-permute-start.2
  156.0 9.1 %collective-permute-done.1 = bf16[8,128,256]{2,1,0:T(8,128)(2,1)S(1)} collective-permute-done((bf16[8,128,256]{2,1,0:T(8,128)(2,1)}, bf16[8,128,256]{2,1,0:T(8,128)(2,1)S(1)}, u32[]{:S(2)}, u32[]{:S(2)}) %collective-permute-start.1) | collective-permute-done | bytes 524320 | tf_op jit(solution)/shard_map/ppermute | solution.py:350
  165.1 12.4 %collective-permute-done.2 = bf16[8,128,256]{2,1,0:T(8,128)(2,1)S(1)} collective-permute-done((bf16[8,128,256]{2,1,0:T(8,128)(2,1)}, bf16[8,128,256]{2,1,0:T(8,128)(2,1)S(1)}, u32[]{:S(2)}, u32[]{:S(2)}) %collective-permute-start.2) | collective-permute-done | bytes 524320 | tf_op jit(solution)/shard_map/ppermute | solution.py:350
  178.6 2.3 mix_pass.1
  182.3 2.8 collective-permute-start.5
  185.2 9.7 %collective-permute-done.4.g1 = bf16[8,128,256]{2,1,0:T(8,128)(2,1)S(1)} collective-permute-done((bf16[8,128,256]{2,1,0:T(8,128)(2,1)}, bf16[8,128,256]{2,1,0:T(8,128)(2,1)S(1)}, u32[]{:S(2)}, u32[]{:S(2)}) %collective-permute-start.4) | collective-permute-done | bytes 524320 | tf_op jit(solution)/shard_map/ppermute | solution.py:350
  194.9 13.3 %collective-permute-done.5.g2 = bf16[8,128,256]{2,1,0:T(8,128)(2,1)S(1)} collective-permute-done((bf16[8,128,256]{2,1,0:T(8,128)(2,1)}, bf16[8,128,256]{2,1,0:T(8,128)(2,1)S(1)}, u32[]{:S(2)}, u32[]{:S(2)}) %collective-permute-start.5) | collective-permute-done | bytes 524320 | tf_op jit(solution)/shard_map/ppermute | solution.py:350
  209.2 3.4 gate_pass.1
  212.6 11.3 %all-to-all-start.2 = ((bf16[32,16,8,256]{3,2,1,0:T(8,128)(2,1)}), bf16[32,16,8,256]{3,2,1,0:T(8,128)(2,1)}, u32[]{:S(2)}, u32[]{:S(2)}) async-start(bf16[32,16,8,256]{3,2,1,0:T(8,128)(2,1)} %get-tuple-element.35), calls=%async_computation.2 | async-start | bytes 4194304 | tf_op jit(solution)/shard_map/all_to_all | solution.py:336
  224.0 50.0 %all-to-all-done.2.in_ref = bf16[32,16,8,256]{3,2,1,0:T(8,128)(2,1)} async-done(((bf16[32,16,8,256]{3,2,1,0:T(8,128)(2,1)}), bf16[32,16,8,256]{3,2,1,0:T(8,128)(2,1)}, u32[]{:S(2)}, u32[]{:S(2)}) %all-to-all-start.2) | async-done | bytes 2097184 | tf_op jit(solution)/shard_map/all_to_all | solution.py:336
  274.0 4.3 %left_pass.3 = bf16[32,16,8,256]{3,2,1,0:T(8,128)(2,1)} custom-call(bf16[256,256]{1,0:T(8,128)(2,1)S(1)} %bitcast.51, bf16[32,16,8,256]{3,2,1,0:T(8,128)(2,1)} %all-to-all-done.2.in_ref), custom_call_target="tpu_custom_call" | custom-call | flops 536870912 | bytes 4194304 | tf_op jit(solution)/shard_map/left_pass/pallas_call | solution.py:87
  278.3 6.4 %all-to-all-start.3 = ((bf16[32,16,8,256]{3,2,1,0:T(8,128)(2,1)}), bf16[32,16,8,256]{3,2,1,0:T(8,128)(2,1)}, u32[]{:S(2)}, u32[]{:S(2)}) async-start(bf16[32,16,8,256]{3,2,1,0:T(8,128)(2,1)} %left_pass.3), calls=%async_computation.3 | async-start | bytes 4194304 | tf_op jit(solution)/shard_map/all_to_all | solution.py:336
  284.8 1.6 copy-done.3
  286.4 5.3 %out_pass.1 = (bf16[8,512,256]{2,1,0:T(8,128)(2,1)}, bf16[8,128,256]{2,1,0:T(8,128)(2,1)}, bf16[8,128,256]{2,1,0:T(8,128)(2,1)}, bf16[8,128,256]{2,1,0:T(8,128)(2,1)}, bf16[8,128,256]{2,1,0:T(8,128)(2,1)}) custom-call(s32[1]{0:T(128)} %bitcast.s, bf16[32,16,8,256]{3,2,1,0:T(8,128)(2,1)} %all-to-all-done.1.wire_ref, bf16[8,512,256]{2,1,0:T(8,128)(2,1)S(1)} %copy-done.3, ...), custom_call_target="tpu_custom_call" | custom-call | flops 2097152 | bytes 10485760 | tf_op jit(solution)/shard_map/out_pass/pallas_call | solution.py:244
  292.0 2.7 collective-permute-start.9
  294.7 11.6 %collective-permute-done.8 = bf16[8,128,256]{2,1,0:T(8,128)(2,1)S(1)} collective-permute-done((bf16[8,128,256]{2,1,0:T(8,128)(2,1)}, bf16[8,128,256]{2,1,0:T(8,128)(2,1)S(1)}, u32[]{:S(2)}, u32[]{:S(2)}) %collective-permute-start.8) | collective-permute-done | bytes 524320 | tf_op jit(solution)/shard_map/ppermute | solution.py:350
  306.3 11.4 %collective-permute-done.9 = bf16[8,128,256]{2,1,0:T(8,128)(2,1)S(1)} collective-permute-done((bf16[8,128,256]{2,1,0:T(8,128)(2,1)}, bf16[8,128,256]{2,1,0:T(8,128)(2,1)S(1)}, u32[]{:S(2)}, u32[]{:S(2)}) %collective-permute-start.9) | collective-permute-done | bytes 524320 | tf_op jit(solution)/shard_map/ppermute | solution.py:350
  319.0 2.4 mix_back.1
  321.3 3.3 collective-permute-start.16
  325.2 21.7 %collective-permute-done.16 = bf16[8,128,256]{2,1,0:T(8,128)(2,1)S(1)} collective-permute-done((bf16[8,128,256]{2,1,0:T(8,128)(2,1)}, bf16[8,128,256]{2,1,0:T(8,128)(2,1)S(1)}, u32[]{:S(2)}, u32[]{:S(2)}) %collective-permute-start.16) | collective-permute-done | bytes 524320 | tf_op jit(solution)/shard_map/ppermute | solution.py:350
  348.4 2.4 collective-permute-done.12
  352.3 2.1 copy.10
  354.4 32.7 %collective-permute-done.7.bo_ref = bf16[256,512]{1,0:T(8,128)(2,1)S(1)} collective-permute-done((bf16[256,512]{1,0:T(8,128)(2,1)S(1)}, bf16[256,512]{1,0:T(8,128)(2,1)S(1)}, u32[]{:S(2)}, u32[]{:S(2)}) %collective-permute-start.7) | collective-permute-done | bytes 262176 | tf_op jit(solution)/shard_map/ppermute | solution.py:346
  390.8 2.3 chan_pass.6.refs_2_
  393.1 2.3 chan_pass.5.refs_1_
  395.4 9.0 %tail_pass.1 = bf16[8,512,256]{2,1,0:T(8,128)(2,1)} custom-call(s32[1]{0:T(128)} %bitcast.s, bf16[32,16,8,256]{3,2,1,0:T(8,128)(2,1)} %all-to-all-done.3.wire_ref, bf16[512,512]{1,0:T(8,128)(2,1)} %bitcast.55, f32[8,512]{1,0:T(8,128)} %tw_ref.3, bf16[1024,256]{1,0:T(8,128)(2,1)} %chan_pass.4.refs_0_, bf16[1024,256]{1,0:T(8,128)(2,1)} %chan_pass.5.refs_1_, ...), custom_call_target="tpu_custom_call" | custom-call | flops 1073741824 | bytes 7340032 | tf_op jit(solution)/shard_map/tail_pass/pallas_call | solution.py:314
  (46 shorter events, 15.2 us)
Async XLA Ops:
  5.2 63.2 %copy-start.8 = (bf16[256,256]{1,0:T(8,128)(2,1)S(1)}, bf16[256,256]{1,0:T(8,128)(2,1)}, u32[]{:S(2)}) copy-start(bf16[256,256]{1,0:T(8,128)(2,1)} %l_ref.1) | copy-start | bytes 393220
  71.1 6.0 %copy-start.1 = (bf16[4096,256]{1,0:T(8,128)(2,1)S(1)}, bf16[4096,256]{1,0:T(8,128)(2,1)}, u32[]{:S(2)}) copy-start(bf16[4096,256]{1,0:T(8,128)(2,1)} %param.7) | copy-start | bytes 6291460
  71.1 74.7 %copy-start.2 = (bf16[256,512]{1,0:T(8,128)(2,1)S(1)}, bf16[256,512]{1,0:T(8,128)(2,1)}, u32[]{:S(2)}) copy-start(bf16[256,512]{1,0:T(8,128)(2,1)} %b_ref.9) | copy-start | bytes 786436
  71.1 141.5 %all-to-all-start.1 = ((bf16[32,16,8,256]{3,2,1,0:T(8,128)(2,1)}), bf16[32,16,8,256]{3,2,1,0:T(8,128)(2,1)}, u32[]{:S(2)}, u32[]{:S(2)}) async-start(bf16[32,16,8,256]{3,2,1,0:T(8,128)(2,1)} %left_pass.2), calls=%async_computation.1 | async-start | bytes 4194304 | tf_op jit(solution)/shard_map/all_to_all | solution.py:336
  77.1 68.6 %collective-permute-start = (bf16[4096,256]{1,0:T(8,128)(2,1)S(1)}, bf16[4096,256]{1,0:T(8,128)(2,1)}, u32[]{:S(2)}, u32[]{:S(2)}) collective-permute-start(bf16[4096,256]{1,0:T(8,128)(2,1)S(1)} %copy-done.1), channel_id=1, source_target_pairs={{0,1},{1,0},{2,3},{3,2},{4,5},{5,4},{6,7},{7,6},{8,9},{9,8},{10,11... | collective-permute-start | bytes 6291464 | tf_op jit(solution)/shard_map/ppermute | solution.py:346
  145.7 31.8 %copy-start.9 = (f32[512,4,4]{0,2,1:T(4,128)S(1)}, f32[512,4,4]{0,2,1:T(4,128)}, u32[]{:S(2)}) copy-start(f32[512,4,4]{0,2,1:T(4,128)} %param.12) | copy-start | bytes 98308
  151.0 57.1 %copy-start = (bf16[4096,256]{1,0:T(8,128)(2,1)S(1)}, bf16[4096,256]{1,0:T(8,128)(2,1)}, u32[]{:S(2)}) copy-start(bf16[4096,256]{1,0:T(8,128)(2,1)} %param.13) | copy-start | bytes 6291460
  151.0 14.1 %collective-permute-start.1 = (bf16[8,128,256]{2,1,0:T(8,128)(2,1)}, bf16[8,128,256]{2,1,0:T(8,128)(2,1)S(1)}, u32[]{:S(2)}, u32[]{:S(2)}) collective-permute-start(bf16[8,128,256]{2,1,0:T(8,128)(2,1)} %get-tuple-element.24), channel_id=1, source_target_pairs={{0,2},{1,3},{2,4},{3,5},{4,6},{5,7},{6,0},{7,1},{8,10},{9,11},{10,... | collective-permute-start | bytes 1572872 | tf_op jit(solution)/shard_map/ppermute | solution.py:350
  152.3 25.2 %collective-permute-start.2 = (bf16[8,128,256]{2,1,0:T(8,128)(2,1)}, bf16[8,128,256]{2,1,0:T(8,128)(2,1)S(1)}, u32[]{:S(2)}, u32[]{:S(2)}) collective-permute-start(bf16[8,128,256]{2,1,0:T(8,128)(2,1)} %get-tuple-element.25), channel_id=1, source_target_pairs={{0,4},{1,5},{2,6},{3,7},{4,0},{5,1},{6,2},{7,3},{8,12},{9,13},{10,... | collective-permute-start | bytes 1572872 | tf_op jit(solution)/shard_map/ppermute | solution.py:350
  154.9 22.6 %collective-permute-start.3 = (bf16[8,128,256]{2,1,0:T(8,128)(2,1)}, bf16[8,128,256]{2,1,0:T(8,128)(2,1)S(1)}, u32[]{:S(2)}, u32[]{:S(2)}) collective-permute-start(bf16[8,128,256]{2,1,0:T(8,128)(2,1)} %get-tuple-element.26), channel_id=1, source_target_pairs={{0,6},{1,7},{2,0},{3,1},{4,2},{5,3},{6,4},{7,5},{8,14},{9,15},{10,... | collective-permute-start | bytes 1572872 | tf_op jit(solution)/shard_map/ppermute | solution.py:350
  177.5 1.0 copy-start.7
  180.9 14.0 %collective-permute-start.4 = (bf16[8,128,256]{2,1,0:T(8,128)(2,1)}, bf16[8,128,256]{2,1,0:T(8,128)(2,1)S(1)}, u32[]{:S(2)}, u32[]{:S(2)}) collective-permute-start(bf16[8,128,256]{2,1,0:T(8,128)(2,1)} %bitcast.62), channel_id=1, source_target_pairs={{0,2},{1,3},{2,4},{3,5},{4,6},{5,7},{6,0},{7,1},{8,10},{9,11},{10,... | collective-permute-start | bytes 1572872 | tf_op jit(solution)/shard_map/ppermute | solution.py:350
  182.3 25.8 %collective-permute-start.5 = (bf16[8,128,256]{2,1,0:T(8,128)(2,1)}, bf16[8,128,256]{2,1,0:T(8,128)(2,1)S(1)}, u32[]{:S(2)}, u32[]{:S(2)}) collective-permute-start(bf16[8,128,256]{2,1,0:T(8,128)(2,1)} %bitcast.61), channel_id=1, source_target_pairs={{0,4},{1,5},{2,6},{3,7},{4,0},{5,1},{6,2},{7,3},{8,12},{9,13},{10,... | collective-permute-start | bytes 1572872 | tf_op jit(solution)/shard_map/ppermute | solution.py:350
  185.2 23.0 %collective-permute-start.6 = (bf16[8,128,256]{2,1,0:T(8,128)(2,1)}, bf16[8,128,256]{2,1,0:T(8,128)(2,1)S(1)}, u32[]{:S(2)}, u32[]{:S(2)}) collective-permute-start(bf16[8,128,256]{2,1,0:T(8,128)(2,1)} %bitcast.59), channel_id=1, source_target_pairs={{0,6},{1,7},{2,0},{3,1},{4,2},{5,3},{6,4},{7,5},{8,14},{9,15},{10,... | collective-permute-start | bytes 1572872 | tf_op jit(solution)/shard_map/ppermute | solution.py:350
  208.1 1.0 copy-start.6
  212.6 61.4 %all-to-all-start.2 = ((bf16[32,16,8,256]{3,2,1,0:T(8,128)(2,1)}), bf16[32,16,8,256]{3,2,1,0:T(8,128)(2,1)}, u32[]{:S(2)}, u32[]{:S(2)}) async-start(bf16[32,16,8,256]{3,2,1,0:T(8,128)(2,1)} %get-tuple-element.35), calls=%async_computation.2 | async-start | bytes 4194304 | tf_op jit(solution)/shard_map/all_to_all | solution.py:336
  278.3 117.0 %all-to-all-start.3 = ((bf16[32,16,8,256]{3,2,1,0:T(8,128)(2,1)}), bf16[32,16,8,256]{3,2,1,0:T(8,128)(2,1)}, u32[]{:S(2)}, u32[]{:S(2)}) async-start(bf16[32,16,8,256]{3,2,1,0:T(8,128)(2,1)} %left_pass.3), calls=%async_computation.3 | async-start | bytes 4194304 | tf_op jit(solution)/shard_map/all_to_all | solution.py:336
  284.8 1.6 copy-start.3
  291.6 14.7 %collective-permute-start.8 = (bf16[8,128,256]{2,1,0:T(8,128)(2,1)}, bf16[8,128,256]{2,1,0:T(8,128)(2,1)S(1)}, u32[]{:S(2)}, u32[]{:S(2)}) collective-permute-start(bf16[8,128,256]{2,1,0:T(8,128)(2,1)} %get-tuple-element.37), channel_id=1, source_target_pairs={{0,2},{1,3},{2,4},{3,5},{4,6},{5,7},{6,0},{7,1},{8,10},{9,11},{10,... | collective-permute-start | bytes 1572872 | tf_op jit(solution)/shard_map/ppermute | solution.py:350
  292.0 25.8 %collective-permute-start.9 = (bf16[8,128,256]{2,1,0:T(8,128)(2,1)}, bf16[8,128,256]{2,1,0:T(8,128)(2,1)S(1)}, u32[]{:S(2)}, u32[]{:S(2)}) collective-permute-start(bf16[8,128,256]{2,1,0:T(8,128)(2,1)} %get-tuple-element.38), channel_id=1, source_target_pairs={{0,4},{1,5},{2,6},{3,7},{4,0},{5,1},{6,2},{7,3},{8,12},{9,13},{10,... | collective-permute-start | bytes 1572872 | tf_op jit(solution)/shard_map/ppermute | solution.py:350
  294.6 23.3 %collective-permute-start.10 = (bf16[8,128,256]{2,1,0:T(8,128)(2,1)}, bf16[8,128,256]{2,1,0:T(8,128)(2,1)S(1)}, u32[]{:S(2)}, u32[]{:S(2)}) collective-permute-start(bf16[8,128,256]{2,1,0:T(8,128)(2,1)} %get-tuple-element.39), channel_id=1, source_target_pairs={{0,6},{1,7},{2,0},{3,1},{4,2},{5,3},{6,4},{7,5},{8,14},{9,15},{10,... | collective-permute-start | bytes 1572872 | tf_op jit(solution)/shard_map/ppermute | solution.py:350
  317.9 1.0 copy-start.5
  321.3 25.6 %collective-permute-start.16 = (bf16[8,128,256]{2,1,0:T(8,128)(2,1)}, bf16[8,128,256]{2,1,0:T(8,128)(2,1)S(1)}, u32[]{:S(2)}, u32[]{:S(2)}) collective-permute-start(bf16[8,128,256]{2,1,0:T(8,128)(2,1)} %bitcast.60), channel_id=1, source_target_pairs={{0,6},{1,7},{2,0},{3,1},{4,2},{5,3},{6,4},{7,5},{8,14},{9,15},{10,... | collective-permute-start | bytes 1572872 | tf_op jit(solution)/shard_map/ppermute | solution.py:350
  324.6 22.3 %collective-permute-start.14 = (bf16[8,128,256]{2,1,0:T(8,128)(2,1)}, bf16[8,128,256]{2,1,0:T(8,128)(2,1)S(1)}, u32[]{:S(2)}, u32[]{:S(2)}) collective-permute-start(bf16[8,128,256]{2,1,0:T(8,128)(2,1)} %bitcast.58), channel_id=1, source_target_pairs={{0,4},{1,5},{2,6},{3,7},{4,0},{5,1},{6,2},{7,3},{8,12},{9,13},{10,... | collective-permute-start | bytes 1572872 | tf_op jit(solution)/shard_map/ppermute | solution.py:350
  324.6 26.2 %collective-permute-start.12 = (bf16[8,128,256]{2,1,0:T(8,128)(2,1)}, bf16[8,128,256]{2,1,0:T(8,128)(2,1)S(1)}, u32[]{:S(2)}, u32[]{:S(2)}) collective-permute-start(bf16[8,128,256]{2,1,0:T(8,128)(2,1)} %bitcast.57), channel_id=1, source_target_pairs={{0,2},{1,3},{2,4},{3,5},{4,6},{5,7},{6,0},{7,1},{8,10},{9,11},{10,... | collective-permute-start | bytes 1572872 | tf_op jit(solution)/shard_map/ppermute | solution.py:350
  325.2 61.9 %collective-permute-start.11 = (bf16[8,128,256]{2,1,0:T(8,128)(2,1)}, bf16[8,128,256]{2,1,0:T(8,128)(2,1)S(1)}, u32[]{:S(2)}, u32[]{:S(2)}) collective-permute-start(bf16[8,128,256]{2,1,0:T(8,128)(2,1)} %bitcast.37), channel_id=1, source_target_pairs={{0,1},{1,0},{2,3},{3,2},{4,5},{5,4},{6,7},{7,6},{8,9},{9,8},{10,11... | collective-permute-start | bytes 1572872 | tf_op jit(solution)/shard_map/ppermute | solution.py:346
  346.9 42.5 %collective-permute-start.17 = (bf16[8,128,256]{2,1,0:T(8,128)(2,1)S(1)}, bf16[8,128,256]{2,1,0:T(8,128)(2,1)S(1)}, u32[]{:S(2)}, u32[]{:S(2)}) collective-permute-start(bf16[8,128,256]{2,1,0:T(8,128)(2,1)S(1)} %collective-permute-done.16), channel_id=1, source_target_pairs={{0,1},{1,0},{2,3},{3,2},{4,5},{5,4},{6,7},{7,6},{8,9},{9,8},{10,11... | collective-permute-start | bytes 1572872 | tf_op jit(solution)/shard_map/ppermute | solution.py:346
  346.9 43.9 %collective-permute-start.15 = (bf16[8,128,256]{2,1,0:T(8,128)(2,1)S(1)}, bf16[8,128,256]{2,1,0:T(8,128)(2,1)}, u32[]{:S(2)}, u32[]{:S(2)}) collective-permute-start(bf16[8,128,256]{2,1,0:T(8,128)(2,1)S(1)} %collective-permute-done.14), channel_id=1, source_target_pairs={{0,1},{1,0},{2,3},{3,2},{4,5},{5,4},{6,7},{7,6},{8,9},{9,8},{10,11... | collective-permute-start | bytes 1572872 | tf_op jit(solution)/shard_map/ppermute | solution.py:346
  350.9 42.2 %collective-permute-start.13 = (bf16[8,128,256]{2,1,0:T(8,128)(2,1)S(1)}, bf16[8,128,256]{2,1,0:T(8,128)(2,1)}, u32[]{:S(2)}, u32[]{:S(2)}) collective-permute-start(bf16[8,128,256]{2,1,0:T(8,128)(2,1)S(1)} %collective-permute-done.12), channel_id=1, source_target_pairs={{0,1},{1,0},{2,3},{3,2},{4,5},{5,4},{6,7},{7,6},{8,9},{9,8},{10,11... | collective-permute-start | bytes 1572872 | tf_op jit(solution)/shard_map/ppermute | solution.py:346
  350.9 36.3 %collective-permute-start.7 = (bf16[256,512]{1,0:T(8,128)(2,1)S(1)}, bf16[256,512]{1,0:T(8,128)(2,1)S(1)}, u32[]{:S(2)}, u32[]{:S(2)}) collective-permute-start(bf16[256,512]{1,0:T(8,128)(2,1)S(1)} %copy-done.2), channel_id=1, source_target_pairs={{0,1},{1,0},{2,3},{3,2},{4,5},{5,4},{6,7},{7,6},{8,9},{9,8},{10,11... | collective-permute-start | bytes 786440 | tf_op jit(solution)/shard_map/ppermute | solution.py:346
  387.1 1.0 copy-start.4

commit v4 on v3

--- a/solution.py
+++ b/solution.py
@@ -11,6 +11,7 @@
 F32 = jnp.float32
 BF16 = jnp.bfloat16
 NY = 4
+CHUNKS = 2
 
 
 def _params(mib=32):
@@ -81,7 +82,7 @@
 
 def left_pass(left, wire):
     seq, per, outer, chan = wire.shape
-    steps = 4
+    steps = 8
     full = seq * outer
     block = (seq, per // steps, outer, chan)
     return pl.pallas_call(
@@ -108,7 +109,7 @@
     dims = (((1,), (1,)), ((), ()))
     acc = lax.dot_general(x_ref[...].reshape(outer * rows, chan), own, dims, preferred_element_type=F32)
     acc += lax.dot_general(xp_ref[...].reshape(outer * rows, chan), other, dims, preferred_element_type=F32)
-    value = acc.astype(BF16).reshape(outer, rows, chan)
+    value = acc.astype(BF16)
     for i in range(NY):
 
         @pl.when(d == i)
@@ -116,10 +117,11 @@
             outs[i][...] = value
 
 
-def middle_pass(s, x3, xp3, blocks):
-    outer, inner, chan = x3.shape
+def middle_pass(s, x3, xp3, blocks, u):
+    part, inner, chan = xp3.shape
     rows = inner // NY
-    block = (outer, rows, chan)
+    block = (part, rows, chan)
+    out = (part * rows, chan)
     return pl.pallas_call(
         middle_kernel,
         name="middle_pass",
@@ -127,15 +129,15 @@
             num_scalar_prefetch=1,
             grid=(NY,),
             in_specs=[
-                pl.BlockSpec(block, lambda d, s: (0, _fwd(s, d), 0)),
+                pl.BlockSpec(block, lambda d, s: (u, _fwd(s, d), 0)),
                 pl.BlockSpec(block, lambda d, s: (0, _fwd(s, d), 0)),
                 pl.BlockSpec(blocks.shape, lambda d, s: (0, 0)),
             ],
-            out_specs=[pl.BlockSpec(block, lambda d, s: (0, 0, 0))] * NY,
-        ),
-        out_shape=[_hbm(block)] * NY,
-        compiler_params=_params(),
-        cost_estimate=_cost(4 * outer * inner * chan * chan, 6 << 20),
+            out_specs=[pl.BlockSpec(out, lambda d, s: (0, 0))] * NY,
+        ),
+        out_shape=[_hbm(out)] * NY,
+        compiler_params=_params(),
+        cost_estimate=_cost(4 * part * inner * chan * chan, 3 << 20),
     )(s, x3, xp3, blocks)
 
 
@@ -155,11 +157,10 @@
 
 
 def mix_pass(s, mixer, parts, flip):
-    outer, rows, chan = parts[0].shape
-    total = outer * rows
-    steps = 4
+    total, chan = parts[0].shape
+    steps = 2
     block = pl.BlockSpec((total // steps, chan), lambda g, s: (g, 0))
-    outs = pl.pallas_call(
+    return pl.pallas_call(
         functools.partial(mix_kernel, flip),
         name="mix_back" if flip else "mix_pass",
         grid_spec=pltpu.PrefetchScalarGridSpec(
@@ -170,20 +171,22 @@
         ),
         out_shape=[_hbm((total, chan))] * NY,
         compiler_params=_params(),
-        cost_estimate=_cost(2 * NY * NY * total * chan, 4 << 20),
-    )(s, mixer, *[p.reshape(total, chan) for p in parts])
-    return [o.reshape(outer, rows, chan) for o in outs]
-
-
-def gate_kernel(s, og_ref, g0, g1, g2, g3, gate_ref, wire_ref, scr):
+        cost_estimate=_cost(2 * NY * NY * total * chan, 2 << 20),
+    )(s, mixer, *parts)
+
+
+def gate_kernel(s, og_ref, *refs):
+    pieces, (gate_ref, wire_ref, scr) = refs[: CHUNKS * NY], refs[CHUNKS * NY :]
     d = pl.program_id(0)
     outer, rows, chan = og_ref.shape
-    for i, g_ref in enumerate((g0, g1, g2, g3)):
+    part = outer // CHUNKS
+    for i in range(NY):
 
         @pl.when(d == i)
         def _():
             for a in range(outer):
-                g = g_ref[a]
+                at = (a % part) * rows
+                g = pieces[a // part * NY + i][at : at + rows, :]
                 gate_ref[a] = g
                 for c in range(chan // 128):
                     cols = slice(c * 128, c * 128 + 128)
@@ -193,7 +196,7 @@
         wire_ref[:, :, :, c * 128 : c * 128 + 128] = scr[c].reshape(*wire_ref.shape[:3], 128).astype(BF16)
 
 
-def gate_pass(s, og3, parts, seq):
+def gate_pass(s, og3, pieces, seq):
     outer, inner, chan = og3.shape
     rows = inner // NY
     per = inner // seq
@@ -205,7 +208,7 @@
         grid_spec=pltpu.PrefetchScalarGridSpec(
             num_scalar_prefetch=1,
             grid=(NY,),
-            in_specs=[nat] + [pl.BlockSpec(block, lambda d, s: (0, 0, 0))] * NY,
+            in_specs=[nat] + [pl.BlockSpec(pieces[0].shape, lambda d, s: (0, 0))] * (CHUNKS * NY),
             out_specs=[nat, pl.BlockSpec((seq // NY, per, outer, chan), lambda d, s: (_back(s, d), 0, 0, 0))],
             scratch_shapes=[pltpu.VMEM((chan // 128, rows * outer, 128), F32)],
         ),
@@ -215,15 +218,16 @@
         ],
         compiler_params=_params(),
         cost_estimate=_cost(outer * inner * chan, 8 << 20),
-    )(s, og3, *parts)
-
-
-def out_kernel(s, wire_ref, gate_ref, og_ref, out_ref, o0, o1, o2, o3, scr):
+    )(s, og3, *pieces)
+
+
+def cot_kernel(s, wire_ref, og_ref, *refs):
+    pieces, scr = refs[:NY], refs[NY]
     d = pl.program_id(0)
     outer, rows, chan = og_ref.shape
     for c in range(chan // 128):
         scr[c] = wire_ref[:, :, :, c * 128 : c * 128 + 128].astype(F32).reshape(scr.shape[1:])
-    for i, gg_ref in enumerate((o0, o1, o2, o3)):
+    for i in range(NY):
 
         @pl.when(d == i)
         def _():
@@ -231,67 +235,101 @@
                 for c in range(chan // 128):
                     cols = slice(c * 128, c * 128 + 128)
                     m = scr[c, pl.ds(a, rows, stride=outer), :]
-                    out_ref[a, :, cols] = (gate_ref[a, :, cols].astype(F32) * m).astype(BF16)
-                    gg_ref[a, :, cols] = (og_ref[a, :, cols].astype(F32) * m).astype(BF16)
-
-
-def out_pass(s, wire, gate3, og3):
+                    pieces[i][a * rows : a * rows + rows, cols] = (og_ref[a, :, cols].astype(F32) * m).astype(BF16)
+
+
+def cot_pass(s, wire, og3, u):
     outer, inner, chan = og3.shape
     seq, per = wire.shape[:2]
-    rows = inner // NY
-    block = (outer, rows, chan)
-    nat = pl.BlockSpec(block, lambda d, s: (0, _fwd(s, d), 0))
-    res = pl.pallas_call(
-        out_kernel,
-        name="out_pass",
+    parts = NY * CHUNKS
+    rows = inner // parts
+    piece = (outer * rows, chan)
+    return pl.pallas_call(
+        cot_kernel,
+        name="cot_pass",
         grid_spec=pltpu.PrefetchScalarGridSpec(
             num_scalar_prefetch=1,
             grid=(NY,),
-            in_specs=[pl.BlockSpec((seq // NY, per, outer, chan), lambda d, s: (_fwd(s, d), 0, 0, 0)), nat, nat],
-            out_specs=[nat] + [pl.BlockSpec(block, lambda d, s: (0, 0, 0))] * NY,
+            in_specs=[
+                pl.BlockSpec((seq // parts, per, outer, chan), lambda d, s: (_fwd(s, d) * CHUNKS + u, 0, 0, 0)),
+                pl.BlockSpec((outer, rows, chan), lambda d, s: (0, _fwd(s, d) * CHUNKS + u, 0)),
+            ],
+            out_specs=[pl.BlockSpec(piece, lambda d, s: (0, 0))] * NY,
             scratch_shapes=[pltpu.VMEM((chan // 128, rows * outer, 128), F32)],
         ),
-        out_shape=[_hbm(og3.shape)] + [_hbm(block)] * NY,
-        compiler_params=_params(),
-        cost_estimate=_cost(2 * outer * inner * chan, 10 << 20),
-    )(s, wire, gate3, og3)
-    return res[0], res[1:]
-
-
-def chan_kernel(s, b_ref, bo_ref, own_ref, other_ref, out_ref):
-    chan = out_ref.shape[1]
+        out_shape=[_hbm(piece)] * NY,
+        compiler_params=_params(),
+        cost_estimate=_cost(outer * inner * chan // CHUNKS, 3 << 20),
+    )(s, wire, og3)
+
+
+def out_kernel(wire_ref, gate_ref, out_ref, scr):
+    outer, rows, chan = out_ref.shape
+    for c in range(chan // 128):
+        scr[c] = wire_ref[:, :, :, c * 128 : c * 128 + 128].astype(F32).reshape(scr.shape[1:])
+    for a in range(outer):
+        for c in range(chan // 128):
+            cols = slice(c * 128, c * 128 + 128)
+            m = scr[c, pl.ds(a, rows, stride=outer), :]
+            out_ref[a, :, cols] = (gate_ref[a, :, cols].astype(F32) * m).astype(BF16)
+
+
+def out_pass(wire, gate3):
+    outer, inner, chan = gate3.shape
+    seq, per = wire.shape[:2]
+    rows = inner // NY
+    nat = pl.BlockSpec((outer, rows, chan), lambda d: (0, d, 0))
+    return pl.pallas_call(
+        out_kernel,
+        name="out_pass",
+        grid=(NY,),
+        in_specs=[pl.BlockSpec((seq // NY, per, outer, chan), lambda d: (d, 0, 0, 0)), nat],
+        out_specs=nat,
+        out_shape=_hbm(gate3.shape),
+        scratch_shapes=[pltpu.VMEM((chan // 128, rows * outer, 128), F32)],
+        compiler_params=_params(),
+        cost_estimate=_cost(outer * inner * chan, 6 << 20),
+    )(wire, gate3)
+
+
+def chan_kernel(s, b_ref, bo_ref, *refs):
+    own, other, out_ref = refs[:NY], refs[NY : 2 * NY], refs[2 * NY]
+    d = pl.program_id(0)
+    chan = out_ref.shape[2]
     cols = pl.ds(pl.multiple_of(lax.rem(s[0], 2) * chan, 128), chan)
-    acc = jnp.dot(own_ref[...], b_ref[:, cols], preferred_element_type=F32)
-    acc += jnp.dot(other_ref[...], bo_ref[:, cols], preferred_element_type=F32)
-    out_ref[...] = acc.astype(BF16)
+    for i in range(NY):
+
+        @pl.when(d == i)
+        def _():
+            acc = jnp.dot(own[i][...], b_ref[:, cols], preferred_element_type=F32)
+            acc += jnp.dot(other[i][...], bo_ref[:, cols], preferred_element_type=F32)
+            out_ref[0] = acc.astype(BF16)
 
 
 def chan_pass(s, blocks, blocks_other, own, other):
-    outer, rows, chan = own.shape
-    total = outer * rows
-    steps = 2
-    whole = pl.BlockSpec(blocks.shape, lambda i, s: (0, 0))
-    tile = pl.BlockSpec((total // steps, chan), lambda i, s: (i, 0))
+    total, chan = own[0].shape
+    whole = pl.BlockSpec(blocks.shape, lambda d, s: (0, 0))
+    tile = pl.BlockSpec((total, chan), lambda d, s: (0, 0))
     return pl.pallas_call(
         chan_kernel,
         name="chan_pass",
         grid_spec=pltpu.PrefetchScalarGridSpec(
             num_scalar_prefetch=1,
-            grid=(steps,),
-            in_specs=[whole, whole, tile, tile],
-            out_specs=tile,
-        ),
-        out_shape=_hbm((total, chan)),
-        compiler_params=_params(),
-        cost_estimate=_cost(4 * total * chan * chan, 2 << 20),
-    )(s, blocks, blocks_other, own.reshape(total, chan), other.reshape(total, chan))
-
-
-def tail_kernel(s, wire_ref, rt_ref, tw_ref, *refs):
-    parts, (out_ref, scr, total_ref) = refs[:NY], refs[NY:]
+            grid=(NY,),
+            in_specs=[whole, whole] + [tile] * (2 * NY),
+            out_specs=pl.BlockSpec((1, total, chan), lambda d, s: (_back(s, d), 0, 0)),
+        ),
+        out_shape=_hbm((NY, total, chan)),
+        compiler_params=_params(),
+        cost_estimate=_cost(4 * NY * total * chan * chan, 3 << 20),
+    )(s, blocks, blocks_other, *own, *other)
+
+
+def tail_kernel(wire_ref, rt_ref, tw_ref, *refs):
+    parts, (out_ref, scr) = refs[:CHUNKS], refs[CHUNKS:]
     outer, inner = tw_ref.shape
     chan = out_ref.shape[2]
-    rows = inner // NY
+    rows = inner // NY // CHUNKS
     a = pl.program_id(0)
 
     @pl.when(a == 0)
@@ -301,35 +339,33 @@
 
     col = _column(tw_ref[pl.ds(a, 1), :], inner)
     grad = [(scr[c, pl.ds(a, inner, stride=outer), :] * col).astype(BF16) for c in range(chan // 128)]
-    total_ref[...] = jnp.dot(rt_ref[...], jnp.concatenate(grad, axis=1), preferred_element_type=F32)
-    for d in range(NY):
-        at = pl.ds(pl.multiple_of(_back(s, d) * rows, rows), rows)
-        out_ref[0, at, :] = (total_ref[at, :] + parts[d][...].astype(F32)).astype(BF16)
-
-
-def tail_pass(s, wire, right_t, twiddle, parts):
+    acc = jnp.dot(rt_ref[...], jnp.concatenate(grad, axis=1), preferred_element_type=F32)
+    for q in range(NY):
+        for u in range(CHUNKS):
+            at = (q * CHUNKS + u) * rows
+            out_ref[0, at : at + rows, :] = (acc[at : at + rows] + parts[u][q].astype(F32)).astype(BF16)
+
+
+def tail_pass(wire, right_t, twiddle, parts):
     outer, inner = twiddle.shape
     chan = wire.shape[3]
-    part = pl.BlockSpec((inner // NY, chan), lambda a, s: (a, 0))
+    part = pl.BlockSpec((NY, inner // NY // CHUNKS, chan), lambda a: (0, a, 0))
     return pl.pallas_call(
         tail_kernel,
         name="tail_pass",
-        grid_spec=pltpu.PrefetchScalarGridSpec(
-            num_scalar_prefetch=1,
-            grid=(outer,),
-            in_specs=[
-                pl.BlockSpec(wire.shape, lambda a, s: (0, 0, 0, 0)),
-                pl.BlockSpec(right_t.shape, lambda a, s: (0, 0)),
-                pl.BlockSpec(twiddle.shape, lambda a, s: (0, 0)),
-            ]
-            + [part] * NY,
-            out_specs=pl.BlockSpec((1, inner, chan), lambda a, s: (a, 0, 0)),
-            scratch_shapes=[pltpu.VMEM((chan // 128, outer * inner, 128), F32), pltpu.VMEM((inner, chan), F32)],
-        ),
+        grid=(outer,),
+        in_specs=[
+            pl.BlockSpec(wire.shape, lambda a: (0, 0, 0, 0)),
+            pl.BlockSpec(right_t.shape, lambda a: (0, 0)),
+            pl.BlockSpec(twiddle.shape, lambda a: (0, 0)),
+        ]
+        + [part] * CHUNKS,
+        out_specs=pl.BlockSpec((1, inner, chan), lambda a: (a, 0, 0)),
+        scratch_shapes=[pltpu.VMEM((chan // 128, outer * inner, 128), F32)],
         out_shape=jax.ShapeDtypeStruct((outer, inner, chan), BF16),
         compiler_params=_params(64),
         cost_estimate=_cost(2 * outer * inner * inner * chan, 7 << 20),
-    )(s, wire, right_t, twiddle, *parts)
+    )(wire, right_t, twiddle, *parts)
 
 
 def seq_swap(wire):
@@ -355,29 +391,41 @@
     og3 = out_grad.reshape(outer, inner, chan)
     mixer = jnp.transpose(block_mixer, (1, 2, 0))
 
-    xp3 = to_pair(inputs).reshape(x3.shape)
+    part = outer // CHUNKS
+    middle = []
+    xp = to_pair(x3[:part])
     twisted = seq_swap(right_pass(x3, right_factor, twiddle, seq))
-    middle = middle_pass(s, x3, xp3, blocks)
-    middle = around(middle)
+    middle.append(middle_pass(s, x3, xp, blocks, 0))
+    later, _ = lax.optimization_barrier((x3, middle[0][0]))
+    xp = to_pair(later[part:])
+    middle.append(middle_pass(s, x3, xp, blocks, 1))
     mixed_wire = left_pass(left_factor, twisted)
-
     mixed = seq_swap(mixed_wire)
-    pieces = around(mix_pass(s, mixer, middle, False))
+    pieces = []
+    for u in range(CHUNKS):
+        mixes = mix_pass(s, mixer, around(middle[u]), False)
+        pieces += around(mixes)
+    blocks_other = to_pair(blocks)
     gate3, grad_mixed = gate_pass(s, og3, pieces, seq)
 
     grad_mixed, mixed = lax.optimization_barrier((grad_mixed, mixed))
     grad_wire = seq_swap(grad_mixed)
-    output, pieces = out_pass(s, mixed, gate3, og3)
-    grad_middle = mix_pass(s, mixer, around(pieces), True)
+    grads, others = [], []
+    for u in range(CHUNKS):
+        cots = cot_pass(s, mixed, og3, u)
+        cots = around(cots)
+        cots = mix_pass(s, mixer, cots, True)
+        grads.append(around(cots))
+        others.append([None] * NY)
+        for d in (0, 1, 3, 2):
+            others[u][d] = to_pair(grads[u][d])
+    output = out_pass(mixed, gate3)
     grad_wire = left_pass(left_factor.T, grad_wire)
-    blocks_other = to_pair(blocks)
-
-    grad_middle = around(grad_middle)
     grad_twisted = seq_swap(grad_wire)
-    parts = [None] * NY
-    for d in (0, 1, 3, 2):
-        parts[d] = chan_pass(s, blocks, blocks_other, grad_middle[d], to_pair(grad_middle[d]))
-    input_grad = tail_pass(s, grad_twisted, right_factor.T, twiddle, parts)
+    parts = []
+    for u in range(CHUNKS):
+        parts.append(chan_pass(s, blocks, blocks_other, grads[u], others[u]))
+    input_grad = tail_pass(grad_twisted, right_factor.T, twiddle, parts)
     return (output.reshape(inputs.shape), input_grad.reshape(inputs.shape))
 
 

time: 407 us -> 372 us (0.914)
  waiting for transfers between devices: 243 us -> 176 us
  starting transfers between devices: 43.3 us -> 61.8 us
  local copies, waits for them, and re-layouts: 7.93 us -> 15.3 us
  Pallas kernels: 46.3 us -> 52 us
    ppermute x12 -> x24, waiting for transfers between devices: 91.8 us -> 47.4 us  [around(): lax.ppermute(parts[d], 'chan', [(c, (c + 2 * d) % n) for c in range(n)])]
    ppermute x6 -> x11, waiting for transfers between devices: 101 us -> 78.4 us  [to_pair(): return lax.ppermute(v, 'chan', [(c, c ^ 1) for c in range(n)])]
    ppermute x12 -> x24, starting transfers between devices: 16.2 us -> 29.5 us  [around(): lax.ppermute(parts[d], 'chan', [(c, (c + 2 * d) % n) for c in range(n)])]
    unnamed x22 -> x50, local copies, waits for them, and re-layouts: 7.93 us -> 12.9 us
    pallas_call x2 -> x4, Pallas kernels: 14.2 us -> 15.3 us  [the longest x1 8.69 us: tail_pass(): pl.pallas_call(tail_kernel, name='tail_pass', grid=(outer,), in_specs=[pl...]
  transfers between devices with their start and end apart: 21 -> 38, of which waited for: 12 -> 25; matrix products, arithmetic and copies ran while one was open for 1% -> 1% of each run, Pallas kernels for 6% -> 8%
where the time goes in v4:
time: 372 us; the launch traced here: 369 us
  waiting for transfers between devices  176 us (47%)
  blocking collectives  63.2 us (17%)
  starting transfers between devices  61.8 us (17%)
  Pallas kernels  52 us (14%)
  local copies, waits for them, and re-layouts  15.3 us (4%)
    ppermute x11, waiting for transfers between devices, to_pair(): return lax.ppermute(v, 'chan', [(c, c ^ 1) for c in range(n)])  78.4 us
    all_to_all x1, blocking collectives, seq_swap(): return lax.all_to_all(wire, 'seq', split_axis=0, concat_axis=0, tiled=True)  63.2 us
    all_to_all x3, waiting for transfers between devices, seq_swap(): return lax.all_to_all(wire, 'seq', split_axis=0, concat_axis=0, tiled=True)  50 us
    ppermute x24, waiting for transfers between devices, around(): lax.ppermute(parts[d], 'chan', [(c, (c + 2 * d) % n) for c in range(n)])  47.4 us
    ppermute x24, starting transfers between devices, around(): lax.ppermute(parts[d], 'chan', [(c, (c + 2 * d) % n) for c in range(n)])  29.5 us
    all_to_all x3, starting transfers between devices, seq_swap(): return lax.all_to_all(wire, 'seq', split_axis=0, concat_axis=0, tiled=True)  25.5 us
    unnamed x50, local copies, waits for them, and re-layouts  12.9 us
    pallas_call x2, Pallas kernels, left_pass(): pl.pallas_call(left_kernel, name='left_pass', grid=(steps,), in_specs=[pl...  10.5 us
  transfers between devices with their start and end apart: 38, of which 25 were waited for; matrix products, arithmetic and copies ran while one was open for 1% of the time, Pallas kernels for 8%

profile of v4, /device:TPU:1, one launch (start us, length us, event | category | flops | bytes accessed | tf_op | source)
XLA Modules:
  0.0 368.8 jit_solution(9081302305505476830)
XLA Ops:
  0.6 4.6 %right_pass.1 = bf16[32,16,8,256]{3,2,1,0:T(8,128)(2,1)} custom-call(bf16[8,512,256]{2,1,0:T(8,128)(2,1)} %bitcast.9, bf16[512,512]{1,0:T(8,128)(2,1)} %r_ref.1, f32[8,512]{1,0:T(8,128)} %tw_ref.3), custom_call_target="tpu_custom_call" | custom-call | flops 1073741824 | bytes 6291456 | tf_op jit(solution)/shard_map/right_pass/pallas_call | solution.py:58
  5.2 63.2 %all_to_all.20.in_ref = bf16[32,16,8,256]{3,2,1,0:T(8,128)(2,1)S(1)} all-to-all(bf16[32,16,8,256]{3,2,1,0:T(8,128)(2,1)} %right_pass.1), channel_id=1, replica_groups=mesh['seq'=32,'chan'=8] {'seq'}, dimensions={0} | all-to-all | bytes 4194304 | tf_op jit(solution)/shard_map/all_to_all | solution.py:372
  68.4 4.1 %left_pass.2 = bf16[32,16,8,256]{3,2,1,0:T(8,128)(2,1)} custom-call(bf16[256,256]{1,0:T(8,128)(2,1)S(1)} %copy-done.6, bf16[32,16,8,256]{3,2,1,0:T(8,128)(2,1)S(1)} %all_to_all.20.in_ref), custom_call_target="tpu_custom_call" | custom-call | flops 536870912 | bytes 4194304 | tf_op jit(solution)/shard_map/left_pass/pallas_call | solution.py:88
  72.5 5.8 %all-to-all-start.1 = ((bf16[32,16,8,256]{3,2,1,0:T(8,128)(2,1)}), bf16[32,16,8,256]{3,2,1,0:T(8,128)(2,1)S(1)}, u32[]{:S(2)}, u32[]{:S(2)}) async-start(bf16[32,16,8,256]{3,2,1,0:T(8,128)(2,1)} %left_pass.2), calls=%async_computation.1 | async-start | bytes 4194304 | tf_op jit(solution)/shard_map/all_to_all | solution.py:372
  78.4 2.3 slice.9
  81.0 43.4 %collective-permute-done.xp_ref = bf16[4,512,256]{2,1,0:T(8,128)(2,1)S(1)} collective-permute-done((bf16[4,512,256]{2,1,0:T(8,128)(2,1)}, bf16[4,512,256]{2,1,0:T(8,128)(2,1)S(1)}, u32[]{:S(2)}, u32[]{:S(2)}) %collective-permute-start) | collective-permute-done | bytes 1048608 | tf_op jit(solution)/shard_map/ppermute | solution.py:382
  126.0 2.8 middle_pass.2
  131.5 2.6 collective-permute-start.2
  135.2 17.5 %collective-permute-done.7.xp_ref = bf16[4,512,256]{2,1,0:T(8,128)(2,1)S(1)} collective-permute-done((bf16[4,512,256]{2,1,0:T(8,128)(2,1)S(1)}, bf16[4,512,256]{2,1,0:T(8,128)(2,1)S(1)}, u32[]{:S(2)}, u32[]{:S(2)}) %collective-permute-start.7) | collective-permute-done | bytes 1048608 | tf_op jit(solution)/shard_map/ppermute | solution.py:382
  152.8 2.8 middle_pass.3
  156.8 2.7 collective-permute-start.9
  164.8 5.2 %collective-permute-done.9.refs_2_ = bf16[512,256]{1,0:T(8,128)(2,1)S(1)} collective-permute-done((bf16[512,256]{1,0:T(8,128)(2,1)}, bf16[512,256]{1,0:T(8,128)(2,1)S(1)}, u32[]{:S(2)}, u32[]{:S(2)}) %collective-permute-start.9) | collective-permute-done | bytes 262176 | tf_op jit(solution)/shard_map/ppermute | solution.py:386
  175.3 3.1 collective-permute-start.12
  178.4 2.9 collective-permute-done.5.refs_2_
  182.3 4.4 %collective-permute-done.11.refs_5_ = bf16[512,256]{1,0:T(8,128)(2,1)S(1)} collective-permute-done((bf16[512,256]{1,0:T(8,128)(2,1)}, bf16[512,256]{1,0:T(8,128)(2,1)S(1)}, u32[]{:S(2)}, u32[]{:S(2)}) %collective-permute-start.11) | collective-permute-done | bytes 262176 | tf_op jit(solution)/shard_map/ppermute | solution.py:386
  186.7 5.8 %collective-permute-done.12.refs_6_ = bf16[512,256]{1,0:T(8,128)(2,1)S(1)} collective-permute-done((bf16[512,256]{1,0:T(8,128)(2,1)}, bf16[512,256]{1,0:T(8,128)(2,1)S(1)}, u32[]{:S(2)}, u32[]{:S(2)}) %collective-permute-start.12) | collective-permute-done | bytes 262176 | tf_op jit(solution)/shard_map/ppermute | solution.py:386
  194.4 3.4 gate_pass.1
  197.8 13.3 %all-to-all-start.2 = ((bf16[32,16,8,256]{3,2,1,0:T(8,128)(2,1)}), bf16[32,16,8,256]{3,2,1,0:T(8,128)(2,1)}, u32[]{:S(2)}, u32[]{:S(2)}) async-start(bf16[32,16,8,256]{3,2,1,0:T(8,128)(2,1)} %get-tuple-element.59), calls=%async_computation.2 | async-start | bytes 4194304 | tf_op jit(solution)/shard_map/all_to_all | solution.py:372
  211.2 50.0 %all-to-all-done.2.in_ref = bf16[32,16,8,256]{3,2,1,0:T(8,128)(2,1)} async-done(((bf16[32,16,8,256]{3,2,1,0:T(8,128)(2,1)}), bf16[32,16,8,256]{3,2,1,0:T(8,128)(2,1)}, u32[]{:S(2)}, u32[]{:S(2)}) %all-to-all-start.2) | async-done | bytes 2097184 | tf_op jit(solution)/shard_map/all_to_all | solution.py:372
  261.2 6.4 %left_pass.3 = bf16[32,16,8,256]{3,2,1,0:T(8,128)(2,1)} custom-call(bf16[256,256]{1,0:T(8,128)(2,1)S(1)} %bitcast.20, bf16[32,16,8,256]{3,2,1,0:T(8,128)(2,1)} %all-to-all-done.2.in_ref), custom_call_target="tpu_custom_call" | custom-call | flops 536870912 | bytes 4194304 | tf_op jit(solution)/shard_map/left_pass/pallas_call | solution.py:88
  267.6 6.4 %all-to-all-start.3 = ((bf16[32,16,8,256]{3,2,1,0:T(8,128)(2,1)}), bf16[32,16,8,256]{3,2,1,0:T(8,128)(2,1)}, u32[]{:S(2)}, u32[]{:S(2)}) async-start(bf16[32,16,8,256]{3,2,1,0:T(8,128)(2,1)} %left_pass.3), calls=%async_computation.3 | async-start | bytes 4194304 | tf_op jit(solution)/shard_map/all_to_all | solution.py:372
  287.1 5.4 %collective-permute-done.26.refs_2_ = bf16[512,256]{1,0:T(8,128)(2,1)S(1)} collective-permute-done((bf16[512,256]{1,0:T(8,128)(2,1)}, bf16[512,256]{1,0:T(8,128)(2,1)S(1)}, u32[]{:S(2)}, u32[]{:S(2)}) %collective-permute-start.26) | collective-permute-done | bytes 262176 | tf_op jit(solution)/shard_map/ppermute | solution.py:386
  299.3 4.4 %collective-permute-done.16.refs_2_ = bf16[512,256]{1,0:T(8,128)(2,1)S(1)} collective-permute-done((bf16[512,256]{1,0:T(8,128)(2,1)}, bf16[512,256]{1,0:T(8,128)(2,1)S(1)}, u32[]{:S(2)}, u32[]{:S(2)}) %collective-permute-start.16) | collective-permute-done | bytes 262176 | tf_op jit(solution)/shard_map/ppermute | solution.py:386
  311.4 3.7 collective-permute-done.29.refs_2_
  321.9 4.4 %collective-permute-done.19.refs_2_ = bf16[512,256]{1,0:T(8,128)(2,1)} collective-permute-done((bf16[512,256]{1,0:T(8,128)(2,1)}, bf16[512,256]{1,0:T(8,128)(2,1)}, u32[]{:S(2)}, u32[]{:S(2)}) %collective-permute-start.19) | collective-permute-done | bytes 262176 | tf_op jit(solution)/shard_map/ppermute | solution.py:386
  334.6 2.8 out_pass.1
  337.4 3.4 chan_pass.3.refs_1_
  340.8 4.2 %collective-permute-done.22.refs_5_ = bf16[512,256]{1,0:T(8,128)(2,1)} collective-permute-done((bf16[512,256]{1,0:T(8,128)(2,1)}, bf16[512,256]{1,0:T(8,128)(2,1)}, u32[]{:S(2)}, u32[]{:S(2)}) %collective-permute-start.22) | collective-permute-done | bytes 262176 | tf_op jit(solution)/shard_map/ppermute | solution.py:382
  345.0 5.6 %collective-permute-done.23.refs_6_ = bf16[512,256]{1,0:T(8,128)(2,1)} collective-permute-done((bf16[512,256]{1,0:T(8,128)(2,1)}, bf16[512,256]{1,0:T(8,128)(2,1)}, u32[]{:S(2)}, u32[]{:S(2)}) %collective-permute-start.23) | collective-permute-done | bytes 262176 | tf_op jit(solution)/shard_map/ppermute | solution.py:382
  350.6 5.6 %collective-permute-done.24.refs_7_ = bf16[512,256]{1,0:T(8,128)(2,1)} collective-permute-done((bf16[512,256]{1,0:T(8,128)(2,1)}, bf16[512,256]{1,0:T(8,128)(2,1)}, u32[]{:S(2)}, u32[]{:S(2)}) %collective-permute-start.24) | collective-permute-done | bytes 262176 | tf_op jit(solution)/shard_map/ppermute | solution.py:382
  356.3 3.8 %chan_pass.2.refs_0_ = bf16[4,512,256]{2,1,0:T(8,128)(2,1)} custom-call(s32[1]{0:T(128)} %bitcast.s, bf16[256,512]{1,0:T(8,128)(2,1)S(1)} %copy-done.3, bf16[256,512]{1,0:T(8,128)(2,1)S(1)} %collective-permute-done.14.bo_ref, bf16[512,256]{1,0:T(8,128)(2,1)S(1)} %copy-done.14, bf16[512,256]{1,0:T(8,128)(2,1)} %collective-permute-done.18.refs_1_, ...), custom_call_target="tpu_custom_call" | custom-call | flops 536870912 | bytes 3145728 | tf_op jit(solution)/shard_map/chan_pass/pallas_call | solution.py:313
  360.1 8.7 %tail_pass.1 = bf16[8,512,256]{2,1,0:T(8,128)(2,1)} custom-call(bf16[32,16,8,256]{3,2,1,0:T(8,128)(2,1)} %all-to-all-done.3.wire_ref, bf16[512,512]{1,0:T(8,128)(2,1)} %bitcast.23, f32[8,512]{1,0:T(8,128)} %tw_ref.3, bf16[4,512,256]{2,1,0:T(8,128)(2,1)} %chan_pass.2.refs_0_, bf16[4,512,256]{2,1,0:T(8,128)(2,1)} %chan_pass.3.refs_1_), custom_call_target="tpu_custom_call" | custom-call | flops 1073741824 | bytes 7340032 | tf_op jit(solution)/shard_map/tail_pass/pallas_call | solution.py:353
  (113 shorter events, 63.3 us)
Async XLA Ops:
  72.5 125.3 %all-to-all-start.1 = ((bf16[32,16,8,256]{3,2,1,0:T(8,128)(2,1)}), bf16[32,16,8,256]{3,2,1,0:T(8,128)(2,1)S(1)}, u32[]{:S(2)}, u32[]{:S(2)}) async-start(bf16[32,16,8,256]{3,2,1,0:T(8,128)(2,1)} %left_pass.2), calls=%async_computation.1 | async-start | bytes 4194304 | tf_op jit(solution)/shard_map/all_to_all | solution.py:372
  80.7 43.7 %collective-permute-start = (bf16[4,512,256]{2,1,0:T(8,128)(2,1)}, bf16[4,512,256]{2,1,0:T(8,128)(2,1)S(1)}, u32[]{:S(2)}, u32[]{:S(2)}) collective-permute-start(bf16[4,512,256]{2,1,0:T(8,128)(2,1)} %bitcast.4), channel_id=1, source_target_pairs={{0,1},{1,0},{2,3},{3,2},{4,5},{5,4},{6,7},{7,6},{8,9},{9,8},{10,11... | collective-permute-start | bytes 3145736 | tf_op jit(solution)/shard_map/ppermute | solution.py:382
  128.9 23.9 %collective-permute-start.7 = (bf16[4,512,256]{2,1,0:T(8,128)(2,1)S(1)}, bf16[4,512,256]{2,1,0:T(8,128)(2,1)S(1)}, u32[]{:S(2)}, u32[]{:S(2)}) collective-permute-start(bf16[4,512,256]{2,1,0:T(8,128)(2,1)S(1)} %slice.11), channel_id=1, source_target_pairs={{0,1},{1,0},{2,3},{3,2},{4,5},{5,4},{6,7},{7,6},{8,9},{9,8},{10,11... | collective-permute-start | bytes 3145736 | tf_op jit(solution)/shard_map/ppermute | solution.py:382
  130.2 29.2 %collective-permute-start.1 = (bf16[512,256]{1,0:T(8,128)(2,1)S(1)}, bf16[512,256]{1,0:T(8,128)(2,1)S(1)}, u32[]{:S(2)}, u32[]{:S(2)}) collective-permute-start(bf16[512,256]{1,0:T(8,128)(2,1)S(1)} %copy-done.23), channel_id=1, source_target_pairs={{0,2},{1,3},{2,4},{3,5},{4,6},{5,7},{6,0},{7,1},{8,10},{9,11},{10,... | collective-permute-start | bytes 786440 | tf_op jit(solution)/shard_map/ppermute | solution.py:386
  131.5 29.0 %collective-permute-start.2 = (bf16[512,256]{1,0:T(8,128)(2,1)S(1)}, bf16[512,256]{1,0:T(8,128)(2,1)S(1)}, u32[]{:S(2)}, u32[]{:S(2)}) collective-permute-start(bf16[512,256]{1,0:T(8,128)(2,1)S(1)} %copy-done.22), channel_id=1, source_target_pairs={{0,4},{1,5},{2,6},{3,7},{4,0},{5,1},{6,2},{7,3},{8,12},{9,13},{10,... | collective-permute-start | bytes 786440 | tf_op jit(solution)/shard_map/ppermute | solution.py:386
  134.2 26.4 %collective-permute-start.3 = (bf16[512,256]{1,0:T(8,128)(2,1)S(1)}, bf16[512,256]{1,0:T(8,128)(2,1)S(1)}, u32[]{:S(2)}, u32[]{:S(2)}) collective-permute-start(bf16[512,256]{1,0:T(8,128)(2,1)S(1)} %copy-done.21), channel_id=1, source_target_pairs={{0,6},{1,7},{2,0},{3,1},{4,2},{5,3},{6,4},{7,5},{8,14},{9,15},{10,... | collective-permute-start | bytes 786440 | tf_op jit(solution)/shard_map/ppermute | solution.py:386
  156.8 13.2 %collective-permute-start.9 = (bf16[512,256]{1,0:T(8,128)(2,1)}, bf16[512,256]{1,0:T(8,128)(2,1)S(1)}, u32[]{:S(2)}, u32[]{:S(2)}) collective-permute-start(bf16[512,256]{1,0:T(8,128)(2,1)} %get-tuple-element.50), channel_id=1, source_target_pairs={{0,4},{1,5},{2,6},{3,7},{4,0},{5,1},{6,2},{7,3},{8,12},{9,13},{10,... | collective-permute-start | bytes 786440 | tf_op jit(solution)/shard_map/ppermute | solution.py:386
  162.0 16.4 %collective-permute-start.4 = (bf16[512,256]{1,0:T(8,128)(2,1)}, bf16[512,256]{1,0:T(8,128)(2,1)S(1)}, u32[]{:S(2)}, u32[]{:S(2)}) collective-permute-start(bf16[512,256]{1,0:T(8,128)(2,1)} %get-tuple-element.44), channel_id=1, source_target_pairs={{0,2},{1,3},{2,4},{3,5},{4,6},{5,7},{6,0},{7,1},{8,10},{9,11},{10,... | collective-permute-start | bytes 786440 | tf_op jit(solution)/shard_map/ppermute | solution.py:386
  162.4 18.9 %collective-permute-start.5 = (bf16[512,256]{1,0:T(8,128)(2,1)}, bf16[512,256]{1,0:T(8,128)(2,1)S(1)}, u32[]{:S(2)}, u32[]{:S(2)}) collective-permute-start(bf16[512,256]{1,0:T(8,128)(2,1)} %get-tuple-element.45), channel_id=1, source_target_pairs={{0,4},{1,5},{2,6},{3,7},{4,0},{5,1},{6,2},{7,3},{8,12},{9,13},{10,... | collective-permute-start | bytes 786440 | tf_op jit(solution)/shard_map/ppermute | solution.py:386
  163.2 19.1 %collective-permute-start.6 = (bf16[512,256]{1,0:T(8,128)(2,1)}, bf16[512,256]{1,0:T(8,128)(2,1)S(1)}, u32[]{:S(2)}, u32[]{:S(2)}) collective-permute-start(bf16[512,256]{1,0:T(8,128)(2,1)} %get-tuple-element.46), channel_id=1, source_target_pairs={{0,6},{1,7},{2,0},{3,1},{4,2},{5,3},{6,4},{7,5},{8,14},{9,15},{10,... | collective-permute-start | bytes 786440 | tf_op jit(solution)/shard_map/ppermute | solution.py:386
  173.4 13.3 %collective-permute-start.11 = (bf16[512,256]{1,0:T(8,128)(2,1)}, bf16[512,256]{1,0:T(8,128)(2,1)S(1)}, u32[]{:S(2)}, u32[]{:S(2)}) collective-permute-start(bf16[512,256]{1,0:T(8,128)(2,1)} %get-tuple-element.53), channel_id=1, source_target_pairs={{0,2},{1,3},{2,4},{3,5},{4,6},{5,7},{6,0},{7,1},{8,10},{9,11},{10,... | collective-permute-start | bytes 786440 | tf_op jit(solution)/shard_map/ppermute | solution.py:386
  175.3 17.2 %collective-permute-start.12 = (bf16[512,256]{1,0:T(8,128)(2,1)}, bf16[512,256]{1,0:T(8,128)(2,1)S(1)}, u32[]{:S(2)}, u32[]{:S(2)}) collective-permute-start(bf16[512,256]{1,0:T(8,128)(2,1)} %get-tuple-element.54), channel_id=1, source_target_pairs={{0,4},{1,5},{2,6},{3,7},{4,0},{5,1},{6,2},{7,3},{8,12},{9,13},{10,... | collective-permute-start | bytes 786440 | tf_op jit(solution)/shard_map/ppermute | solution.py:386
  178.4 14.2 %collective-permute-start.13 = (bf16[512,256]{1,0:T(8,128)(2,1)}, bf16[512,256]{1,0:T(8,128)(2,1)S(1)}, u32[]{:S(2)}, u32[]{:S(2)}) collective-permute-start(bf16[512,256]{1,0:T(8,128)(2,1)} %get-tuple-element.55), channel_id=1, source_target_pairs={{0,6},{1,7},{2,0},{3,1},{4,2},{5,3},{6,4},{7,5},{8,14},{9,15},{10,... | collective-permute-start | bytes 786440 | tf_op jit(solution)/shard_map/ppermute | solution.py:386
  197.8 63.4 %all-to-all-start.2 = ((bf16[32,16,8,256]{3,2,1,0:T(8,128)(2,1)}), bf16[32,16,8,256]{3,2,1,0:T(8,128)(2,1)}, u32[]{:S(2)}, u32[]{:S(2)}) async-start(bf16[32,16,8,256]{3,2,1,0:T(8,128)(2,1)} %get-tuple-element.59), calls=%async_computation.2 | async-start | bytes 4194304 | tf_op jit(solution)/shard_map/all_to_all | solution.py:372
  267.6 92.5 %all-to-all-start.3 = ((bf16[32,16,8,256]{3,2,1,0:T(8,128)(2,1)}), bf16[32,16,8,256]{3,2,1,0:T(8,128)(2,1)}, u32[]{:S(2)}, u32[]{:S(2)}) async-start(bf16[32,16,8,256]{3,2,1,0:T(8,128)(2,1)} %left_pass.3), calls=%async_computation.3 | async-start | bytes 4194304 | tf_op jit(solution)/shard_map/all_to_all | solution.py:372
  278.3 14.2 %collective-permute-start.26 = (bf16[512,256]{1,0:T(8,128)(2,1)}, bf16[512,256]{1,0:T(8,128)(2,1)S(1)}, u32[]{:S(2)}, u32[]{:S(2)}) collective-permute-start(bf16[512,256]{1,0:T(8,128)(2,1)} %get-tuple-element.70), channel_id=1, source_target_pairs={{0,4},{1,5},{2,6},{3,7},{4,0},{5,1},{6,2},{7,3},{8,12},{9,13},{10,... | collective-permute-start | bytes 786440 | tf_op jit(solution)/shard_map/ppermute | solution.py:386
  280.4 12.5 %collective-permute-start.27 = (bf16[512,256]{1,0:T(8,128)(2,1)}, bf16[512,256]{1,0:T(8,128)(2,1)S(1)}, u32[]{:S(2)}, u32[]{:S(2)}) collective-permute-start(bf16[512,256]{1,0:T(8,128)(2,1)} %get-tuple-element.71), channel_id=1, source_target_pairs={{0,6},{1,7},{2,0},{3,1},{4,2},{5,3},{6,4},{7,5},{8,14},{9,15},{10,... | collective-permute-start | bytes 786440 | tf_op jit(solution)/shard_map/ppermute | solution.py:386
  283.8 14.9 %collective-permute-start.15 = (bf16[512,256]{1,0:T(8,128)(2,1)}, bf16[512,256]{1,0:T(8,128)(2,1)S(1)}, u32[]{:S(2)}, u32[]{:S(2)}) collective-permute-start(bf16[512,256]{1,0:T(8,128)(2,1)} %get-tuple-element.61), channel_id=1, source_target_pairs={{0,2},{1,3},{2,4},{3,5},{4,6},{5,7},{6,0},{7,1},{8,10},{9,11},{10,... | collective-permute-start | bytes 786440 | tf_op jit(solution)/shard_map/ppermute | solution.py:386
  283.8 19.9 %collective-permute-start.16 = (bf16[512,256]{1,0:T(8,128)(2,1)}, bf16[512,256]{1,0:T(8,128)(2,1)S(1)}, u32[]{:S(2)}, u32[]{:S(2)}) collective-permute-start(bf16[512,256]{1,0:T(8,128)(2,1)} %get-tuple-element.62), channel_id=1, source_target_pairs={{0,4},{1,5},{2,6},{3,7},{4,0},{5,1},{6,2},{7,3},{8,12},{9,13},{10,... | collective-permute-start | bytes 786440 | tf_op jit(solution)/shard_map/ppermute | solution.py:386
  286.6 17.5 %collective-permute-start.17 = (bf16[512,256]{1,0:T(8,128)(2,1)}, bf16[512,256]{1,0:T(8,128)(2,1)S(1)}, u32[]{:S(2)}, u32[]{:S(2)}) collective-permute-start(bf16[512,256]{1,0:T(8,128)(2,1)} %get-tuple-element.63), channel_id=1, source_target_pairs={{0,6},{1,7},{2,0},{3,1},{4,2},{5,3},{6,4},{7,5},{8,14},{9,15},{10,... | collective-permute-start | bytes 786440 | tf_op jit(solution)/shard_map/ppermute | solution.py:386
  292.5 13.9 %collective-permute-start.14 = (bf16[256,512]{1,0:T(8,128)(2,1)S(1)}, bf16[256,512]{1,0:T(8,128)(2,1)S(1)}, u32[]{:S(2)}, u32[]{:S(2)}) collective-permute-start(bf16[256,512]{1,0:T(8,128)(2,1)S(1)} %copy-done.3), channel_id=1, source_target_pairs={{0,1},{1,0},{2,3},{3,2},{4,5},{5,4},{6,7},{7,6},{8,9},{9,8},{10,11... | collective-permute-start | bytes 786440 | tf_op jit(solution)/shard_map/ppermute | solution.py:382
  294.2 16.4 %collective-permute-start.28 = (bf16[512,256]{1,0:T(8,128)(2,1)}, bf16[512,256]{1,0:T(8,128)(2,1)S(1)}, u32[]{:S(2)}, u32[]{:S(2)}) collective-permute-start(bf16[512,256]{1,0:T(8,128)(2,1)} %get-tuple-element.73), channel_id=1, source_target_pairs={{0,2},{1,3},{2,4},{3,5},{4,6},{5,7},{6,0},{7,1},{8,10},{9,11},{10,... | collective-permute-start | bytes 786440 | tf_op jit(solution)/shard_map/ppermute | solution.py:386
  298.7 16.3 %collective-permute-start.29 = (bf16[512,256]{1,0:T(8,128)(2,1)}, bf16[512,256]{1,0:T(8,128)(2,1)S(1)}, u32[]{:S(2)}, u32[]{:S(2)}) collective-permute-start(bf16[512,256]{1,0:T(8,128)(2,1)} %get-tuple-element.74), channel_id=1, source_target_pairs={{0,4},{1,5},{2,6},{3,7},{4,0},{5,1},{6,2},{7,3},{8,12},{9,13},{10,... | collective-permute-start | bytes 786440 | tf_op jit(solution)/shard_map/ppermute | solution.py:386
  304.1 13.1 %collective-permute-start.31 = (bf16[512,256]{1,0:T(8,128)(2,1)}, bf16[512,256]{1,0:T(8,128)(2,1)S(1)}, u32[]{:S(2)}, u32[]{:S(2)}) collective-permute-start(bf16[512,256]{1,0:T(8,128)(2,1)} %get-tuple-element.72.refs_0_), channel_id=1, source_target_pairs={{0,1},{1,0},{2,3},{3,2},{4,5},{5,4},{6,7},{7,6},{8,9},{9,8},{10,11... | collective-permute-start | bytes 786440 | tf_op jit(solution)/shard_map/ppermute | solution.py:382
  306.4 15.5 %collective-permute-start.18 = (bf16[512,256]{1,0:T(8,128)(2,1)}, bf16[512,256]{1,0:T(8,128)(2,1)}, u32[]{:S(2)}, u32[]{:S(2)}) collective-permute-start(bf16[512,256]{1,0:T(8,128)(2,1)} %get-tuple-element.65), channel_id=1, source_target_pairs={{0,2},{1,3},{2,4},{3,5},{4,6},{5,7},{6,0},{7,1},{8,10},{9,11},{10,... | collective-permute-start | bytes 786440 | tf_op jit(solution)/shard_map/ppermute | solution.py:386
  310.6 15.6 %collective-permute-start.19 = (bf16[512,256]{1,0:T(8,128)(2,1)}, bf16[512,256]{1,0:T(8,128)(2,1)}, u32[]{:S(2)}, u32[]{:S(2)}) collective-permute-start(bf16[512,256]{1,0:T(8,128)(2,1)} %get-tuple-element.66), channel_id=1, source_target_pairs={{0,4},{1,5},{2,6},{3,7},{4,0},{5,1},{6,2},{7,3},{8,12},{9,13},{10,... | collective-permute-start | bytes 786440 | tf_op jit(solution)/shard_map/ppermute | solution.py:386
  315.1 12.6 %collective-permute-start.32 = (bf16[512,256]{1,0:T(8,128)(2,1)S(1)}, bf16[512,256]{1,0:T(8,128)(2,1)S(1)}, u32[]{:S(2)}, u32[]{:S(2)}) collective-permute-start(bf16[512,256]{1,0:T(8,128)(2,1)S(1)} %collective-permute-done.28.refs_1_), channel_id=1, source_target_pairs={{0,1},{1,0},{2,3},{3,2},{4,5},{5,4},{6,7},{7,6},{8,9},{9,8},{10,11... | collective-permute-start | bytes 786440 | tf_op jit(solution)/shard_map/ppermute | solution.py:382
  321.9 15.5 %collective-permute-start.34 = (bf16[512,256]{1,0:T(8,128)(2,1)S(1)}, bf16[512,256]{1,0:T(8,128)(2,1)}, u32[]{:S(2)}, u32[]{:S(2)}) collective-permute-start(bf16[512,256]{1,0:T(8,128)(2,1)S(1)} %collective-permute-done.30.refs_3_), channel_id=1, source_target_pairs={{0,1},{1,0},{2,3},{3,2},{4,5},{5,4},{6,7},{7,6},{8,9},{9,8},{10,11... | collective-permute-start | bytes 786440 | tf_op jit(solution)/shard_map/ppermute | solution.py:382
  326.3 14.6 %collective-permute-start.21 = (bf16[512,256]{1,0:T(8,128)(2,1)}, bf16[512,256]{1,0:T(8,128)(2,1)}, u32[]{:S(2)}, u32[]{:S(2)}) collective-permute-start(bf16[512,256]{1,0:T(8,128)(2,1)} %get-tuple-element.64.refs_0_), channel_id=1, source_target_pairs={{0,1},{1,0},{2,3},{3,2},{4,5},{5,4},{6,7},{7,6},{8,9},{9,8},{10,11... | collective-permute-start | bytes 786440 | tf_op jit(solution)/shard_map/ppermute | solution.py:382
  326.4 18.6 %collective-permute-start.22 = (bf16[512,256]{1,0:T(8,128)(2,1)}, bf16[512,256]{1,0:T(8,128)(2,1)}, u32[]{:S(2)}, u32[]{:S(2)}) collective-permute-start(bf16[512,256]{1,0:T(8,128)(2,1)} %collective-permute-done.18.refs_1_), channel_id=1, source_target_pairs={{0,1},{1,0},{2,3},{3,2},{4,5},{5,4},{6,7},{7,6},{8,9},{9,8},{10,11... | collective-permute-start | bytes 786440 | tf_op jit(solution)/shard_map/ppermute | solution.py:382
  328.4 22.2 %collective-permute-start.23 = (bf16[512,256]{1,0:T(8,128)(2,1)}, bf16[512,256]{1,0:T(8,128)(2,1)}, u32[]{:S(2)}, u32[]{:S(2)}) collective-permute-start(bf16[512,256]{1,0:T(8,128)(2,1)} %collective-permute-done.19.refs_2_), channel_id=1, source_target_pairs={{0,1},{1,0},{2,3},{3,2},{4,5},{5,4},{6,7},{7,6},{8,9},{9,8},{10,11... | collective-permute-start | bytes 786440 | tf_op jit(solution)/shard_map/ppermute | solution.py:382
  329.3 27.0 %collective-permute-start.24 = (bf16[512,256]{1,0:T(8,128)(2,1)}, bf16[512,256]{1,0:T(8,128)(2,1)}, u32[]{:S(2)}, u32[]{:S(2)}) collective-permute-start(bf16[512,256]{1,0:T(8,128)(2,1)} %collective-permute-done.20.refs_3_), channel_id=1, source_target_pairs={{0,1},{1,0},{2,3},{3,2},{4,5},{5,4},{6,7},{7,6},{8,9},{9,8},{10,11... | collective-permute-start | bytes 786440 | tf_op jit(solution)/shard_map/ppermute | solution.py:382
  (30 other events, 355.6 us)

commit v5 on v4

--- a/solution.py
+++ b/solution.py
@@ -14,7 +14,7 @@
 CHUNKS = 2
 
 
-def _params(mib=32):
+def _params(mib=64):
     return pltpu.CompilerParams(vmem_limit_bytes=min(mib << 20, 67043328))
 
 
@@ -38,9 +38,11 @@
     return jnp.transpose(jnp.broadcast_to(row, (128, length)))
 
 
-def right_kernel(x_ref, r_ref, tw_ref, out_ref, scr):
+def right_kernel(x_ref, r_ref, tw_ref, out_ref, first_ref, scr):
     outer, _, chan = x_ref.shape
     rows = r_ref.shape[0]
+    at = pl.ds(pl.multiple_of(pl.program_id(0) * rows, rows), rows)
+    first_ref[...] = x_ref[: first_ref.shape[0], at, :]
     for a in range(outer):
         acc = jnp.dot(r_ref[...], x_ref[a], preferred_element_type=F32)
         col = _column(tw_ref[a : a + 1, :], rows)
@@ -64,10 +66,13 @@
             pl.BlockSpec((rows, inner), lambda g: (g, 0)),
             pl.BlockSpec((outer, rows), lambda g: (0, g)),
         ],
-        out_specs=pl.BlockSpec((seq // steps, per, outer, chan), lambda g: (g, 0, 0, 0)),
-        out_shape=_hbm((seq, per, outer, chan)),
+        out_specs=[
+            pl.BlockSpec((seq // steps, per, outer, chan), lambda g: (g, 0, 0, 0)),
+            pl.BlockSpec((outer // CHUNKS, rows, chan), lambda g: (0, g, 0)),
+        ],
+        out_shape=[_hbm((seq, per, outer, chan)), _hbm((outer // CHUNKS, inner, chan))],
         scratch_shapes=[pltpu.VMEM((chan // 128, rows * outer, 128), F32)],
-        compiler_params=_params(64),
+        compiler_params=_params(),
         cost_estimate=_cost(2 * outer * inner * inner * chan, 6 << 20),
     )(x3, right, twiddle)
 
@@ -82,7 +87,7 @@
 
 def left_pass(left, wire):
     seq, per, outer, chan = wire.shape
-    steps = 8
+    steps = 2
     full = seq * outer
     block = (seq, per // steps, outer, chan)
     return pl.pallas_call(
@@ -98,6 +103,20 @@
         compiler_params=_params(),
         cost_estimate=_cost(2 * full * full * per * chan, 4 << 20),
     )(left, wire)
+
+
+def turn_kernel(in_ref, out_ref):
+    out_ref[...] = jnp.transpose(in_ref[...].astype(F32)).astype(BF16)
+
+
+def turn_pass(matrix):
+    return pl.pallas_call(
+        turn_kernel,
+        name="turn_pass",
+        out_shape=_hbm(matrix.shape),
+        compiler_params=_params(),
+        cost_estimate=_cost(0, 1 << 18),
+    )(matrix)
 
 
 def middle_kernel(s, x_ref, xp_ref, b_ref, *outs):
@@ -325,45 +344,49 @@
     )(s, blocks, blocks_other, *own, *other)
 
 
-def tail_kernel(wire_ref, rt_ref, tw_ref, *refs):
+def tail_kernel(group, wire_ref, rt_ref, tw_ref, *refs):
     parts, (out_ref, scr) = refs[:CHUNKS], refs[CHUNKS:]
     outer, inner = tw_ref.shape
     chan = out_ref.shape[2]
     rows = inner // NY // CHUNKS
-    a = pl.program_id(0)
-
-    @pl.when(a == 0)
+    g = pl.program_id(0)
+
+    @pl.when(g == 0)
     def _():
         for c in range(chan // 128):
             scr[c] = wire_ref[:, :, :, c * 128 : c * 128 + 128].astype(F32).reshape(scr.shape[1:])
 
-    col = _column(tw_ref[pl.ds(a, 1), :], inner)
-    grad = [(scr[c, pl.ds(a, inner, stride=outer), :] * col).astype(BF16) for c in range(chan // 128)]
-    acc = jnp.dot(rt_ref[...], jnp.concatenate(grad, axis=1), preferred_element_type=F32)
-    for q in range(NY):
-        for u in range(CHUNKS):
-            at = (q * CHUNKS + u) * rows
-            out_ref[0, at : at + rows, :] = (acc[at : at + rows] + parts[u][q].astype(F32)).astype(BF16)
+    for k in range(group):
+        a = g * group + k
+        col = _column(tw_ref[pl.ds(a, 1), :], inner)
+        grad = [(scr[c, pl.ds(a, inner, stride=outer), :] * col).astype(BF16) for c in range(chan // 128)]
+        acc = jnp.dot(rt_ref[...], jnp.concatenate(grad, axis=1), preferred_element_type=F32)
+        for q in range(NY):
+            for u in range(CHUNKS):
+                at = (q * CHUNKS + u) * rows
+                part = parts[u][q, k * rows : k * rows + rows].astype(F32)
+                out_ref[k, at : at + rows, :] = (acc[at : at + rows] + part).astype(BF16)
 
 
 def tail_pass(wire, right_t, twiddle, parts):
     outer, inner = twiddle.shape
     chan = wire.shape[3]
-    part = pl.BlockSpec((NY, inner // NY // CHUNKS, chan), lambda a: (0, a, 0))
-    return pl.pallas_call(
-        tail_kernel,
+    group = outer // 2
+    part = pl.BlockSpec((NY, group * inner // NY // CHUNKS, chan), lambda g: (0, g, 0))
+    return pl.pallas_call(
+        functools.partial(tail_kernel, group),
         name="tail_pass",
-        grid=(outer,),
+        grid=(outer // group,),
         in_specs=[
-            pl.BlockSpec(wire.shape, lambda a: (0, 0, 0, 0)),
-            pl.BlockSpec(right_t.shape, lambda a: (0, 0)),
-            pl.BlockSpec(twiddle.shape, lambda a: (0, 0)),
+            pl.BlockSpec(wire.shape, lambda g: (0, 0, 0, 0)),
+            pl.BlockSpec(right_t.shape, lambda g: (0, 0)),
+            pl.BlockSpec(twiddle.shape, lambda g: (0, 0)),
         ]
         + [part] * CHUNKS,
-        out_specs=pl.BlockSpec((1, inner, chan), lambda a: (a, 0, 0)),
+        out_specs=pl.BlockSpec((group, inner, chan), lambda g: (g, 0, 0)),
         scratch_shapes=[pltpu.VMEM((chan // 128, outer * inner, 128), F32)],
         out_shape=jax.ShapeDtypeStruct((outer, inner, chan), BF16),
-        compiler_params=_params(64),
+        compiler_params=_params(),
         cost_estimate=_cost(2 * outer * inner * inner * chan, 7 << 20),
     )(wire, right_t, twiddle, *parts)
 
@@ -393,8 +416,10 @@
 
     part = outer // CHUNKS
     middle = []
-    xp = to_pair(x3[:part])
-    twisted = seq_swap(right_pass(x3, right_factor, twiddle, seq))
+    twisted, first = right_pass(x3, right_factor, twiddle, seq)
+    xp = to_pair(first)
+    left_t = turn_pass(left_factor)
+    twisted = seq_swap(twisted)
     middle.append(middle_pass(s, x3, xp, blocks, 0))
     later, _ = lax.optimization_barrier((x3, middle[0][0]))
     xp = to_pair(later[part:])
@@ -420,7 +445,7 @@
         for d in (0, 1, 3, 2):
             others[u][d] = to_pair(grads[u][d])
     output = out_pass(mixed, gate3)
-    grad_wire = left_pass(left_factor.T, grad_wire)
+    grad_wire = left_pass(left_t, grad_wire)
     grad_twisted = seq_swap(grad_wire)
     parts = []
     for u in range(CHUNKS):

time: 372 us -> 368 us (0.989)
  local copies, waits for them, and re-layouts: 15.3 us -> 3.34 us
  Pallas kernels: 52 us -> 62.6 us
  waiting for transfers between devices: 176 us -> 170 us
    unnamed x50 -> x3, local copies, waits for them, and re-layouts: 12.9 us -> 2.05 us
    ppermute x24, waiting for transfers between devices: 47.4 us -> 40.9 us  [around(): lax.ppermute(parts[d], 'chan', [(c, (c + 2 * d) % n) for c in range(n)])]
    pallas_call x4, Pallas kernels: 5.46 us -> 10.1 us  [mix_pass(): pl.pallas_call(functools.partial(mix_kernel, flip), name='mix_back' if fl...]
    pallas_call x2, Pallas kernels: 10.5 us -> 6.2 us  [left_pass(): pl.pallas_call(left_kernel, name='left_pass', grid=(steps,), in_specs=[pl...]
    pallas_call x1 -> x2, Pallas kernels: 8.69 us -> 6.78 us  [the longest x1 5.12 us: tail_pass(): pl.pallas_call(functools.partial(tail_kernel, group), name='tail_pass', g...]
  transfers between devices with their start and end apart: 38 -> 38, of which waited for: 25 -> 24; matrix products, arithmetic and copies ran while one was open for 1% -> 1% of each run, Pallas kernels for 8% -> 13%
where the time goes in v5:
time: 368 us; the launch traced here: 364 us
  waiting for transfers between devices  170 us (46%)
  starting transfers between devices  63.8 us (17%)
  blocking collectives  63.2 us (17%)
  Pallas kernels  62.6 us (17%)
    ppermute x11, waiting for transfers between devices, to_pair(): return lax.ppermute(v, 'chan', [(c, c ^ 1) for c in range(n)])  80.7 us
    all_to_all x1, blocking collectives, seq_swap(): return lax.all_to_all(wire, 'seq', split_axis=0, concat_axis=0, tiled=True)  63.2 us
    all_to_all x3, waiting for transfers between devices, seq_swap(): return lax.all_to_all(wire, 'seq', split_axis=0, concat_axis=0, tiled=True)  48.5 us
    ppermute x24, waiting for transfers between devices, around(): lax.ppermute(parts[d], 'chan', [(c, (c + 2 * d) % n) for c in range(n)])  40.9 us
    ppermute x24, starting transfers between devices, around(): lax.ppermute(parts[d], 'chan', [(c, (c + 2 * d) % n) for c in range(n)])  32.8 us
    all_to_all x3, starting transfers between devices, seq_swap(): return lax.all_to_all(wire, 'seq', split_axis=0, concat_axis=0, tiled=True)  24.9 us
    pallas_call x4, Pallas kernels, mix_pass(): pl.pallas_call(functools.partial(mix_kernel, flip), name='mix_back' if fl...  10.1 us
    pallas_call x2, Pallas kernels, middle_pass(): pl.pallas_call(middle_kernel, name='middle_pass', grid_spec=pltpu.Prefetc...  8.78 us
  transfers between devices with their start and end apart: 38, of which 24 were waited for; matrix products, arithmetic and copies ran while one was open for 1% of the time, Pallas kernels for 13%

profile of v5, /device:TPU:1, one launch (start us, length us, event | category | flops | bytes accessed | tf_op | source)
XLA Modules:
  0.0 363.7 jit_solution(7319692861114426520)
XLA Ops:
  0.6 4.8 %right_pass.1 = (bf16[32,16,8,256]{3,2,1,0:T(8,128)(2,1)}, bf16[4,512,256]{2,1,0:T(8,128)(2,1)}) custom-call(bf16[8,512,256]{2,1,0:T(8,128)(2,1)} %bitcast.10, bf16[512,512]{1,0:T(8,128)(2,1)} %r_ref.1, f32[8,512]{1,0:T(8,128)} %tw_ref.3), custom_call_target="tpu_custom_call" | custom-call | flops 1073741824 | bytes 6291456 | tf_op jit(solution)/shard_map/right_pass/pallas_call | solution.py:60
  5.4 63.2 %all_to_all.20.in_ref = bf16[32,16,8,256]{3,2,1,0:T(8,128)(2,1)} all-to-all(bf16[32,16,8,256]{3,2,1,0:T(8,128)(2,1)} %get-tuple-element.60), channel_id=1, replica_groups=mesh['seq'=32,'chan'=8] {'seq'}, dimensions={0} | all-to-all | bytes 4194304 | tf_op jit(solution)/shard_map/all_to_all | solution.py:395
  68.6 3.1 left_pass.2
  71.7 6.0 %all-to-all-start.1 = ((bf16[32,16,8,256]{3,2,1,0:T(8,128)(2,1)}), bf16[32,16,8,256]{3,2,1,0:T(8,128)(2,1)}, u32[]{:S(2)}, u32[]{:S(2)}) async-start(bf16[32,16,8,256]{3,2,1,0:T(8,128)(2,1)} %left_pass.2), calls=%async_computation.1 | async-start | bytes 4194304 | tf_op jit(solution)/shard_map/all_to_all | solution.py:395
  78.2 45.7 %collective-permute-done.xp_ref = bf16[4,512,256]{2,1,0:T(8,128)(2,1)} collective-permute-done((bf16[4,512,256]{2,1,0:T(8,128)(2,1)S(1)}, bf16[4,512,256]{2,1,0:T(8,128)(2,1)}, u32[]{:S(2)}, u32[]{:S(2)}) %collective-permute-start) | collective-permute-done | bytes 1048608 | tf_op jit(solution)/shard_map/ppermute | solution.py:405
  123.9 4.4 %middle_pass.2 = (bf16[512,256]{1,0:T(8,128)(2,1)}, bf16[512,256]{1,0:T(8,128)(2,1)}, bf16[512,256]{1,0:T(8,128)(2,1)}, bf16[512,256]{1,0:T(8,128)(2,1)}) custom-call(s32[1]{0:T(128)} %bitcast.s, bf16[8,512,256]{2,1,0:T(8,128)(2,1)} %bitcast.11, bf16[4,512,256]{2,1,0:T(8,128)(2,1)} %collective-permute-done.xp_ref, bf16[256,512]{1,0:T(8,128)(2,1)} %b_ref.7), custom_call_target="tpu_custom_call" | custom-call | flops 536870912 | bytes 3145728 | tf_op jit(solution)/shard_map/middle_pass/pallas_call | solution.py:144
  135.8 17.8 %collective-permute-done.7.xp_ref = bf16[4,512,256]{2,1,0:T(8,128)(2,1)} collective-permute-done((bf16[4,512,256]{2,1,0:T(8,128)(2,1)S(1)}, bf16[4,512,256]{2,1,0:T(8,128)(2,1)}, u32[]{:S(2)}, u32[]{:S(2)}) %collective-permute-start.7) | collective-permute-done | bytes 1048608 | tf_op jit(solution)/shard_map/ppermute | solution.py:405
  153.6 4.4 %middle_pass.3 = (bf16[512,256]{1,0:T(8,128)(2,1)}, bf16[512,256]{1,0:T(8,128)(2,1)}, bf16[512,256]{1,0:T(8,128)(2,1)}, bf16[512,256]{1,0:T(8,128)(2,1)}) custom-call(s32[1]{0:T(128)} %bitcast.s, bf16[8,512,256]{2,1,0:T(8,128)(2,1)} %bitcast.13, bf16[4,512,256]{2,1,0:T(8,128)(2,1)} %collective-permute-done.7.xp_ref, bf16[256,512]{1,0:T(8,128)(2,1)} %b_ref.7), custom_call_target="tpu_custom_call" | custom-call | flops 536870912 | bytes 3145728 | tf_op jit(solution)/shard_map/middle_pass/pallas_call | solution.py:144
  168.5 4.1 %collective-permute-done.9.refs_2_ = bf16[512,256]{1,0:T(8,128)(2,1)} collective-permute-done((bf16[512,256]{1,0:T(8,128)(2,1)}, bf16[512,256]{1,0:T(8,128)(2,1)}, u32[]{:S(2)}, u32[]{:S(2)}) %collective-permute-start.9) | collective-permute-done | bytes 262176 | tf_op jit(solution)/shard_map/ppermute | solution.py:409
  178.1 3.1 collective-permute-start.12
  184.8 4.7 %collective-permute-done.11.refs_5_ = bf16[512,256]{1,0:T(8,128)(2,1)} collective-permute-done((bf16[512,256]{1,0:T(8,128)(2,1)}, bf16[512,256]{1,0:T(8,128)(2,1)}, u32[]{:S(2)}, u32[]{:S(2)}) %collective-permute-start.11) | collective-permute-done | bytes 262176 | tf_op jit(solution)/shard_map/ppermute | solution.py:409
  189.5 5.6 %collective-permute-done.12.refs_6_ = bf16[512,256]{1,0:T(8,128)(2,1)} collective-permute-done((bf16[512,256]{1,0:T(8,128)(2,1)}, bf16[512,256]{1,0:T(8,128)(2,1)}, u32[]{:S(2)}, u32[]{:S(2)}) %collective-permute-start.12) | collective-permute-done | bytes 262176 | tf_op jit(solution)/shard_map/ppermute | solution.py:409
  195.1 5.5 %gate_pass.1 = (bf16[8,512,256]{2,1,0:T(8,128)(2,1)}, bf16[32,16,8,256]{3,2,1,0:T(8,128)(2,1)}) custom-call(s32[1]{0:T(128)} %bitcast.s, bf16[8,512,256]{2,1,0:T(8,128)(2,1)} %bitcast.7, bf16[512,256]{1,0:T(8,128)(2,1)} %get-tuple-element.46.refs_0_, bf16[512,256]{1,0:T(8,128)(2,1)} %collective-permute-done.4.refs_1_, ...), custom_call_target="tpu_custom_call" | custom-call | flops 1048576 | bytes 8388608 | tf_op jit(solution)/shard_map/gate_pass/pallas_call | solution.py:224
  200.6 12.4 %all-to-all-start.2 = ((bf16[32,16,8,256]{3,2,1,0:T(8,128)(2,1)}), bf16[32,16,8,256]{3,2,1,0:T(8,128)(2,1)}, u32[]{:S(2)}, u32[]{:S(2)}) async-start(bf16[32,16,8,256]{3,2,1,0:T(8,128)(2,1)} %get-tuple-element.63), calls=%async_computation.2 | async-start | bytes 4194304 | tf_op jit(solution)/shard_map/all_to_all | solution.py:395
  214.7 48.4 %all-to-all-done.2.in_ref = bf16[32,16,8,256]{3,2,1,0:T(8,128)(2,1)} async-done(((bf16[32,16,8,256]{3,2,1,0:T(8,128)(2,1)}), bf16[32,16,8,256]{3,2,1,0:T(8,128)(2,1)}, u32[]{:S(2)}, u32[]{:S(2)}) %all-to-all-start.2) | async-done | bytes 2097184 | tf_op jit(solution)/shard_map/all_to_all | solution.py:395
  263.2 3.1 left_pass.3
  266.3 6.4 %all-to-all-start.3 = ((bf16[32,16,8,256]{3,2,1,0:T(8,128)(2,1)}), bf16[32,16,8,256]{3,2,1,0:T(8,128)(2,1)}, u32[]{:S(2)}, u32[]{:S(2)}) async-start(bf16[32,16,8,256]{3,2,1,0:T(8,128)(2,1)} %left_pass.3), calls=%async_computation.3 | async-start | bytes 4194304 | tf_op jit(solution)/shard_map/all_to_all | solution.py:395
  272.7 3.8 %cot_pass.3 = (bf16[512,256]{1,0:T(8,128)(2,1)}, bf16[512,256]{1,0:T(8,128)(2,1)}, bf16[512,256]{1,0:T(8,128)(2,1)}, bf16[512,256]{1,0:T(8,128)(2,1)}) custom-call(s32[1]{0:T(128)} %bitcast.s, bf16[32,16,8,256]{3,2,1,0:T(8,128)(2,1)} %all-to-all-done.1.wire_ref, bf16[8,512,256]{2,1,0:T(8,128)(2,1)} %bitcast.8), custom_call_target="tpu_custom_call" | custom-call | flops 524288 | bytes 3145728 | tf_op jit(solution)/shard_map/cot_pass/pallas_call | solution.py:266
  280.7 3.7 %cot_pass.2 = (bf16[512,256]{1,0:T(8,128)(2,1)}, bf16[512,256]{1,0:T(8,128)(2,1)}, bf16[512,256]{1,0:T(8,128)(2,1)}, bf16[512,256]{1,0:T(8,128)(2,1)}) custom-call(s32[1]{0:T(128)} %bitcast.s, bf16[32,16,8,256]{3,2,1,0:T(8,128)(2,1)} %all-to-all-done.1.wire_ref, bf16[8,512,256]{2,1,0:T(8,128)(2,1)} %bitcast.9), custom_call_target="tpu_custom_call" | custom-call | flops 524288 | bytes 3145728 | tf_op jit(solution)/shard_map/cot_pass/pallas_call | solution.py:266
  287.3 4.1 %collective-permute-done.26.refs_2_ = bf16[512,256]{1,0:T(8,128)(2,1)} collective-permute-done((bf16[512,256]{1,0:T(8,128)(2,1)}, bf16[512,256]{1,0:T(8,128)(2,1)}, u32[]{:S(2)}, u32[]{:S(2)}) %collective-permute-start.26) | collective-permute-done | bytes 262176 | tf_op jit(solution)/shard_map/ppermute | solution.py:409
  299.5 3.3 collective-permute-done.16.refs_2_
  305.6 2.7 collective-permute-start.18
  310.7 3.2 collective-permute-done.29.refs_2_
  317.5 3.4 collective-permute-done.18.refs_1_
  320.9 4.4 %collective-permute-done.19.refs_2_ = bf16[512,256]{1,0:T(8,128)(2,1)} collective-permute-done((bf16[512,256]{1,0:T(8,128)(2,1)}, bf16[512,256]{1,0:T(8,128)(2,1)}, u32[]{:S(2)}, u32[]{:S(2)}) %collective-permute-start.19) | collective-permute-done | bytes 262176 | tf_op jit(solution)/shard_map/ppermute | solution.py:409
  330.5 4.7 %out_pass.1 = bf16[8,512,256]{2,1,0:T(8,128)(2,1)} custom-call(bf16[32,16,8,256]{3,2,1,0:T(8,128)(2,1)} %all-to-all-done.1.wire_ref, bf16[8,512,256]{2,1,0:T(8,128)(2,1)} %get-tuple-element.62.gate_ref), custom_call_target="tpu_custom_call" | custom-call | flops 1048576 | bytes 6291456 | tf_op jit(solution)/shard_map/out_pass/pallas_call | solution.py:301
  335.2 4.1 %chan_pass.3.refs_1_ = bf16[4,512,256]{2,1,0:T(8,128)(2,1)} custom-call(s32[1]{0:T(128)} %bitcast.s, bf16[256,512]{1,0:T(8,128)(2,1)} %b_ref.7, bf16[256,512]{1,0:T(8,128)(2,1)} %collective-permute-done.14.bo_ref, bf16[512,256]{1,0:T(8,128)(2,1)} %get-tuple-element.76.refs_0_, bf16[512,256]{1,0:T(8,128)(2,1)} %collective-permute-done.28.refs_1_, ...), custom_call_target="tpu_custom_call" | custom-call | flops 536870912 | bytes 3145728 | tf_op jit(solution)/shard_map/chan_pass/pallas_call | solution.py:332
  339.3 3.9 %collective-permute-done.22.refs_5_ = bf16[512,256]{1,0:T(8,128)(2,1)} collective-permute-done((bf16[512,256]{1,0:T(8,128)(2,1)}, bf16[512,256]{1,0:T(8,128)(2,1)}, u32[]{:S(2)}, u32[]{:S(2)}) %collective-permute-start.22) | collective-permute-done | bytes 262176 | tf_op jit(solution)/shard_map/ppermute | solution.py:405
  343.2 5.6 %collective-permute-done.23.refs_6_ = bf16[512,256]{1,0:T(8,128)(2,1)} collective-permute-done((bf16[512,256]{1,0:T(8,128)(2,1)}, bf16[512,256]{1,0:T(8,128)(2,1)}, u32[]{:S(2)}, u32[]{:S(2)}) %collective-permute-start.23) | collective-permute-done | bytes 262176 | tf_op jit(solution)/shard_map/ppermute | solution.py:405
  348.9 5.6 %collective-permute-done.24.refs_7_ = bf16[512,256]{1,0:T(8,128)(2,1)} collective-permute-done((bf16[512,256]{1,0:T(8,128)(2,1)}, bf16[512,256]{1,0:T(8,128)(2,1)}, u32[]{:S(2)}, u32[]{:S(2)}) %collective-permute-start.24) | collective-permute-done | bytes 262176 | tf_op jit(solution)/shard_map/ppermute | solution.py:405
  354.5 4.1 %chan_pass.2.refs_0_ = bf16[4,512,256]{2,1,0:T(8,128)(2,1)} custom-call(s32[1]{0:T(128)} %bitcast.s, bf16[256,512]{1,0:T(8,128)(2,1)} %b_ref.7, bf16[256,512]{1,0:T(8,128)(2,1)} %collective-permute-done.14.bo_ref, bf16[512,256]{1,0:T(8,128)(2,1)} %get-tuple-element.68.refs_0_, bf16[512,256]{1,0:T(8,128)(2,1)} %collective-permute-done.18.refs_1_, ...), custom_call_target="tpu_custom_call" | custom-call | flops 536870912 | bytes 3145728 | tf_op jit(solution)/shard_map/chan_pass/pallas_call | solution.py:332
  358.6 5.1 %tail_pass.1 = bf16[8,512,256]{2,1,0:T(8,128)(2,1)} custom-call(bf16[32,16,8,256]{3,2,1,0:T(8,128)(2,1)} %all-to-all-done.3.wire_ref, bf16[512,512]{1,0:T(8,128)(2,1)} %bitcast.16, f32[8,512]{1,0:T(8,128)} %tw_ref.3, bf16[4,512,256]{2,1,0:T(8,128)(2,1)} %chan_pass.2.refs_0_, bf16[4,512,256]{2,1,0:T(8,128)(2,1)} %chan_pass.3.refs_1_), custom_call_target="tpu_custom_call" | custom-call | flops 1073741824 | bytes 7340032 | tf_op jit(solution)/shard_map/tail_pass/pallas_call | solution.py:376
  (66 shorter events, 58.3 us)
Async XLA Ops:
  71.7 128.9 %all-to-all-start.1 = ((bf16[32,16,8,256]{3,2,1,0:T(8,128)(2,1)}), bf16[32,16,8,256]{3,2,1,0:T(8,128)(2,1)}, u32[]{:S(2)}, u32[]{:S(2)}) async-start(bf16[32,16,8,256]{3,2,1,0:T(8,128)(2,1)} %left_pass.2), calls=%async_computation.1 | async-start | bytes 4194304 | tf_op jit(solution)/shard_map/all_to_all | solution.py:395
  77.8 46.1 %collective-permute-start = (bf16[4,512,256]{2,1,0:T(8,128)(2,1)S(1)}, bf16[4,512,256]{2,1,0:T(8,128)(2,1)}, u32[]{:S(2)}, u32[]{:S(2)}) collective-permute-start(bf16[4,512,256]{2,1,0:T(8,128)(2,1)S(1)} %copy-done), channel_id=1, source_target_pairs={{0,1},{1,0},{2,3},{3,2},{4,5},{5,4},{6,7},{7,6},{8,9},{9,8},{10,11... | collective-permute-start | bytes 3145736 | tf_op jit(solution)/shard_map/ppermute | solution.py:405
  129.6 24.0 %collective-permute-start.7 = (bf16[4,512,256]{2,1,0:T(8,128)(2,1)S(1)}, bf16[4,512,256]{2,1,0:T(8,128)(2,1)}, u32[]{:S(2)}, u32[]{:S(2)}) collective-permute-start(bf16[4,512,256]{2,1,0:T(8,128)(2,1)S(1)} %slice.3), channel_id=1, source_target_pairs={{0,1},{1,0},{2,3},{3,2},{4,5},{5,4},{6,7},{7,6},{8,9},{9,8},{10,11... | collective-permute-start | bytes 3145736 | tf_op jit(solution)/shard_map/ppermute | solution.py:405
  130.8 31.1 %collective-permute-start.1 = (bf16[512,256]{1,0:T(8,128)(2,1)}, bf16[512,256]{1,0:T(8,128)(2,1)}, u32[]{:S(2)}, u32[]{:S(2)}) collective-permute-start(bf16[512,256]{1,0:T(8,128)(2,1)} %get-tuple-element.43), channel_id=1, source_target_pairs={{0,2},{1,3},{2,4},{3,5},{4,6},{5,7},{6,0},{7,1},{8,10},{9,11},{10,... | collective-permute-start | bytes 786440 | tf_op jit(solution)/shard_map/ppermute | solution.py:409
  132.1 30.9 %collective-permute-start.2 = (bf16[512,256]{1,0:T(8,128)(2,1)}, bf16[512,256]{1,0:T(8,128)(2,1)}, u32[]{:S(2)}, u32[]{:S(2)}) collective-permute-start(bf16[512,256]{1,0:T(8,128)(2,1)} %get-tuple-element.44), channel_id=1, source_target_pairs={{0,4},{1,5},{2,6},{3,7},{4,0},{5,1},{6,2},{7,3},{8,12},{9,13},{10,... | collective-permute-start | bytes 786440 | tf_op jit(solution)/shard_map/ppermute | solution.py:409
  134.7 28.3 %collective-permute-start.3 = (bf16[512,256]{1,0:T(8,128)(2,1)}, bf16[512,256]{1,0:T(8,128)(2,1)}, u32[]{:S(2)}, u32[]{:S(2)}) collective-permute-start(bf16[512,256]{1,0:T(8,128)(2,1)} %get-tuple-element.45), channel_id=1, source_target_pairs={{0,6},{1,7},{2,0},{3,1},{4,2},{5,3},{6,4},{7,5},{8,14},{9,15},{10,... | collective-permute-start | bytes 786440 | tf_op jit(solution)/shard_map/ppermute | solution.py:409
  159.3 13.2 %collective-permute-start.9 = (bf16[512,256]{1,0:T(8,128)(2,1)}, bf16[512,256]{1,0:T(8,128)(2,1)}, u32[]{:S(2)}, u32[]{:S(2)}) collective-permute-start(bf16[512,256]{1,0:T(8,128)(2,1)} %get-tuple-element.53), channel_id=1, source_target_pairs={{0,4},{1,5},{2,6},{3,7},{4,0},{5,1},{6,2},{7,3},{8,12},{9,13},{10,... | collective-permute-start | bytes 786440 | tf_op jit(solution)/shard_map/ppermute | solution.py:409
  165.5 15.6 %collective-permute-start.4 = (bf16[512,256]{1,0:T(8,128)(2,1)}, bf16[512,256]{1,0:T(8,128)(2,1)}, u32[]{:S(2)}, u32[]{:S(2)}) collective-permute-start(bf16[512,256]{1,0:T(8,128)(2,1)} %get-tuple-element.47), channel_id=1, source_target_pairs={{0,2},{1,3},{2,4},{3,5},{4,6},{5,7},{6,0},{7,1},{8,10},{9,11},{10,... | collective-permute-start | bytes 786440 | tf_op jit(solution)/shard_map/ppermute | solution.py:409
  166.0 17.9 %collective-permute-start.5 = (bf16[512,256]{1,0:T(8,128)(2,1)}, bf16[512,256]{1,0:T(8,128)(2,1)}, u32[]{:S(2)}, u32[]{:S(2)}) collective-permute-start(bf16[512,256]{1,0:T(8,128)(2,1)} %get-tuple-element.48), channel_id=1, source_target_pairs={{0,4},{1,5},{2,6},{3,7},{4,0},{5,1},{6,2},{7,3},{8,12},{9,13},{10,... | collective-permute-start | bytes 786440 | tf_op jit(solution)/shard_map/ppermute | solution.py:409
  166.8 18.0 %collective-permute-start.6 = (bf16[512,256]{1,0:T(8,128)(2,1)}, bf16[512,256]{1,0:T(8,128)(2,1)}, u32[]{:S(2)}, u32[]{:S(2)}) collective-permute-start(bf16[512,256]{1,0:T(8,128)(2,1)} %get-tuple-element.49), channel_id=1, source_target_pairs={{0,6},{1,7},{2,0},{3,1},{4,2},{5,3},{6,4},{7,5},{8,14},{9,15},{10,... | collective-permute-start | bytes 786440 | tf_op jit(solution)/shard_map/ppermute | solution.py:409
  176.0 13.5 %collective-permute-start.11 = (bf16[512,256]{1,0:T(8,128)(2,1)}, bf16[512,256]{1,0:T(8,128)(2,1)}, u32[]{:S(2)}, u32[]{:S(2)}) collective-permute-start(bf16[512,256]{1,0:T(8,128)(2,1)} %get-tuple-element.56), channel_id=1, source_target_pairs={{0,2},{1,3},{2,4},{3,5},{4,6},{5,7},{6,0},{7,1},{8,10},{9,11},{10,... | collective-permute-start | bytes 786440 | tf_op jit(solution)/shard_map/ppermute | solution.py:409
  178.1 17.0 %collective-permute-start.12 = (bf16[512,256]{1,0:T(8,128)(2,1)}, bf16[512,256]{1,0:T(8,128)(2,1)}, u32[]{:S(2)}, u32[]{:S(2)}) collective-permute-start(bf16[512,256]{1,0:T(8,128)(2,1)} %get-tuple-element.57), channel_id=1, source_target_pairs={{0,4},{1,5},{2,6},{3,7},{4,0},{5,1},{6,2},{7,3},{8,12},{9,13},{10,... | collective-permute-start | bytes 786440 | tf_op jit(solution)/shard_map/ppermute | solution.py:409
  181.2 13.9 %collective-permute-start.13 = (bf16[512,256]{1,0:T(8,128)(2,1)}, bf16[512,256]{1,0:T(8,128)(2,1)}, u32[]{:S(2)}, u32[]{:S(2)}) collective-permute-start(bf16[512,256]{1,0:T(8,128)(2,1)} %get-tuple-element.58), channel_id=1, source_target_pairs={{0,6},{1,7},{2,0},{3,1},{4,2},{5,3},{6,4},{7,5},{8,14},{9,15},{10,... | collective-permute-start | bytes 786440 | tf_op jit(solution)/shard_map/ppermute | solution.py:409
  200.6 62.5 %all-to-all-start.2 = ((bf16[32,16,8,256]{3,2,1,0:T(8,128)(2,1)}), bf16[32,16,8,256]{3,2,1,0:T(8,128)(2,1)}, u32[]{:S(2)}, u32[]{:S(2)}) async-start(bf16[32,16,8,256]{3,2,1,0:T(8,128)(2,1)} %get-tuple-element.63), calls=%async_computation.2 | async-start | bytes 4194304 | tf_op jit(solution)/shard_map/all_to_all | solution.py:395
  266.3 92.3 %all-to-all-start.3 = ((bf16[32,16,8,256]{3,2,1,0:T(8,128)(2,1)}), bf16[32,16,8,256]{3,2,1,0:T(8,128)(2,1)}, u32[]{:S(2)}, u32[]{:S(2)}) async-start(bf16[32,16,8,256]{3,2,1,0:T(8,128)(2,1)} %left_pass.3), calls=%async_computation.3 | async-start | bytes 4194304 | tf_op jit(solution)/shard_map/all_to_all | solution.py:395
  277.3 14.2 %collective-permute-start.26 = (bf16[512,256]{1,0:T(8,128)(2,1)}, bf16[512,256]{1,0:T(8,128)(2,1)}, u32[]{:S(2)}, u32[]{:S(2)}) collective-permute-start(bf16[512,256]{1,0:T(8,128)(2,1)} %get-tuple-element.74), channel_id=1, source_target_pairs={{0,4},{1,5},{2,6},{3,7},{4,0},{5,1},{6,2},{7,3},{8,12},{9,13},{10,... | collective-permute-start | bytes 786440 | tf_op jit(solution)/shard_map/ppermute | solution.py:409
  279.4 12.4 %collective-permute-start.27 = (bf16[512,256]{1,0:T(8,128)(2,1)}, bf16[512,256]{1,0:T(8,128)(2,1)}, u32[]{:S(2)}, u32[]{:S(2)}) collective-permute-start(bf16[512,256]{1,0:T(8,128)(2,1)} %get-tuple-element.75), channel_id=1, source_target_pairs={{0,6},{1,7},{2,0},{3,1},{4,2},{5,3},{6,4},{7,5},{8,14},{9,15},{10,... | collective-permute-start | bytes 786440 | tf_op jit(solution)/shard_map/ppermute | solution.py:409
  284.4 13.9 %collective-permute-start.15 = (bf16[512,256]{1,0:T(8,128)(2,1)}, bf16[512,256]{1,0:T(8,128)(2,1)}, u32[]{:S(2)}, u32[]{:S(2)}) collective-permute-start(bf16[512,256]{1,0:T(8,128)(2,1)} %get-tuple-element.65), channel_id=1, source_target_pairs={{0,2},{1,3},{2,4},{3,5},{4,6},{5,7},{6,0},{7,1},{8,10},{9,11},{10,... | collective-permute-start | bytes 786440 | tf_op jit(solution)/shard_map/ppermute | solution.py:409
  284.5 18.2 %collective-permute-start.16 = (bf16[512,256]{1,0:T(8,128)(2,1)}, bf16[512,256]{1,0:T(8,128)(2,1)}, u32[]{:S(2)}, u32[]{:S(2)}) collective-permute-start(bf16[512,256]{1,0:T(8,128)(2,1)} %get-tuple-element.66), channel_id=1, source_target_pairs={{0,4},{1,5},{2,6},{3,7},{4,0},{5,1},{6,2},{7,3},{8,12},{9,13},{10,... | collective-permute-start | bytes 786440 | tf_op jit(solution)/shard_map/ppermute | solution.py:409
  285.6 17.4 %collective-permute-start.17 = (bf16[512,256]{1,0:T(8,128)(2,1)}, bf16[512,256]{1,0:T(8,128)(2,1)}, u32[]{:S(2)}, u32[]{:S(2)}) collective-permute-start(bf16[512,256]{1,0:T(8,128)(2,1)} %get-tuple-element.67), channel_id=1, source_target_pairs={{0,6},{1,7},{2,0},{3,1},{4,2},{5,3},{6,4},{7,5},{8,14},{9,15},{10,... | collective-permute-start | bytes 786440 | tf_op jit(solution)/shard_map/ppermute | solution.py:409
  291.4 14.1 %collective-permute-start.14 = (bf16[256,512]{1,0:T(8,128)(2,1)}, bf16[256,512]{1,0:T(8,128)(2,1)}, u32[]{:S(2)}, u32[]{:S(2)}) collective-permute-start(bf16[256,512]{1,0:T(8,128)(2,1)} %b_ref.7), channel_id=1, source_target_pairs={{0,1},{1,0},{2,3},{3,2},{4,5},{5,4},{6,7},{7,6},{8,9},{9,8},{10,11... | collective-permute-start | bytes 786440 | tf_op jit(solution)/shard_map/ppermute | solution.py:405
  294.3 15.3 %collective-permute-start.28 = (bf16[512,256]{1,0:T(8,128)(2,1)}, bf16[512,256]{1,0:T(8,128)(2,1)}, u32[]{:S(2)}, u32[]{:S(2)}) collective-permute-start(bf16[512,256]{1,0:T(8,128)(2,1)} %get-tuple-element.77), channel_id=1, source_target_pairs={{0,2},{1,3},{2,4},{3,5},{4,6},{5,7},{6,0},{7,1},{8,10},{9,11},{10,... | collective-permute-start | bytes 786440 | tf_op jit(solution)/shard_map/ppermute | solution.py:409
  298.3 15.7 %collective-permute-start.29 = (bf16[512,256]{1,0:T(8,128)(2,1)}, bf16[512,256]{1,0:T(8,128)(2,1)}, u32[]{:S(2)}, u32[]{:S(2)}) collective-permute-start(bf16[512,256]{1,0:T(8,128)(2,1)} %get-tuple-element.78), channel_id=1, source_target_pairs={{0,4},{1,5},{2,6},{3,7},{4,0},{5,1},{6,2},{7,3},{8,12},{9,13},{10,... | collective-permute-start | bytes 786440 | tf_op jit(solution)/shard_map/ppermute | solution.py:409
  303.0 13.1 %collective-permute-start.31 = (bf16[512,256]{1,0:T(8,128)(2,1)}, bf16[512,256]{1,0:T(8,128)(2,1)}, u32[]{:S(2)}, u32[]{:S(2)}) collective-permute-start(bf16[512,256]{1,0:T(8,128)(2,1)} %get-tuple-element.76.refs_0_), channel_id=1, source_target_pairs={{0,1},{1,0},{2,3},{3,2},{4,5},{5,4},{6,7},{7,6},{8,9},{9,8},{10,11... | collective-permute-start | bytes 786440 | tf_op jit(solution)/shard_map/ppermute | solution.py:405
  305.6 15.3 %collective-permute-start.18 = (bf16[512,256]{1,0:T(8,128)(2,1)}, bf16[512,256]{1,0:T(8,128)(2,1)}, u32[]{:S(2)}, u32[]{:S(2)}) collective-permute-start(bf16[512,256]{1,0:T(8,128)(2,1)} %get-tuple-element.69), channel_id=1, source_target_pairs={{0,2},{1,3},{2,4},{3,5},{4,6},{5,7},{6,0},{7,1},{8,10},{9,11},{10,... | collective-permute-start | bytes 786440 | tf_op jit(solution)/shard_map/ppermute | solution.py:409
  309.6 15.6 %collective-permute-start.19 = (bf16[512,256]{1,0:T(8,128)(2,1)}, bf16[512,256]{1,0:T(8,128)(2,1)}, u32[]{:S(2)}, u32[]{:S(2)}) collective-permute-start(bf16[512,256]{1,0:T(8,128)(2,1)} %get-tuple-element.70), channel_id=1, source_target_pairs={{0,4},{1,5},{2,6},{3,7},{4,0},{5,1},{6,2},{7,3},{8,12},{9,13},{10,... | collective-permute-start | bytes 786440 | tf_op jit(solution)/shard_map/ppermute | solution.py:409
  314.1 12.6 %collective-permute-start.32 = (bf16[512,256]{1,0:T(8,128)(2,1)}, bf16[512,256]{1,0:T(8,128)(2,1)}, u32[]{:S(2)}, u32[]{:S(2)}) collective-permute-start(bf16[512,256]{1,0:T(8,128)(2,1)} %collective-permute-done.28.refs_1_), channel_id=1, source_target_pairs={{0,1},{1,0},{2,3},{3,2},{4,5},{5,4},{6,7},{7,6},{8,9},{9,8},{10,11... | collective-permute-start | bytes 786440 | tf_op jit(solution)/shard_map/ppermute | solution.py:405
  320.9 14.4 %collective-permute-start.34 = (bf16[512,256]{1,0:T(8,128)(2,1)}, bf16[512,256]{1,0:T(8,128)(2,1)}, u32[]{:S(2)}, u32[]{:S(2)}) collective-permute-start(bf16[512,256]{1,0:T(8,128)(2,1)} %collective-permute-done.30.refs_3_), channel_id=1, source_target_pairs={{0,1},{1,0},{2,3},{3,2},{4,5},{5,4},{6,7},{7,6},{8,9},{9,8},{10,11... | collective-permute-start | bytes 786440 | tf_op jit(solution)/shard_map/ppermute | solution.py:405
  325.2 14.1 %collective-permute-start.21 = (bf16[512,256]{1,0:T(8,128)(2,1)}, bf16[512,256]{1,0:T(8,128)(2,1)}, u32[]{:S(2)}, u32[]{:S(2)}) collective-permute-start(bf16[512,256]{1,0:T(8,128)(2,1)} %get-tuple-element.68.refs_0_), channel_id=1, source_target_pairs={{0,1},{1,0},{2,3},{3,2},{4,5},{5,4},{6,7},{7,6},{8,9},{9,8},{10,11... | collective-permute-start | bytes 786440 | tf_op jit(solution)/shard_map/ppermute | solution.py:405
  325.3 17.9 %collective-permute-start.22 = (bf16[512,256]{1,0:T(8,128)(2,1)}, bf16[512,256]{1,0:T(8,128)(2,1)}, u32[]{:S(2)}, u32[]{:S(2)}) collective-permute-start(bf16[512,256]{1,0:T(8,128)(2,1)} %collective-permute-done.18.refs_1_), channel_id=1, source_target_pairs={{0,1},{1,0},{2,3},{3,2},{4,5},{5,4},{6,7},{7,6},{8,9},{9,8},{10,11... | collective-permute-start | bytes 786440 | tf_op jit(solution)/shard_map/ppermute | solution.py:405
  326.7 22.2 %collective-permute-start.23 = (bf16[512,256]{1,0:T(8,128)(2,1)}, bf16[512,256]{1,0:T(8,128)(2,1)}, u32[]{:S(2)}, u32[]{:S(2)}) collective-permute-start(bf16[512,256]{1,0:T(8,128)(2,1)} %collective-permute-done.19.refs_2_), channel_id=1, source_target_pairs={{0,1},{1,0},{2,3},{3,2},{4,5},{5,4},{6,7},{7,6},{8,9},{9,8},{10,11... | collective-permute-start | bytes 786440 | tf_op jit(solution)/shard_map/ppermute | solution.py:405
  326.8 27.7 %collective-permute-start.24 = (bf16[512,256]{1,0:T(8,128)(2,1)}, bf16[512,256]{1,0:T(8,128)(2,1)}, u32[]{:S(2)}, u32[]{:S(2)}) collective-permute-start(bf16[512,256]{1,0:T(8,128)(2,1)} %collective-permute-done.20.refs_3_), channel_id=1, source_target_pairs={{0,1},{1,0},{2,3},{3,2},{4,5},{5,4},{6,7},{7,6},{8,9},{9,8},{10,11... | collective-permute-start | bytes 786440 | tf_op jit(solution)/shard_map/ppermute | solution.py:405
  (7 other events, 69.0 us)

commit v6 on v5

v6 whole, which is shorter than its diff:
```python
import functools

import jax
import jax.numpy as jnp
from jax import lax
from jax.experimental import pallas as pl
from jax.experimental.pallas import tpu as pltpu
from jax.sharding import PartitionSpec as P


F32 = jnp.float32
BF16 = jnp.bfloat16
NY = 4
CHUNKS = 2


def _params(mib=64):
    return pltpu.CompilerParams(vmem_limit_bytes=min(mib << 20, 67043328))


def _hbm(shape):
    return pltpu.HBM(shape, BF16)


def _cost(flops, nbytes):
    return pl.CostEstimate(flops=flops, bytes_accessed=nbytes, transcendentals=0)


def _fwd(s, d):
    return lax.rem(s[0] // 2 + d, NY)


def _back(s, d):
    return lax.rem(s[0] // 2 + NY - d, NY)


def _column(row, length):
    return jnp.transpose(jnp.broadcast_to(row, (128, length)))


def right_kernel(x_ref, r_ref, tw_ref, out_ref, first_ref, scr):
    outer, _, chan = x_ref.shape
    rows = r_ref.shape[0]
    part = x_ref.shape[1] // (NY * CHUNKS)
    for k in range(first_ref.shape[1] // part):
        at = pl.multiple_of(pl.program_id(0) * rows, rows) + k * part * CHUNKS
        first_ref[:, k * part : k * part + part, :] = x_ref[:, pl.ds(at, part), :]
    for a in range(outer):
        acc = jnp.dot(r_ref[...], x_ref[a], preferred_element_type=F32)
        col = _column(tw_ref[a : a + 1, :], rows)
        for c in range(chan // 128):
            scr[c, pl.ds(a, rows, stride=outer), :] = acc[:, c * 128 : c * 128 + 128] * col
    for c in range(chan // 128):
        out_ref[:, :, :, c * 128 : c * 128 + 128] = scr[c].reshape(*out_ref.shape[:3], 128).astype(BF16)


def right_pass(x3, right, twiddle, seq):
    outer, inner, chan = x3.shape
    steps = 2
    rows = inner // steps
    per = inner // seq
    return pl.pallas_call(
        right_kernel,
        name="right",
        grid=(steps,),
        in_specs=[
            pl.BlockSpec((outer, inner, chan), lambda g: (0, 0, 0)),
            pl.BlockSpec((rows, inner), lambda g: (g, 0)),
            pl.BlockSpec((outer, rows), lambda g: (0, g)),
        ],
        out_specs=[
            pl.BlockSpec((seq // steps, per, outer, chan), lambda g: (g, 0, 0, 0)),
            pl.BlockSpec((outer, rows // CHUNKS, chan), lambda g: (0, g, 0)),
        ],
        out_shape=[_hbm((seq, per, outer, chan)), _hbm((outer, inner // CHUNKS, chan))],
        scratch_shapes=[pltpu.VMEM((chan // 128, rows * outer, 128), F32)],
        compiler_params=_params(),
        cost_estimate=_cost(2 * outer * inner * inner * chan, 6 << 20),
    )(x3, right, twiddle)


def left_kernel(l_ref, in_ref, out_ref):
    seq, per, outer, chan = in_ref.shape
    for j in range(per):
        block = in_ref[:, j].astype(F32).reshape(seq * outer, chan).astype(BF16)
        acc = jnp.dot(l_ref[...], block, preferred_element_type=F32)
        out_ref[:, j] = acc.reshape(seq, outer, chan).astype(BF16)


def left_pass(left, wire):
    seq, per, outer, chan = wire.shape
    steps = 2
    full = seq * outer
    block = (seq, per // steps, outer, chan)
    return pl.pallas_call(
        left_kernel,
        name="left",
        grid=(steps,),
        in_specs=[
            pl.BlockSpec((full, full), lambda g: (0, 0)),
            pl.BlockSpec(block, lambda g: (0, g, 0, 0)),
        ],
        out_specs=pl.BlockSpec(block, lambda g: (0, g, 0, 0)),
        out_shape=_hbm(wire.shape),
        compiler_params=_params(),
        cost_estimate=_cost(2 * full * full * per * chan, 4 << 20),
    )(left, wire)


def turn_kernel(in_ref, out_ref):
    out_ref[...] = jnp.transpose(in_ref[...].astype(F32)).astype(BF16)


def turn_pass(matrix):
    return pl.pallas_call(
        turn_kernel,
        name="turn",
        out_shape=_hbm(matrix.shape),
        compiler_params=_params(),
        cost_estimate=_cost(0, 1 << 18),
    )(matrix)


def pick_kernel(x_ref, out_ref):
    out_ref[...] = x_ref[...]


def pick_pass(x3, u):
    outer, inner, chan = x3.shape
    rows = inner // (NY * CHUNKS)
    x5 = x3.reshape(outer, NY, CHUNKS * rows, chan)
    out = pl.pallas_call(
        pick_kernel,
        name="pick",
        grid=(1,),
        in_specs=[pl.BlockSpec((outer, NY, rows, chan), lambda g: (0, 0, u, 0))],
        out_specs=pl.BlockSpec((outer, NY, rows, chan), lambda g: (0, 0, 0, 0)),
        out_shape=_hbm((outer, NY, rows, chan)),
        compiler_params=_params(),
        cost_estimate=_cost(0, 2 << 20),
    )(x5)
    return out.reshape(outer, NY * rows, chan)


def middle_kernel(s, x_ref, xp_ref, b_ref, *outs):
    outer, _, rows, chan = x_ref.shape
    half = lax.rem(s[0], 2)
    own = b_ref[:, pl.ds(pl.multiple_of(half * chan, 128), chan)]
    other = b_ref[:, pl.ds(pl.multiple_of((1 - half) * chan, 128), chan)]
    dims = (((1,), (1,)), ((), ()))
    for d in range(NY):
        q = _fwd(s, d)
        x = x_ref[:, pl.ds(q, 1)].reshape(outer * rows, chan)
        xp = xp_ref[:, pl.ds(q, 1)].reshape(outer * rows, chan)
        acc = lax.dot_general(x, own, dims, preferred_element_type=F32)
        acc += lax.dot_general(xp, other, dims, preferred_element_type=F32)
        outs[d][...] = acc.astype(BF16)


def middle_pass(s, x3, xp3, blocks, u):
    outer, inner, chan = x3.shape
    rows = inner // (NY * CHUNKS)
    block = (outer, NY, rows, chan)
    out = (outer * rows, chan)
    return pl.pallas_call(
        middle_kernel,
        name="middle",
        grid_spec=pltpu.PrefetchScalarGridSpec(
            num_scalar_prefetch=1,
            grid=(1,),
            in_specs=[
                pl.BlockSpec(block, lambda g, s: (0, 0, u, 0)),
                pl.BlockSpec(block, lambda g, s: (0, 0, 0, 0)),
                pl.BlockSpec(blocks.shape, lambda g, s: (0, 0)),
            ],
            out_specs=[pl.BlockSpec(out, lambda g, s: (0, 0))] * NY,
        ),
        out_shape=[_hbm(out)] * NY,
        compiler_params=_params(),
        cost_estimate=_cost(4 * outer * rows * NY * chan * chan, 3 << 20),
    )(s, x3.reshape(outer, NY, CHUNKS * rows, chan), xp3.reshape(block), blocks)


def mix_kernel(flip, s, mix_ref, *refs):
    ins, outs = refs[:NY], refs[NY:]
    y = s[0] // 2
    rows = 64

    def rows_of(g, _):
        at = pl.ds(pl.multiple_of(g * rows, rows), rows)
        values = [r[at, :].astype(F32) for r in ins]
        for e in range(NY):
            to = lax.rem(y + e, NY)
            acc = None
            for d in range(NY):
                frm = lax.rem(y + NY - d, NY)
                row = mix_ref[frm, pl.ds(to, 1), :] if flip else mix_ref[to, pl.ds(frm, 1), :]
                term = values[d] * row
                acc = term if acc is None else acc + term
            outs[e][at, :] = acc.astype(BF16)
        return _

    lax.fori_loop(0, ins[0].shape[0] // rows, rows_of, 0)


def mix_pass(s, mixer, parts, flip):
    total, chan = parts[0].shape
    steps = 1
    block = pl.BlockSpec((total // steps, chan), lambda g, s: (g, 0))
    return pl.pallas_call(
        functools.partial(mix_kernel, flip),
        name="mix",
        grid_spec=pltpu.PrefetchScalarGridSpec(
            num_scalar_prefetch=1,
            grid=(steps,),
            in_specs=[pl.BlockSpec((NY, NY, chan), lambda g, s: (0, 0, lax.rem(s[0], 2)))] + [block] * NY,
            out_specs=[block] * NY,
        ),
        out_shape=[_hbm((total, chan))] * NY,
        compiler_params=_params(),
        cost_estimate=_cost(2 * NY * NY * total * chan, 2 << 20),
    )(s, mixer, *parts)


def gate_kernel(s, og_ref, *refs):
    pieces = refs[:NY]
    gate_ref, wire_ref, scr = refs[-3:]
    outer, _, rows, chan = og_ref.shape

    def one(a, _):
        for d in range(NY):
            q = _back(s, d)
            g = pieces[d][pl.ds(pl.multiple_of(a * rows, rows), rows), :]
            gate_ref[a, q] = g
            for c in range(chan // 128):
                cols = slice(c * 128, c * 128 + 128)
                og = og_ref[a, q, :, cols].astype(F32)
                scr[d * (chan // 128) + c, pl.ds(a, rows, stride=outer), :] = og * g[:, cols].astype(F32)
        return _

    lax.fori_loop(0, outer, one, 0)
    for d in range(NY):
        for c in range(chan // 128):
            value = scr[d * (chan // 128) + c].reshape(*wire_ref.shape[1:4], 128).astype(BF16)
            wire_ref[_back(s, d), :, :, :, c * 128 : c * 128 + 128] = value


def gate_pass(s, og3, pieces, seq, u, before):
    outer, inner, chan = og3.shape
    rows = inner // (NY * CHUNKS)
    per = inner // seq
    nat_shape = (outer, NY, CHUNKS * rows, chan)
    wire_shape = (NY, seq // NY, per, outer, chan)
    nat = pl.BlockSpec((outer, NY, rows, chan), lambda g, s: (0, 0, u, 0))
    whole = pl.BlockSpec(pieces[0].shape, lambda g, s: (0, 0))
    wire = pl.BlockSpec((NY, seq // NY // CHUNKS, per, outer, chan), lambda g, s: (0, u, 0, 0, 0))
    return pl.pallas_call(
        gate_kernel,
        name="gate",
        grid_spec=pltpu.PrefetchScalarGridSpec(
            num_scalar_prefetch=1,
            grid=(1,),
            in_specs=[nat] + [whole] * NY + [pl.BlockSpec(memory_space=pl.ANY)] * len(before),
            out_specs=[nat, wire],
            scratch_shapes=[pltpu.VMEM((NY * (chan // 128), rows * outer, 128), F32)],
        ),
        out_shape=[_hbm(nat_shape), _hbm(wire_shape)],
        input_output_aliases={2 + NY + i: i for i in range(len(before))},
        compiler_params=_params(),
        cost_estimate=_cost(outer * rows * NY * chan, 4 << 20),
    )(s, og3.reshape(nat_shape), *pieces, *before)


def cot_kernel(s, wire_ref, og_ref, *refs):
    pieces, scr = refs[:NY], refs[NY]
    outer, _, rows, chan = og_ref.shape
    for d in range(NY):
        for c in range(chan // 128):
            cols = slice(c * 128, c * 128 + 128)
            value = wire_ref[_fwd(s, d), :, :, :, cols].astype(F32)
            scr[d * (chan // 128) + c] = value.reshape(scr.shape[1:])

    def one(a, _):
        at = pl.ds(pl.multiple_of(a * rows, rows), rows)
        for d in range(NY):
            for c in range(chan // 128):
                cols = slice(c * 128, c * 128 + 128)
                m = scr[d * (chan // 128) + c, pl.ds(a, rows, stride=outer), :]
                pieces[d][at, cols] = (og_ref[a, _fwd(s, d), :, cols].astype(F32) * m).astype(BF16)
        return _

    lax.fori_loop(0, outer, one, 0)


def cot_pass(s, wire, og3, u):
    outer, inner, chan = og3.shape
    seq, per = wire.shape[:2]
    rows = inner // (NY * CHUNKS)
    piece = (outer * rows, chan)
    return pl.pallas_call(
        cot_kernel,
        name="cot",
        grid_spec=pltpu.PrefetchScalarGridSpec(
            num_scalar_prefetch=1,
            grid=(1,),
            in_specs=[
                pl.BlockSpec((NY, seq // NY // CHUNKS, per, outer, chan), lambda g, s: (0, u, 0, 0, 0)),
                pl.BlockSpec((outer, NY, rows, chan), lambda g, s: (0, 0, u, 0)),
            ],
            out_specs=[pl.BlockSpec(piece, lambda g, s: (0, 0))] * NY,
            scratch_shapes=[pltpu.VMEM((NY * (chan // 128), rows * outer, 128), F32)],
        ),
        out_shape=[_hbm(piece)] * NY,
        compiler_params=_params(),
        cost_estimate=_cost(outer * rows * NY * chan, 3 << 20),
    )(s, wire.reshape(NY, seq // NY, per, outer, chan), og3.reshape(outer, NY, CHUNKS * rows, chan))


def out_kernel(wire_ref, gate_ref, out_ref, scr):
    outer, rows, chan = out_ref.shape
    for c in range(chan // 128):
        scr[c] = wire_ref[:, :, :, c * 128 : c * 128 + 128].astype(F32).reshape(scr.shape[1:])
    for a in range(outer):
        for c in range(chan // 128):
            cols = slice(c * 128, c * 128 + 128)
            m = scr[c, pl.ds(a, rows, stride=outer), :]
            out_ref[a, :, cols] = (gate_ref[a, :, cols].astype(F32) * m).astype(BF16)


def out_pass(wire, gate3):
    outer, inner, chan = gate3.shape
    seq, per = wire.shape[:2]
    rows = inner // NY
    nat = pl.BlockSpec((outer, rows, chan), lambda d: (0, d, 0))
    return pl.pallas_call(
        out_kernel,
        name="out",
        grid=(NY,),
        in_specs=[pl.BlockSpec((seq // NY, per, outer, chan), lambda d: (d, 0, 0, 0)), nat],
        out_specs=nat,
        out_shape=_hbm(gate3.shape),
        scratch_shapes=[pltpu.VMEM((chan // 128, rows * outer, 128), F32)],
        compiler_params=_params(),
        cost_estimate=_cost(outer * inner * chan, 6 << 20),
    )(wire, gate3)


def chan_kernel(ds, s, b_ref, bo_ref, *refs):
    n = len(ds)
    own, other, out_ref = refs[:n], refs[n : 2 * n], refs[-1]
    chan = out_ref.shape[2]
    cols = pl.ds(pl.multiple_of(lax.rem(s[0], 2) * chan, 128), chan)
    for i in range(n):
        acc = jnp.dot(own[i][...], b_ref[:, cols], preferred_element_type=F32)
        acc += jnp.dot(other[i][...], bo_ref[:, cols], preferred_element_type=F32)
        out_ref[0 if n == 1 else _back(s, ds[i])] = acc.astype(BF16)


def chan_pass(s, blocks, blocks_other, own, other, ds, before):
    total, chan = own[0].shape
    whole = pl.BlockSpec(blocks.shape, lambda g, s: (0, 0))
    tile = pl.BlockSpec((total, chan), lambda g, s: (0, 0))
    if len(ds) == 1:
        out = pl.BlockSpec((1, total, chan), lambda g, s: (_back(s, ds[0]), 0, 0))
    else:
        out = pl.BlockSpec((NY, total, chan), lambda g, s: (0, 0, 0))
    n = 2 * len(ds)
    return pl.pallas_call(
        functools.partial(chan_kernel, ds),
        name="chan",
        grid_spec=pltpu.PrefetchScalarGridSpec(
            num_scalar_prefetch=1,
            grid=(1,),
            in_specs=[whole, whole] + [tile] * n + [pl.BlockSpec(memory_space=pl.ANY)] * len(before),
            out_specs=out,
        ),
        out_shape=_hbm((NY, total, chan)),
        input_output_aliases={3 + n: 0} if before else {},
        compiler_params=_params(),
        cost_estimate=_cost(2 * n * total * chan * chan, n << 19),
    )(s, blocks, blocks_other, *[own[d] for d in ds], *[other[d] for d in ds], *before)


def tail_kernel(group, wire_ref, rt_ref, tw_ref, *refs):
    parts, (out_ref, scr) = refs[:CHUNKS], refs[CHUNKS:]
    outer, inner = tw_ref.shape
    chan = out_ref.shape[2]
    rows = inner // NY // CHUNKS
    g = pl.program_id(0)

    @pl.when(g == 0)
    def _():
        for c in range(chan // 128):
            scr[c] = wire_ref[:, :, :, c * 128 : c * 128 + 128].astype(F32).reshape(scr.shape[1:])

    for k in range(group):
        a = g * group + k
        col = _column(tw_ref[pl.ds(a, 1), :], inner)
        grad = [(scr[c, pl.ds(a, inner, stride=outer), :] * col).astype(BF16) for c in range(chan // 128)]
        acc = jnp.dot(rt_ref[...], jnp.concatenate(grad, axis=1), preferred_element_type=F32)
        for q in range(NY):
            for u in range(CHUNKS):
                at = (q * CHUNKS + u) * rows
                part = parts[u][q, k * rows : k * rows + rows].astype(F32)
                out_ref[k, at : at + rows, :] = (acc[at : at + rows] + part).astype(BF16)


def tail_pass(wire, right_t, twiddle, parts):
    outer, inner = twiddle.shape
    chan = wire.shape[3]
    group = outer // 2
    part = pl.BlockSpec((NY, group * inner // NY // CHUNKS, chan), lambda g: (0, g, 0))
    return pl.pallas_call(
        functools.partial(tail_kernel, group),
        name="tail",
        grid=(outer // group,),
        in_specs=[
            pl.BlockSpec(wire.shape, lambda g: (0, 0, 0, 0)),
            pl.BlockSpec(right_t.shape, lambda g: (0, 0)),
            pl.BlockSpec(twiddle.shape, lambda g: (0, 0)),
        ]
        + [part] * CHUNKS,
        out_specs=pl.BlockSpec((group, inner, chan), lambda g: (g, 0, 0)),
        scratch_shapes=[pltpu.VMEM((chan // 128, outer * inner, 128), F32)],
        out_shape=jax.ShapeDtypeStruct((outer, inner, chan), BF16),
        compiler_params=_params(),
        cost_estimate=_cost(2 * outer * inner * inner * chan, 7 << 20),
    )(wire, right_t, twiddle, *parts)


def seq_swap(wire):
    return lax.all_to_all(wire, "seq", split_axis=0, concat_axis=0, tiled=True)


def body(inputs, twiddle, right_factor, left_factor, blocks, block_mixer, out_grad):
    outer, inner = twiddle.shape
    chan = inputs.shape[1]
    seq = left_factor.shape[0] // outer
    n = 2 * NY

    def to_pair(v):
        return lax.ppermute(v, "chan", [(c, c ^ 1) for c in range(n)])

    def around(parts):
        return [parts[0]] + [
            lax.ppermute(parts[d], "chan", [(c, (c + 2 * d) % n) for c in range(n)]) for d in range(1, NY)
        ]

    s = lax.axis_index("chan").reshape(1)
    x3 = inputs.reshape(outer, inner, chan)
    og3 = out_grad.reshape(outer, inner, chan)
    mixer = jnp.transpose(block_mixer, (1, 2, 0))

    twisted, first = right_pass(x3, right_factor, twiddle, seq)
    xp0 = to_pair(first)
    twisted = seq_swap(twisted)
    left_t = turn_pass(left_factor)
    later = pick_pass(x3, 1)
    xp1 = to_pair(later)
    middle0 = middle_pass(s, x3, xp0, blocks, 0)
    middle1 = middle_pass(s, x3, xp1, blocks, 1)
    mixed_wire = left_pass(left_factor, twisted)
    mixed = seq_swap(mixed_wire)
    blocks_other = to_pair(blocks)
    state = ()
    for u, middle in enumerate((middle0, middle1)):
        middle = around(middle)
        middle = mix_pass(s, mixer, middle, False)
        middle = around(middle)
        state = gate_pass(s, og3, middle, seq, u, state)
    gate3, grad_mixed = state[0].reshape(x3.shape), state[1].reshape(mixed_wire.shape)

    grad_mixed, mixed = lax.optimization_barrier((grad_mixed, mixed))
    grad_wire = seq_swap(grad_mixed)
    grads, others = [], []
    for u in range(CHUNKS):
        cots = cot_pass(s, mixed, og3, u)
        cots = around(cots)
        cots = mix_pass(s, mixer, cots, True)
        grads.append(around(cots))
        others.append([None] * NY)
        for d in (0, 1, 3, 2):
            others[u][d] = to_pair(grads[u][d])
    output = out_pass(mixed, gate3)
    grad_wire = left_pass(left_t, grad_wire)
    grad_twisted = seq_swap(grad_wire)
    part0 = chan_pass(s, blocks, blocks_other, grads[0], others[0], (0, 1, 3, 2), ())
    part1 = chan_pass(s, blocks, blocks_other, grads[1], others[1], (0, 1, 3), ())
    part1 = chan_pass(s, blocks, blocks_other, grads[1], others[1], (2,), (part1,))
    input_grad = tail_pass(grad_twisted, right_factor.T, twiddle, (part0, part1))
    return (output.reshape(inputs.shape), input_grad.reshape(inputs.shape))


def solution(mesh):
    return jax.shard_map(
        body,
        mesh=mesh,
        in_specs=(
            P("seq", "chan"),
            P("seq", None),
            P(),
            P(),
            P("chan", None),
            P(),
            P("seq", "chan"),
        ),
        out_specs=(P("seq", "chan"), P("seq", "chan")),
        check_vma=False,
    )
```

time: 368 us -> 358 us (0.973)
  waiting for transfers between devices: 170 us -> 159 us
    ppermute x24, waiting for transfers between devices: 40.9 us -> 31.9 us  [around(): lax.ppermute(parts[d], 'chan', [(c, (c + 2 * d) % n) for c in range(n)])]
    pallas_call x17 -> x20, Pallas kernels: 62.6 us -> 64.9 us  [the longest x4 11.3 us: mix_pass(): pl.pallas_call(functools.partial(mix_kernel, flip), name='mix', grid_spec...]
  transfers between devices with their start and end apart: 38 -> 38, of which waited for: 24 -> 23; matrix products, arithmetic and copies ran while one was open for 1% -> 1% of each run, Pallas kernels for 13% -> 14%
where the time goes in v6:
time: 358 us; the launch traced here: 354 us
  waiting for transfers between devices  159 us (44%)
  Pallas kernels  64.9 us (18%)
  starting transfers between devices  64.6 us (18%)
  blocking collectives  63.2 us (18%)
    ppermute x11, waiting for transfers between devices, to_pair(): return lax.ppermute(v, 'chan', [(c, c ^ 1) for c in range(n)])  78.7 us
    all_to_all x1, blocking collectives, seq_swap(): return lax.all_to_all(wire, 'seq', split_axis=0, concat_axis=0, tiled=True)  63.2 us
    all_to_all x3, waiting for transfers between devices, seq_swap(): return lax.all_to_all(wire, 'seq', split_axis=0, concat_axis=0, tiled=True)  48.4 us
    ppermute x24, starting transfers between devices, around(): lax.ppermute(parts[d], 'chan', [(c, (c + 2 * d) % n) for c in range(n)])  32.6 us
    ppermute x24, waiting for transfers between devices, around(): lax.ppermute(parts[d], 'chan', [(c, (c + 2 * d) % n) for c in range(n)])  31.9 us
    all_to_all x3, starting transfers between devices, seq_swap(): return lax.all_to_all(wire, 'seq', split_axis=0, concat_axis=0, tiled=True)  24 us
    pallas_call x4, Pallas kernels, mix_pass(): pl.pallas_call(functools.partial(mix_kernel, flip), name='mix', grid_spec...  11.3 us
    pallas_call x3, Pallas kernels, chan_pass(): pl.pallas_call(functools.partial(chan_kernel, ds), name='chan', grid_spec...  8.62 us
  transfers between devices with their start and end apart: 38, of which 23 were waited for; matrix products, arithmetic and copies ran while one was open for 1% of the time, Pallas kernels for 14%

profile of v6, /device:TPU:1, one launch (start us, length us, event | category | flops | bytes accessed | tf_op | source)
XLA Modules:
  0.0 354.4 jit_solution(12744482208110307909)
XLA Ops:
  0.6 4.8 %right.1 = (bf16[32,16,8,256]{3,2,1,0:T(8,128)(2,1)}, bf16[8,256,256]{2,1,0:T(8,128)(2,1)}) custom-call(bf16[8,512,256]{2,1,0:T(8,128)(2,1)} %bitcast.18, bf16[512,512]{1,0:T(8,128)(2,1)} %r_ref.1, f32[8,512]{1,0:T(8,128)} %tw_ref.3), custom_call_target="tpu_custom_call" | custom-call | flops 1073741824 | bytes 6291456 | tf_op jit(solution)/shard_map/right/pallas_call | solution.py:62
  5.4 63.2 %all_to_all.20.in_ref = bf16[32,16,8,256]{3,2,1,0:T(8,128)(2,1)} all-to-all(bf16[32,16,8,256]{3,2,1,0:T(8,128)(2,1)} %get-tuple-element.62), channel_id=1, replica_groups=mesh['seq'=32,'chan'=8] {'seq'}, dimensions={0} | all-to-all | bytes 4194304 | tf_op jit(solution)/shard_map/all_to_all | solution.py:432
  68.6 3.1 left.2
  71.7 5.9 %all-to-all-start.1 = ((bf16[32,16,8,256]{3,2,1,0:T(8,128)(2,1)}), bf16[32,16,8,256]{3,2,1,0:T(8,128)(2,1)}, u32[]{:S(2)}, u32[]{:S(2)}) async-start(bf16[32,16,8,256]{3,2,1,0:T(8,128)(2,1)} %left.2), calls=%async_computation.1 | async-start | bytes 4194304 | tf_op jit(solution)/shard_map/all_to_all | solution.py:432
  81.5 42.3 %collective-permute-done.7 = bf16[8,256,256]{2,1,0:T(8,128)(2,1)} collective-permute-done((bf16[8,256,256]{2,1,0:T(8,128)(2,1)}, bf16[8,256,256]{2,1,0:T(8,128)(2,1)}, u32[]{:S(2)}, u32[]{:S(2)}) %collective-permute-start.7) | collective-permute-done | bytes 1048608 | tf_op jit(solution)/shard_map/ppermute | solution.py:442
  123.8 3.1 middle.3
  131.3 15.0 %collective-permute-done = bf16[8,256,256]{2,1,0:T(8,128)(2,1)} collective-permute-done((bf16[8,256,256]{2,1,0:T(8,128)(2,1)}, bf16[8,256,256]{2,1,0:T(8,128)(2,1)}, u32[]{:S(2)}, u32[]{:S(2)}) %collective-permute-start) | collective-permute-done | bytes 1048608 | tf_op jit(solution)/shard_map/ppermute | solution.py:442
  146.3 3.1 middle.2
  159.9 4.8 %collective-permute-done.2.refs_2_ = bf16[512,256]{1,0:T(8,128)(2,1)} collective-permute-done((bf16[512,256]{1,0:T(8,128)(2,1)}, bf16[512,256]{1,0:T(8,128)(2,1)}, u32[]{:S(2)}, u32[]{:S(2)}) %collective-permute-start.2) | collective-permute-done | bytes 262176 | tf_op jit(solution)/shard_map/ppermute | solution.py:446
  165.3 2.9 mix.4
  168.9 4.3 %collective-permute-start.5 = (bf16[512,256]{1,0:T(8,128)(2,1)}, bf16[512,256]{1,0:T(8,128)(2,1)}, u32[]{:S(2)}, u32[]{:S(2)}) collective-permute-start(bf16[512,256]{1,0:T(8,128)(2,1)} %get-tuple-element.48), channel_id=1, source_target_pairs={{0,4},{1,5},{2,6},{3,7},{4,0},{5,1},{6,2},{7,3},{8,12},{9,13},{10,... | collective-permute-start | bytes 786440 | tf_op jit(solution)/shard_map/ppermute | solution.py:446
  176.5 3.6 %gate.2 = (bf16[8,4,128,256]{3,2,1,0:T(8,128)(2,1)}, bf16[4,8,16,8,256]{4,3,2,1,0:T(8,128)(2,1)}) custom-call(s32[1]{0:T(128)} %bitcast.s, bf16[8,4,128,256]{3,2,1,0:T(8,128)(2,1)} %bitcast.14, bf16[512,256]{1,0:T(8,128)(2,1)} %get-tuple-element.55.refs_0_, bf16[512,256]{1,0:T(8,128)(2,1)} %collective-permute-done.11.refs_1_, ...), custom_call_target="tpu_custom_call" | custom-call | flops 524288 | bytes 4194304 | tf_op jit(solution)/shard_map/gate/pallas_call | solution.py:257
  180.1 4.0 %collective-permute-done.4.refs_1_ = bf16[512,256]{1,0:T(8,128)(2,1)} collective-permute-done((bf16[512,256]{1,0:T(8,128)(2,1)}, bf16[512,256]{1,0:T(8,128)(2,1)}, u32[]{:S(2)}, u32[]{:S(2)}) %collective-permute-start.4) | collective-permute-done | bytes 262176 | tf_op jit(solution)/shard_map/ppermute | solution.py:446
  184.1 3.2 collective-permute-done.5.refs_2_
  187.3 3.6 %gate.3 = (bf16[8,4,128,256]{3,2,1,0:T(8,128)(2,1)}, bf16[4,8,16,8,256]{4,3,2,1,0:T(8,128)(2,1)}) custom-call(s32[1]{0:T(128)} %bitcast.s, bf16[8,4,128,256]{3,2,1,0:T(8,128)(2,1)} %bitcast.15, bf16[512,256]{1,0:T(8,128)(2,1)} %get-tuple-element.46.refs_0_, ...), custom_call_target="tpu_custom_call", output_to_operand_aliasing={{0}: (6, {}), {1}: (7, {})} | custom-call | flops 524288 | bytes 4194304 | tf_op jit(solution)/shard_map/gate/pallas_call | solution.py:257
  191.0 11.7 %all-to-all-start.2 = ((bf16[32,16,8,256]{3,2,1,0:T(8,128)(2,1)}), bf16[32,16,8,256]{3,2,1,0:T(8,128)(2,1)}, u32[]{:S(2)}, u32[]{:S(2)}) async-start(bf16[32,16,8,256]{3,2,1,0:T(8,128)(2,1)} %bitcast.23), calls=%async_computation.2 | async-start | bytes 4194304 | tf_op jit(solution)/shard_map/all_to_all | solution.py:432
  204.3 48.4 %all-to-all-done.2.in_ref = bf16[32,16,8,256]{3,2,1,0:T(8,128)(2,1)} async-done(((bf16[32,16,8,256]{3,2,1,0:T(8,128)(2,1)}), bf16[32,16,8,256]{3,2,1,0:T(8,128)(2,1)}, u32[]{:S(2)}, u32[]{:S(2)}) %all-to-all-start.2) | async-done | bytes 2097184 | tf_op jit(solution)/shard_map/all_to_all | solution.py:432
  252.8 3.1 left.3
  255.9 6.4 %all-to-all-start.3 = ((bf16[32,16,8,256]{3,2,1,0:T(8,128)(2,1)}), bf16[32,16,8,256]{3,2,1,0:T(8,128)(2,1)}, u32[]{:S(2)}, u32[]{:S(2)}) async-start(bf16[32,16,8,256]{3,2,1,0:T(8,128)(2,1)} %left.3), calls=%async_computation.3 | async-start | bytes 4194304 | tf_op jit(solution)/shard_map/all_to_all | solution.py:432
  262.3 3.3 cot.3
  270.0 3.4 cot.2
  276.1 4.5 %collective-permute-done.26.refs_2_ = bf16[512,256]{1,0:T(8,128)(2,1)} collective-permute-done((bf16[512,256]{1,0:T(8,128)(2,1)}, bf16[512,256]{1,0:T(8,128)(2,1)}, u32[]{:S(2)}, u32[]{:S(2)}) %collective-permute-start.26) | collective-permute-done | bytes 262176 | tf_op jit(solution)/shard_map/ppermute | solution.py:446
  287.8 4.1 %collective-permute-done.16.refs_2_ = bf16[512,256]{1,0:T(8,128)(2,1)} collective-permute-done((bf16[512,256]{1,0:T(8,128)(2,1)}, bf16[512,256]{1,0:T(8,128)(2,1)}, u32[]{:S(2)}, u32[]{:S(2)}) %collective-permute-start.16) | collective-permute-done | bytes 262176 | tf_op jit(solution)/shard_map/ppermute | solution.py:446
  300.7 4.6 %collective-permute-done.32.refs_3_ = bf16[512,256]{1,0:T(8,128)(2,1)} collective-permute-done((bf16[512,256]{1,0:T(8,128)(2,1)}, bf16[512,256]{1,0:T(8,128)(2,1)}, u32[]{:S(2)}, u32[]{:S(2)}) %collective-permute-start.32) | collective-permute-done | bytes 262176 | tf_op jit(solution)/shard_map/ppermute | solution.py:442
  310.3 3.6 %collective-permute-done.20.refs_3_ = bf16[512,256]{1,0:T(8,128)(2,1)} collective-permute-done((bf16[512,256]{1,0:T(8,128)(2,1)}, bf16[512,256]{1,0:T(8,128)(2,1)}, u32[]{:S(2)}, u32[]{:S(2)}) %collective-permute-start.20) | collective-permute-done | bytes 262176 | tf_op jit(solution)/shard_map/ppermute | solution.py:446
  321.7 4.7 %out.1 = bf16[8,512,256]{2,1,0:T(8,128)(2,1)} custom-call(bf16[32,16,8,256]{3,2,1,0:T(8,128)(2,1)} %all-to-all-done.1.wire_ref, bf16[8,512,256]{2,1,0:T(8,128)(2,1)} %bitcast.22), custom_call_target="tpu_custom_call" | custom-call | flops 1048576 | bytes 6291456 | tf_op jit(solution)/shard_map/out/pallas_call | solution.py:335
  326.4 3.1 chan.4.refs_2_
  331.7 3.0 collective-permute-done.22.refs_5_
  334.7 5.6 %collective-permute-done.23.refs_6_ = bf16[512,256]{1,0:T(8,128)(2,1)} collective-permute-done((bf16[512,256]{1,0:T(8,128)(2,1)}, bf16[512,256]{1,0:T(8,128)(2,1)}, u32[]{:S(2)}, u32[]{:S(2)}) %collective-permute-start.23) | collective-permute-done | bytes 262176 | tf_op jit(solution)/shard_map/ppermute | solution.py:442
  340.3 5.6 %collective-permute-done.24.refs_7_ = bf16[512,256]{1,0:T(8,128)(2,1)} collective-permute-done((bf16[512,256]{1,0:T(8,128)(2,1)}, bf16[512,256]{1,0:T(8,128)(2,1)}, u32[]{:S(2)}, u32[]{:S(2)}) %collective-permute-start.24) | collective-permute-done | bytes 262176 | tf_op jit(solution)/shard_map/ppermute | solution.py:442
  345.9 3.4 chan.3.refs_0_
  349.3 5.1 %tail.1 = bf16[8,512,256]{2,1,0:T(8,128)(2,1)} custom-call(bf16[32,16,8,256]{3,2,1,0:T(8,128)(2,1)} %all-to-all-done.3.wire_ref, bf16[512,512]{1,0:T(8,128)(2,1)} %bitcast.26, f32[8,512]{1,0:T(8,128)} %tw_ref.3, bf16[4,512,256]{2,1,0:T(8,128)(2,1)} %chan.3.refs_0_, bf16[4,512,256]{2,1,0:T(8,128)(2,1)} %chan.5.refs_1_), custom_call_target="tpu_custom_call" | custom-call | flops 1073741824 | bytes 7340032 | tf_op jit(solution)/shard_map/tail/pallas_call | solution.py:413
  (66 shorter events, 63.0 us)
Async XLA Ops:
  71.7 119.2 %all-to-all-start.1 = ((bf16[32,16,8,256]{3,2,1,0:T(8,128)(2,1)}), bf16[32,16,8,256]{3,2,1,0:T(8,128)(2,1)}, u32[]{:S(2)}, u32[]{:S(2)}) async-start(bf16[32,16,8,256]{3,2,1,0:T(8,128)(2,1)} %left.2), calls=%async_computation.1 | async-start | bytes 4194304 | tf_op jit(solution)/shard_map/all_to_all | solution.py:432
  77.6 46.2 %collective-permute-start.7 = (bf16[8,256,256]{2,1,0:T(8,128)(2,1)}, bf16[8,256,256]{2,1,0:T(8,128)(2,1)}, u32[]{:S(2)}, u32[]{:S(2)}) collective-permute-start(bf16[8,256,256]{2,1,0:T(8,128)(2,1)} %get-tuple-element.50), channel_id=1, source_target_pairs={{0,1},{1,0},{2,3},{3,2},{4,5},{5,4},{6,7},{7,6},{8,9},{9,8},{10,11... | collective-permute-start | bytes 3145736 | tf_op jit(solution)/shard_map/ppermute | solution.py:442
  80.3 65.9 %collective-permute-start = (bf16[8,256,256]{2,1,0:T(8,128)(2,1)}, bf16[8,256,256]{2,1,0:T(8,128)(2,1)}, u32[]{:S(2)}, u32[]{:S(2)}) collective-permute-start(bf16[8,256,256]{2,1,0:T(8,128)(2,1)} %bitcast.27), channel_id=1, source_target_pairs={{0,1},{1,0},{2,3},{3,2},{4,5},{5,4},{6,7},{7,6},{8,9},{9,8},{10,11... | collective-permute-start | bytes 3145736 | tf_op jit(solution)/shard_map/ppermute | solution.py:442
  126.9 26.4 %collective-permute-start.10 = (bf16[512,256]{1,0:T(8,128)(2,1)}, bf16[512,256]{1,0:T(8,128)(2,1)}, u32[]{:S(2)}, u32[]{:S(2)}) collective-permute-start(bf16[512,256]{1,0:T(8,128)(2,1)} %get-tuple-element.54), channel_id=1, source_target_pairs={{0,6},{1,7},{2,0},{3,1},{4,2},{5,3},{6,4},{7,5},{8,14},{9,15},{10,... | collective-permute-start | bytes 786440 | tf_op jit(solution)/shard_map/ppermute | solution.py:446
  129.6 24.7 %collective-permute-start.8 = (bf16[512,256]{1,0:T(8,128)(2,1)}, bf16[512,256]{1,0:T(8,128)(2,1)}, u32[]{:S(2)}, u32[]{:S(2)}) collective-permute-start(bf16[512,256]{1,0:T(8,128)(2,1)} %get-tuple-element.52), channel_id=1, source_target_pairs={{0,2},{1,3},{2,4},{3,5},{4,6},{5,7},{6,0},{7,1},{8,10},{9,11},{10,... | collective-permute-start | bytes 786440 | tf_op jit(solution)/shard_map/ppermute | solution.py:446
  129.7 24.7 %collective-permute-start.9 = (bf16[512,256]{1,0:T(8,128)(2,1)}, bf16[512,256]{1,0:T(8,128)(2,1)}, u32[]{:S(2)}, u32[]{:S(2)}) collective-permute-start(bf16[512,256]{1,0:T(8,128)(2,1)} %get-tuple-element.53), channel_id=1, source_target_pairs={{0,4},{1,5},{2,6},{3,7},{4,0},{5,1},{6,2},{7,3},{8,12},{9,13},{10,... | collective-permute-start | bytes 786440 | tf_op jit(solution)/shard_map/ppermute | solution.py:446
  150.7 14.1 %collective-permute-start.2 = (bf16[512,256]{1,0:T(8,128)(2,1)}, bf16[512,256]{1,0:T(8,128)(2,1)}, u32[]{:S(2)}, u32[]{:S(2)}) collective-permute-start(bf16[512,256]{1,0:T(8,128)(2,1)} %get-tuple-element.44), channel_id=1, source_target_pairs={{0,4},{1,5},{2,6},{3,7},{4,0},{5,1},{6,2},{7,3},{8,12},{9,13},{10,... | collective-permute-start | bytes 786440 | tf_op jit(solution)/shard_map/ppermute | solution.py:446
  153.3 12.0 %collective-permute-start.3 = (bf16[512,256]{1,0:T(8,128)(2,1)}, bf16[512,256]{1,0:T(8,128)(2,1)}, u32[]{:S(2)}, u32[]{:S(2)}) collective-permute-start(bf16[512,256]{1,0:T(8,128)(2,1)} %get-tuple-element.45), channel_id=1, source_target_pairs={{0,6},{1,7},{2,0},{3,1},{4,2},{5,3},{6,4},{7,5},{8,14},{9,15},{10,... | collective-permute-start | bytes 786440 | tf_op jit(solution)/shard_map/ppermute | solution.py:446
  157.2 16.1 %collective-permute-start.11 = (bf16[512,256]{1,0:T(8,128)(2,1)}, bf16[512,256]{1,0:T(8,128)(2,1)}, u32[]{:S(2)}, u32[]{:S(2)}) collective-permute-start(bf16[512,256]{1,0:T(8,128)(2,1)} %get-tuple-element.56), channel_id=1, source_target_pairs={{0,2},{1,3},{2,4},{3,5},{4,6},{5,7},{6,0},{7,1},{8,10},{9,11},{10,... | collective-permute-start | bytes 786440 | tf_op jit(solution)/shard_map/ppermute | solution.py:446
  157.5 18.5 %collective-permute-start.12 = (bf16[512,256]{1,0:T(8,128)(2,1)}, bf16[512,256]{1,0:T(8,128)(2,1)}, u32[]{:S(2)}, u32[]{:S(2)}) collective-permute-start(bf16[512,256]{1,0:T(8,128)(2,1)} %get-tuple-element.57), channel_id=1, source_target_pairs={{0,4},{1,5},{2,6},{3,7},{4,0},{5,1},{6,2},{7,3},{8,12},{9,13},{10,... | collective-permute-start | bytes 786440 | tf_op jit(solution)/shard_map/ppermute | solution.py:446
  158.4 18.1 %collective-permute-start.13 = (bf16[512,256]{1,0:T(8,128)(2,1)}, bf16[512,256]{1,0:T(8,128)(2,1)}, u32[]{:S(2)}, u32[]{:S(2)}) collective-permute-start(bf16[512,256]{1,0:T(8,128)(2,1)} %get-tuple-element.58), channel_id=1, source_target_pairs={{0,6},{1,7},{2,0},{3,1},{4,2},{5,3},{6,4},{7,5},{8,14},{9,15},{10,... | collective-permute-start | bytes 786440 | tf_op jit(solution)/shard_map/ppermute | solution.py:446
  168.2 15.9 %collective-permute-start.4 = (bf16[512,256]{1,0:T(8,128)(2,1)}, bf16[512,256]{1,0:T(8,128)(2,1)}, u32[]{:S(2)}, u32[]{:S(2)}) collective-permute-start(bf16[512,256]{1,0:T(8,128)(2,1)} %get-tuple-element.47), channel_id=1, source_target_pairs={{0,2},{1,3},{2,4},{3,5},{4,6},{5,7},{6,0},{7,1},{8,10},{9,11},{10,... | collective-permute-start | bytes 786440 | tf_op jit(solution)/shard_map/ppermute | solution.py:446
  168.9 18.4 %collective-permute-start.5 = (bf16[512,256]{1,0:T(8,128)(2,1)}, bf16[512,256]{1,0:T(8,128)(2,1)}, u32[]{:S(2)}, u32[]{:S(2)}) collective-permute-start(bf16[512,256]{1,0:T(8,128)(2,1)} %get-tuple-element.48), channel_id=1, source_target_pairs={{0,4},{1,5},{2,6},{3,7},{4,0},{5,1},{6,2},{7,3},{8,12},{9,13},{10,... | collective-permute-start | bytes 786440 | tf_op jit(solution)/shard_map/ppermute | solution.py:446
  173.2 14.1 %collective-permute-start.6 = (bf16[512,256]{1,0:T(8,128)(2,1)}, bf16[512,256]{1,0:T(8,128)(2,1)}, u32[]{:S(2)}, u32[]{:S(2)}) collective-permute-start(bf16[512,256]{1,0:T(8,128)(2,1)} %get-tuple-element.49), channel_id=1, source_target_pairs={{0,6},{1,7},{2,0},{3,1},{4,2},{5,3},{6,4},{7,5},{8,14},{9,15},{10,... | collective-permute-start | bytes 786440 | tf_op jit(solution)/shard_map/ppermute | solution.py:446
  191.0 61.8 %all-to-all-start.2 = ((bf16[32,16,8,256]{3,2,1,0:T(8,128)(2,1)}), bf16[32,16,8,256]{3,2,1,0:T(8,128)(2,1)}, u32[]{:S(2)}, u32[]{:S(2)}) async-start(bf16[32,16,8,256]{3,2,1,0:T(8,128)(2,1)} %bitcast.23), calls=%async_computation.2 | async-start | bytes 4194304 | tf_op jit(solution)/shard_map/all_to_all | solution.py:432
  255.9 93.5 %all-to-all-start.3 = ((bf16[32,16,8,256]{3,2,1,0:T(8,128)(2,1)}), bf16[32,16,8,256]{3,2,1,0:T(8,128)(2,1)}, u32[]{:S(2)}, u32[]{:S(2)}) async-start(bf16[32,16,8,256]{3,2,1,0:T(8,128)(2,1)} %left.3), calls=%async_computation.3 | async-start | bytes 4194304 | tf_op jit(solution)/shard_map/all_to_all | solution.py:432
  266.4 14.2 %collective-permute-start.26 = (bf16[512,256]{1,0:T(8,128)(2,1)}, bf16[512,256]{1,0:T(8,128)(2,1)}, u32[]{:S(2)}, u32[]{:S(2)}) collective-permute-start(bf16[512,256]{1,0:T(8,128)(2,1)} %get-tuple-element.76), channel_id=1, source_target_pairs={{0,4},{1,5},{2,6},{3,7},{4,0},{5,1},{6,2},{7,3},{8,12},{9,13},{10,... | collective-permute-start | bytes 786440 | tf_op jit(solution)/shard_map/ppermute | solution.py:446
  268.5 12.5 %collective-permute-start.27 = (bf16[512,256]{1,0:T(8,128)(2,1)}, bf16[512,256]{1,0:T(8,128)(2,1)}, u32[]{:S(2)}, u32[]{:S(2)}) collective-permute-start(bf16[512,256]{1,0:T(8,128)(2,1)} %get-tuple-element.77), channel_id=1, source_target_pairs={{0,6},{1,7},{2,0},{3,1},{4,2},{5,3},{6,4},{7,5},{8,14},{9,15},{10,... | collective-permute-start | bytes 786440 | tf_op jit(solution)/shard_map/ppermute | solution.py:446
  273.4 14.1 %collective-permute-start.15 = (bf16[512,256]{1,0:T(8,128)(2,1)}, bf16[512,256]{1,0:T(8,128)(2,1)}, u32[]{:S(2)}, u32[]{:S(2)}) collective-permute-start(bf16[512,256]{1,0:T(8,128)(2,1)} %get-tuple-element.67), channel_id=1, source_target_pairs={{0,2},{1,3},{2,4},{3,5},{4,6},{5,7},{6,0},{7,1},{8,10},{9,11},{10,... | collective-permute-start | bytes 786440 | tf_op jit(solution)/shard_map/ppermute | solution.py:446
  273.4 18.5 %collective-permute-start.16 = (bf16[512,256]{1,0:T(8,128)(2,1)}, bf16[512,256]{1,0:T(8,128)(2,1)}, u32[]{:S(2)}, u32[]{:S(2)}) collective-permute-start(bf16[512,256]{1,0:T(8,128)(2,1)} %get-tuple-element.68), channel_id=1, source_target_pairs={{0,4},{1,5},{2,6},{3,7},{4,0},{5,1},{6,2},{7,3},{8,12},{9,13},{10,... | collective-permute-start | bytes 786440 | tf_op jit(solution)/shard_map/ppermute | solution.py:446
  274.7 17.2 %collective-permute-start.17 = (bf16[512,256]{1,0:T(8,128)(2,1)}, bf16[512,256]{1,0:T(8,128)(2,1)}, u32[]{:S(2)}, u32[]{:S(2)}) collective-permute-start(bf16[512,256]{1,0:T(8,128)(2,1)} %get-tuple-element.69), channel_id=1, source_target_pairs={{0,6},{1,7},{2,0},{3,1},{4,2},{5,3},{6,4},{7,5},{8,14},{9,15},{10,... | collective-permute-start | bytes 786440 | tf_op jit(solution)/shard_map/ppermute | solution.py:446
  280.6 16.5 %collective-permute-start.14 = (bf16[256,512]{1,0:T(8,128)(2,1)}, bf16[256,512]{1,0:T(8,128)(2,1)}, u32[]{:S(2)}, u32[]{:S(2)}) collective-permute-start(bf16[256,512]{1,0:T(8,128)(2,1)} %b_ref.9), channel_id=1, source_target_pairs={{0,1},{1,0},{2,3},{3,2},{4,5},{5,4},{6,7},{7,6},{8,9},{9,8},{10,11... | collective-permute-start | bytes 786440 | tf_op jit(solution)/shard_map/ppermute | solution.py:442
  283.8 14.9 %collective-permute-start.30 = (bf16[512,256]{1,0:T(8,128)(2,1)}, bf16[512,256]{1,0:T(8,128)(2,1)}, u32[]{:S(2)}, u32[]{:S(2)}) collective-permute-start(bf16[512,256]{1,0:T(8,128)(2,1)} %get-tuple-element.80), channel_id=1, source_target_pairs={{0,2},{1,3},{2,4},{3,5},{4,6},{5,7},{6,0},{7,1},{8,10},{9,11},{10,... | collective-permute-start | bytes 786440 | tf_op jit(solution)/shard_map/ppermute | solution.py:446
  287.5 12.4 %collective-permute-start.31 = (bf16[512,256]{1,0:T(8,128)(2,1)}, bf16[512,256]{1,0:T(8,128)(2,1)}, u32[]{:S(2)}, u32[]{:S(2)}) collective-permute-start(bf16[512,256]{1,0:T(8,128)(2,1)} %get-tuple-element.81), channel_id=1, source_target_pairs={{0,6},{1,7},{2,0},{3,1},{4,2},{5,3},{6,4},{7,5},{8,14},{9,15},{10,... | collective-permute-start | bytes 786440 | tf_op jit(solution)/shard_map/ppermute | solution.py:446
  291.9 13.5 %collective-permute-start.32 = (bf16[512,256]{1,0:T(8,128)(2,1)}, bf16[512,256]{1,0:T(8,128)(2,1)}, u32[]{:S(2)}, u32[]{:S(2)}) collective-permute-start(bf16[512,256]{1,0:T(8,128)(2,1)} %get-tuple-element.79.refs_0_), channel_id=1, source_target_pairs={{0,1},{1,0},{2,3},{3,2},{4,5},{5,4},{6,7},{7,6},{8,9},{9,8},{10,11... | collective-permute-start | bytes 786440 | tf_op jit(solution)/shard_map/ppermute | solution.py:442
  292.0 15.1 %collective-permute-start.28 = (bf16[512,256]{1,0:T(8,128)(2,1)}, bf16[512,256]{1,0:T(8,128)(2,1)}, u32[]{:S(2)}, u32[]{:S(2)}) collective-permute-start(bf16[512,256]{1,0:T(8,128)(2,1)} %get-tuple-element.78), channel_id=1, source_target_pairs={{0,4},{1,5},{2,6},{3,7},{4,0},{5,1},{6,2},{7,3},{8,12},{9,13},{10,... | collective-permute-start | bytes 786440 | tf_op jit(solution)/shard_map/ppermute | solution.py:446
  299.8 14.1 %collective-permute-start.20 = (bf16[512,256]{1,0:T(8,128)(2,1)}, bf16[512,256]{1,0:T(8,128)(2,1)}, u32[]{:S(2)}, u32[]{:S(2)}) collective-permute-start(bf16[512,256]{1,0:T(8,128)(2,1)} %get-tuple-element.73), channel_id=1, source_target_pairs={{0,4},{1,5},{2,6},{3,7},{4,0},{5,1},{6,2},{7,3},{8,12},{9,13},{10,... | collective-permute-start | bytes 786440 | tf_op jit(solution)/shard_map/ppermute | solution.py:446
  308.9 20.6 %collective-permute-start.29 = (bf16[512,256]{1,0:T(8,128)(2,1)}, bf16[512,256]{1,0:T(8,128)(2,1)}, u32[]{:S(2)}, u32[]{:S(2)}) collective-permute-start(bf16[512,256]{1,0:T(8,128)(2,1)} %collective-permute-done.28.refs_0_), channel_id=1, source_target_pairs={{0,1},{1,0},{2,3},{3,2},{4,5},{5,4},{6,7},{7,6},{8,9},{9,8},{10,11... | collective-permute-start | bytes 786440 | tf_op jit(solution)/shard_map/ppermute | solution.py:442
  308.9 22.8 %collective-permute-start.21 = (bf16[512,256]{1,0:T(8,128)(2,1)}, bf16[512,256]{1,0:T(8,128)(2,1)}, u32[]{:S(2)}, u32[]{:S(2)}) collective-permute-start(bf16[512,256]{1,0:T(8,128)(2,1)} %get-tuple-element.70.refs_0_), channel_id=1, source_target_pairs={{0,1},{1,0},{2,3},{3,2},{4,5},{5,4},{6,7},{7,6},{8,9},{9,8},{10,11... | collective-permute-start | bytes 786440 | tf_op jit(solution)/shard_map/ppermute | solution.py:442
  313.9 20.8 %collective-permute-start.22 = (bf16[512,256]{1,0:T(8,128)(2,1)}, bf16[512,256]{1,0:T(8,128)(2,1)}, u32[]{:S(2)}, u32[]{:S(2)}) collective-permute-start(bf16[512,256]{1,0:T(8,128)(2,1)} %collective-permute-done.18.refs_1_), channel_id=1, source_target_pairs={{0,1},{1,0},{2,3},{3,2},{4,5},{5,4},{6,7},{7,6},{8,9},{9,8},{10,11... | collective-permute-start | bytes 786440 | tf_op jit(solution)/shard_map/ppermute | solution.py:442
  313.9 26.4 %collective-permute-start.23 = (bf16[512,256]{1,0:T(8,128)(2,1)}, bf16[512,256]{1,0:T(8,128)(2,1)}, u32[]{:S(2)}, u32[]{:S(2)}) collective-permute-start(bf16[512,256]{1,0:T(8,128)(2,1)} %collective-permute-done.19.refs_2_), channel_id=1, source_target_pairs={{0,1},{1,0},{2,3},{3,2},{4,5},{5,4},{6,7},{7,6},{8,9},{9,8},{10,11... | collective-permute-start | bytes 786440 | tf_op jit(solution)/shard_map/ppermute | solution.py:442
  317.9 28.1 %collective-permute-start.24 = (bf16[512,256]{1,0:T(8,128)(2,1)}, bf16[512,256]{1,0:T(8,128)(2,1)}, u32[]{:S(2)}, u32[]{:S(2)}) collective-permute-start(bf16[512,256]{1,0:T(8,128)(2,1)} %collective-permute-done.20.refs_3_), channel_id=1, source_target_pairs={{0,1},{1,0},{2,3},{3,2},{4,5},{5,4},{6,7},{7,6},{8,9},{9,8},{10,11... | collective-permute-start | bytes 786440 | tf_op jit(solution)/shard_map/ppermute | solution.py:442
  (6 other events, 59.2 us)

commit v7 on v6

--- a/solution.py
+++ b/solution.py
@@ -11,11 +11,16 @@
 F32 = jnp.float32
 BF16 = jnp.bfloat16
 NY = 4
+MIB = 24
 CHUNKS = 2
 
 
-def _params(mib=64):
+def _params(mib=MIB):
     return pltpu.CompilerParams(vmem_limit_bytes=min(mib << 20, 67043328))
+
+
+def in_hbm(v):
+    return pltpu.with_memory_space_constraint(v, pltpu.HBM)
 
 
 def _hbm(shape):
@@ -74,9 +79,9 @@
         ],
         out_shape=[_hbm((seq, per, outer, chan)), _hbm((outer, inner // CHUNKS, chan))],
         scratch_shapes=[pltpu.VMEM((chan // 128, rows * outer, 128), F32)],
-        compiler_params=_params(),
+        compiler_params=_params(24),
         cost_estimate=_cost(2 * outer * inner * inner * chan, 6 << 20),
-    )(x3, right, twiddle)
+    )(in_hbm(x3), in_hbm(right), in_hbm(twiddle))
 
 
 def left_kernel(l_ref, in_ref, out_ref):
@@ -138,7 +143,7 @@
         out_shape=_hbm((outer, NY, rows, chan)),
         compiler_params=_params(),
         cost_estimate=_cost(0, 2 << 20),
-    )(x5)
+    )(in_hbm(x5))
     return out.reshape(outer, NY * rows, chan)
 
 
@@ -178,7 +183,7 @@
         out_shape=[_hbm(out)] * NY,
         compiler_params=_params(),
         cost_estimate=_cost(4 * outer * rows * NY * chan * chan, 3 << 20),
-    )(s, x3.reshape(outer, NY, CHUNKS * rows, chan), xp3.reshape(block), blocks)
+    )(s, in_hbm(x3.reshape(outer, NY, CHUNKS * rows, chan)), xp3.reshape(block), in_hbm(blocks))
 
 
 def mix_kernel(flip, s, mix_ref, *refs):
@@ -219,7 +224,7 @@
         out_shape=[_hbm((total, chan))] * NY,
         compiler_params=_params(),
         cost_estimate=_cost(2 * NY * NY * total * chan, 2 << 20),
-    )(s, mixer, *parts)
+    )(s, in_hbm(mixer), *parts)
 
 
 def gate_kernel(s, og_ref, *refs):
@@ -268,7 +273,7 @@
         input_output_aliases={2 + NY + i: i for i in range(len(before))},
         compiler_params=_params(),
         cost_estimate=_cost(outer * rows * NY * chan, 4 << 20),
-    )(s, og3.reshape(nat_shape), *pieces, *before)
+    )(s, in_hbm(og3.reshape(nat_shape)), *pieces, *before)
 
 
 def cot_kernel(s, wire_ref, og_ref, *refs):
@@ -313,7 +318,7 @@
         out_shape=[_hbm(piece)] * NY,
         compiler_params=_params(),
         cost_estimate=_cost(outer * rows * NY * chan, 3 << 20),
-    )(s, wire.reshape(NY, seq // NY, per, outer, chan), og3.reshape(outer, NY, CHUNKS * rows, chan))
+    )(s, wire.reshape(NY, seq // NY, per, outer, chan), in_hbm(og3.reshape(outer, NY, CHUNKS * rows, chan)))
 
 
 def out_kernel(wire_ref, gate_ref, out_ref, scr):
@@ -342,7 +347,7 @@
         scratch_shapes=[pltpu.VMEM((chan // 128, rows * outer, 128), F32)],
         compiler_params=_params(),
         cost_estimate=_cost(outer * inner * chan, 6 << 20),
-    )(wire, gate3)
+    )(wire, in_hbm(gate3))
 
 
 def chan_kernel(ds, s, b_ref, bo_ref, *refs):
@@ -378,7 +383,7 @@
         input_output_aliases={3 + n: 0} if before else {},
         compiler_params=_params(),
         cost_estimate=_cost(2 * n * total * chan * chan, n << 19),
-    )(s, blocks, blocks_other, *[own[d] for d in ds], *[other[d] for d in ds], *before)
+    )(s, in_hbm(blocks), blocks_other, *[in_hbm(own[d]) for d in ds], *[other[d] for d in ds], *before)
 
 
 def tail_kernel(group, wire_ref, rt_ref, tw_ref, *refs):
@@ -423,9 +428,9 @@
         out_specs=pl.BlockSpec((group, inner, chan), lambda g: (g, 0, 0)),
         scratch_shapes=[pltpu.VMEM((chan // 128, outer * inner, 128), F32)],
         out_shape=jax.ShapeDtypeStruct((outer, inner, chan), BF16),
-        compiler_params=_params(),
+        compiler_params=_params(24),
         cost_estimate=_cost(2 * outer * inner * inner * chan, 7 << 20),
-    )(wire, right_t, twiddle, *parts)
+    )(wire, right_t, in_hbm(twiddle), *[in_hbm(p) for p in parts])
 
 
 def seq_swap(wire):
@@ -442,7 +447,7 @@
         return lax.ppermute(v, "chan", [(c, c ^ 1) for c in range(n)])
 
     def around(parts):
-        return [parts[0]] + [
+        return [in_hbm(parts[0])] + [
             lax.ppermute(parts[d], "chan", [(c, (c + 2 * d) % n) for c in range(n)]) for d in range(1, NY)
         ]
 
@@ -455,6 +460,7 @@
     xp0 = to_pair(first)
     twisted = seq_swap(twisted)
     left_t = turn_pass(left_factor)
+    right_t = turn_pass(right_factor)
     later = pick_pass(x3, 1)
     xp1 = to_pair(later)
     middle0 = middle_pass(s, x3, xp0, blocks, 0)
@@ -487,7 +493,7 @@
     part0 = chan_pass(s, blocks, blocks_other, grads[0], others[0], (0, 1, 3, 2), ())
     part1 = chan_pass(s, blocks, blocks_other, grads[1], others[1], (0, 1, 3), ())
     part1 = chan_pass(s, blocks, blocks_other, grads[1], others[1], (2,), (part1,))
-    input_grad = tail_pass(grad_twisted, right_factor.T, twiddle, (part0, part1))
+    input_grad = tail_pass(grad_twisted, right_t, twiddle, (part0, part1))
     return (output.reshape(inputs.shape), input_grad.reshape(inputs.shape))
 
 

time: 358 us -> 356 us (level)
  waiting for transfers between devices: 159 us -> 164 us
  Pallas kernels: 64.9 us -> 60.6 us
  transfers between devices with their start and end apart: 38 -> 38, of which waited for: 23 -> 23; matrix products, arithmetic and copies ran while one was open for 1% -> 0% of each run, Pallas kernels for 14% -> 13%
where the time goes in v7:
time: 356 us; the launch traced here: 353 us
  waiting for transfers between devices  164 us (46%)
  starting transfers between devices  63.6 us (18%)
  blocking collectives  63.2 us (18%)
  Pallas kernels  60.6 us (17%)
    ppermute x11, waiting for transfers between devices, to_pair(): return lax.ppermute(v, 'chan', [(c, c ^ 1) for c in range(n)])  80.7 us
    all_to_all x1, blocking collectives, seq_swap(): return lax.all_to_all(wire, 'seq', split_axis=0, concat_axis=0, tiled=True)  63.2 us
    all_to_all x3, waiting for transfers between devices, seq_swap(): return lax.all_to_all(wire, 'seq', split_axis=0, concat_axis=0, tiled=True)  49.3 us
    ppermute x24, waiting for transfers between devices, around(): lax.ppermute(parts[d], 'chan', [(c, (c + 2 * d) % n) for c in range(n)])  33.5 us
    ppermute x24, starting transfers between devices, around(): lax.ppermute(parts[d], 'chan', [(c, (c + 2 * d) % n) for c in range(n)])  31.8 us
    all_to_all x3, starting transfers between devices, seq_swap(): return lax.all_to_all(wire, 'seq', split_axis=0, concat_axis=0, tiled=True)  23.8 us
    pallas_call x4, Pallas kernels, mix_pass(): pl.pallas_call(functools.partial(mix_kernel, flip), name='mix', grid_spec...  10.4 us
    ppermute x11, starting transfers between devices, to_pair(): return lax.ppermute(v, 'chan', [(c, c ^ 1) for c in range(n)])  7.91 us
  transfers between devices with their start and end apart: 38, of which 23 were waited for; matrix products, arithmetic and copies ran while one was open for 0% of the time, Pallas kernels for 13%

profile of v7, /device:TPU:1, one launch (start us, length us, event | category | flops | bytes accessed | tf_op | source)
XLA Modules:
  0.0 352.7 jit_solution(2590310017002837677)
XLA Ops:
  0.6 4.8 %right.1 = (bf16[32,16,8,256]{3,2,1,0:T(8,128)(2,1)}, bf16[8,256,256]{2,1,0:T(8,128)(2,1)}) custom-call(bf16[8,512,256]{2,1,0:T(8,128)(2,1)} %bitcast.20, bf16[512,512]{1,0:T(8,128)(2,1)} %in_ref.3, f32[8,512]{1,0:T(8,128)} %tw_ref.3), custom_call_target="tpu_custom_call" | custom-call | flops 1073741824 | bytes 6291456 | tf_op jit(solution)/shard_map/right/pallas_call | solution.py:67
  5.4 63.2 %all_to_all.20.in_ref = bf16[32,16,8,256]{3,2,1,0:T(8,128)(2,1)S(1)} all-to-all(bf16[32,16,8,256]{3,2,1,0:T(8,128)(2,1)} %get-tuple-element.62), channel_id=1, replica_groups=mesh['seq'=32,'chan'=8] {'seq'}, dimensions={0} | all-to-all | bytes 4194304 | tf_op jit(solution)/shard_map/all_to_all | solution.py:437
  70.7 5.8 %all-to-all-start.1 = ((bf16[32,16,8,256]{3,2,1,0:T(8,128)(2,1)}), bf16[32,16,8,256]{3,2,1,0:T(8,128)(2,1)S(1)}, u32[]{:S(2)}, u32[]{:S(2)}) async-start(bf16[32,16,8,256]{3,2,1,0:T(8,128)(2,1)} %left.2), calls=%async_computation.1 | async-start | bytes 4194304 | tf_op jit(solution)/shard_map/all_to_all | solution.py:437
  80.4 42.4 %collective-permute-done.7 = bf16[8,256,256]{2,1,0:T(8,128)(2,1)} collective-permute-done((bf16[8,256,256]{2,1,0:T(8,128)(2,1)}, bf16[8,256,256]{2,1,0:T(8,128)(2,1)}, u32[]{:S(2)}, u32[]{:S(2)}) %collective-permute-start.7) | collective-permute-done | bytes 1048608 | tf_op jit(solution)/shard_map/ppermute | solution.py:447
  122.8 3.1 middle.3
  125.9 2.7 collective-permute-start.10
  130.3 14.8 %collective-permute-done = bf16[8,256,256]{2,1,0:T(8,128)(2,1)S(1)} collective-permute-done((bf16[8,256,256]{2,1,0:T(8,128)(2,1)}, bf16[8,256,256]{2,1,0:T(8,128)(2,1)S(1)}, u32[]{:S(2)}, u32[]{:S(2)}) %collective-permute-start) | collective-permute-done | bytes 1048608 | tf_op jit(solution)/shard_map/ppermute | solution.py:447
  145.2 2.8 middle.2
  158.4 5.0 %collective-permute-done.2.refs_2_ = bf16[512,256]{1,0:T(8,128)(2,1)S(1)} collective-permute-done((bf16[512,256]{1,0:T(8,128)(2,1)}, bf16[512,256]{1,0:T(8,128)(2,1)S(1)}, u32[]{:S(2)}, u32[]{:S(2)}) %collective-permute-start.2) | collective-permute-done | bytes 262176 | tf_op jit(solution)/shard_map/ppermute | solution.py:451
  167.2 4.2 %collective-permute-start.5 = (bf16[512,256]{1,0:T(8,128)(2,1)}, bf16[512,256]{1,0:T(8,128)(2,1)S(1)}, u32[]{:S(2)}, u32[]{:S(2)}) collective-permute-start(bf16[512,256]{1,0:T(8,128)(2,1)} %get-tuple-element.48), channel_id=1, source_target_pairs={{0,4},{1,5},{2,6},{3,7},{4,0},{5,1},{6,2},{7,3},{8,12},{9,13},{10,... | collective-permute-start | bytes 786440 | tf_op jit(solution)/shard_map/ppermute | solution.py:451
  171.4 3.2 collective-permute-done.12.refs_2_
  175.0 3.4 gate.2
  178.4 4.1 %collective-permute-done.4.refs_1_ = bf16[512,256]{1,0:T(8,128)(2,1)S(1)} collective-permute-done((bf16[512,256]{1,0:T(8,128)(2,1)}, bf16[512,256]{1,0:T(8,128)(2,1)S(1)}, u32[]{:S(2)}, u32[]{:S(2)}) %collective-permute-start.4) | collective-permute-done | bytes 262176 | tf_op jit(solution)/shard_map/ppermute | solution.py:451
  182.5 3.4 collective-permute-done.5.refs_2_
  185.9 3.4 gate.3
  189.3 11.6 %all-to-all-start.2 = ((bf16[32,16,8,256]{3,2,1,0:T(8,128)(2,1)}), bf16[32,16,8,256]{3,2,1,0:T(8,128)(2,1)}, u32[]{:S(2)}, u32[]{:S(2)}) async-start(bf16[32,16,8,256]{3,2,1,0:T(8,128)(2,1)} %bitcast.25), calls=%async_computation.2 | async-start | bytes 4194304 | tf_op jit(solution)/shard_map/all_to_all | solution.py:437
  201.6 49.3 %all-to-all-done.2.in_ref = bf16[32,16,8,256]{3,2,1,0:T(8,128)(2,1)} async-done(((bf16[32,16,8,256]{3,2,1,0:T(8,128)(2,1)}), bf16[32,16,8,256]{3,2,1,0:T(8,128)(2,1)}, u32[]{:S(2)}, u32[]{:S(2)}) %all-to-all-start.2) | async-done | bytes 2097184 | tf_op jit(solution)/shard_map/all_to_all | solution.py:437
  251.9 3.1 left.3
  255.0 6.4 %all-to-all-start.3 = ((bf16[32,16,8,256]{3,2,1,0:T(8,128)(2,1)}), bf16[32,16,8,256]{3,2,1,0:T(8,128)(2,1)}, u32[]{:S(2)}, u32[]{:S(2)}) async-start(bf16[32,16,8,256]{3,2,1,0:T(8,128)(2,1)} %left.3), calls=%async_computation.3 | async-start | bytes 4194304 | tf_op jit(solution)/shard_map/all_to_all | solution.py:437
  261.4 3.1 cot.3
  268.9 3.1 cot.2
  274.8 4.7 %collective-permute-done.26.refs_2_ = bf16[512,256]{1,0:T(8,128)(2,1)S(1)} collective-permute-done((bf16[512,256]{1,0:T(8,128)(2,1)}, bf16[512,256]{1,0:T(8,128)(2,1)S(1)}, u32[]{:S(2)}, u32[]{:S(2)}) %collective-permute-start.26) | collective-permute-done | bytes 262176 | tf_op jit(solution)/shard_map/ppermute | solution.py:451
  286.5 4.3 %collective-permute-done.16.refs_2_ = bf16[512,256]{1,0:T(8,128)(2,1)S(1)} collective-permute-done((bf16[512,256]{1,0:T(8,128)(2,1)}, bf16[512,256]{1,0:T(8,128)(2,1)S(1)}, u32[]{:S(2)}, u32[]{:S(2)}) %collective-permute-start.16) | collective-permute-done | bytes 262176 | tf_op jit(solution)/shard_map/ppermute | solution.py:451
  299.4 5.1 %collective-permute-done.32.refs_3_ = bf16[512,256]{1,0:T(8,128)(2,1)S(1)} collective-permute-done((bf16[512,256]{1,0:T(8,128)(2,1)}, bf16[512,256]{1,0:T(8,128)(2,1)S(1)}, u32[]{:S(2)}, u32[]{:S(2)}) %collective-permute-start.32) | collective-permute-done | bytes 262176 | tf_op jit(solution)/shard_map/ppermute | solution.py:447
  309.5 3.3 collective-permute-done.20.refs_3_
  319.4 4.4 %out.1 = bf16[8,512,256]{2,1,0:T(8,128)(2,1)} custom-call(bf16[32,16,8,256]{3,2,1,0:T(8,128)(2,1)S(1)} %all-to-all-done.1.wire_ref, bf16[8,512,256]{2,1,0:T(8,128)(2,1)} %bitcast.24), custom_call_target="tpu_custom_call" | custom-call | flops 1048576 | bytes 6291456 | tf_op jit(solution)/shard_map/out/pallas_call | solution.py:340
  323.9 2.8 chan.4.refs_2_
  328.7 4.7 %collective-permute-done.22.refs_5_ = bf16[512,256]{1,0:T(8,128)(2,1)S(1)} collective-permute-done((bf16[512,256]{1,0:T(8,128)(2,1)S(1)}, bf16[512,256]{1,0:T(8,128)(2,1)S(1)}, u32[]{:S(2)}, u32[]{:S(2)}) %collective-permute-start.22) | collective-permute-done | bytes 262176 | tf_op jit(solution)/shard_map/ppermute | solution.py:447
  333.5 5.6 %collective-permute-done.23.refs_6_ = bf16[512,256]{1,0:T(8,128)(2,1)S(1)} collective-permute-done((bf16[512,256]{1,0:T(8,128)(2,1)S(1)}, bf16[512,256]{1,0:T(8,128)(2,1)S(1)}, u32[]{:S(2)}, u32[]{:S(2)}) %collective-permute-start.23) | collective-permute-done | bytes 262176 | tf_op jit(solution)/shard_map/ppermute | solution.py:447
  339.1 5.6 %collective-permute-done.24.refs_7_ = bf16[512,256]{1,0:T(8,128)(2,1)S(1)} collective-permute-done((bf16[512,256]{1,0:T(8,128)(2,1)S(1)}, bf16[512,256]{1,0:T(8,128)(2,1)S(1)}, u32[]{:S(2)}, u32[]{:S(2)}) %collective-permute-start.24) | collective-permute-done | bytes 262176 | tf_op jit(solution)/shard_map/ppermute | solution.py:447
  344.7 3.0 chan.3.refs_0_
  347.8 4.9 %tail.1 = bf16[8,512,256]{2,1,0:T(8,128)(2,1)} custom-call(bf16[32,16,8,256]{3,2,1,0:T(8,128)(2,1)} %all-to-all-done.3.wire_ref, bf16[512,512]{1,0:T(8,128)(2,1)S(1)} %copy-done, f32[8,512]{1,0:T(8,128)} %tw_ref.3, bf16[4,512,256]{2,1,0:T(8,128)(2,1)} %chan.3.refs_0_, bf16[4,512,256]{2,1,0:T(8,128)(2,1)} %chan.5.refs_1_), custom_call_target="tpu_custom_call" | custom-call | flops 1073741824 | bytes 7340032 | tf_op jit(solution)/shard_map/tail/pallas_call | solution.py:418
  (92 shorter events, 60.2 us)
Async XLA Ops:
  70.7 118.6 %all-to-all-start.1 = ((bf16[32,16,8,256]{3,2,1,0:T(8,128)(2,1)}), bf16[32,16,8,256]{3,2,1,0:T(8,128)(2,1)S(1)}, u32[]{:S(2)}, u32[]{:S(2)}) async-start(bf16[32,16,8,256]{3,2,1,0:T(8,128)(2,1)} %left.2), calls=%async_computation.1 | async-start | bytes 4194304 | tf_op jit(solution)/shard_map/all_to_all | solution.py:437
  76.5 46.3 %collective-permute-start.7 = (bf16[8,256,256]{2,1,0:T(8,128)(2,1)}, bf16[8,256,256]{2,1,0:T(8,128)(2,1)}, u32[]{:S(2)}, u32[]{:S(2)}) collective-permute-start(bf16[8,256,256]{2,1,0:T(8,128)(2,1)} %get-tuple-element.50), channel_id=1, source_target_pairs={{0,1},{1,0},{2,3},{3,2},{4,5},{5,4},{6,7},{7,6},{8,9},{9,8},{10,11... | collective-permute-start | bytes 3145736 | tf_op jit(solution)/shard_map/ppermute | solution.py:447
  79.3 65.9 %collective-permute-start = (bf16[8,256,256]{2,1,0:T(8,128)(2,1)}, bf16[8,256,256]{2,1,0:T(8,128)(2,1)S(1)}, u32[]{:S(2)}, u32[]{:S(2)}) collective-permute-start(bf16[8,256,256]{2,1,0:T(8,128)(2,1)} %bitcast.28), channel_id=1, source_target_pairs={{0,1},{1,0},{2,3},{3,2},{4,5},{5,4},{6,7},{7,6},{8,9},{9,8},{10,11... | collective-permute-start | bytes 3145736 | tf_op jit(solution)/shard_map/ppermute | solution.py:447
  125.9 26.0 %collective-permute-start.10 = (bf16[512,256]{1,0:T(8,128)(2,1)}, bf16[512,256]{1,0:T(8,128)(2,1)S(1)}, u32[]{:S(2)}, u32[]{:S(2)}) collective-permute-start(bf16[512,256]{1,0:T(8,128)(2,1)} %get-tuple-element.54), channel_id=1, source_target_pairs={{0,6},{1,7},{2,0},{3,1},{4,2},{5,3},{6,4},{7,5},{8,14},{9,15},{10,... | collective-permute-start | bytes 786440 | tf_op jit(solution)/shard_map/ppermute | solution.py:451
  128.7 24.3 %collective-permute-start.8 = (bf16[512,256]{1,0:T(8,128)(2,1)}, bf16[512,256]{1,0:T(8,128)(2,1)S(1)}, u32[]{:S(2)}, u32[]{:S(2)}) collective-permute-start(bf16[512,256]{1,0:T(8,128)(2,1)} %get-tuple-element.52), channel_id=1, source_target_pairs={{0,2},{1,3},{2,4},{3,5},{4,6},{5,7},{6,0},{7,1},{8,10},{9,11},{10,... | collective-permute-start | bytes 786440 | tf_op jit(solution)/shard_map/ppermute | solution.py:451
  128.7 24.3 %collective-permute-start.9 = (bf16[512,256]{1,0:T(8,128)(2,1)}, bf16[512,256]{1,0:T(8,128)(2,1)S(1)}, u32[]{:S(2)}, u32[]{:S(2)}) collective-permute-start(bf16[512,256]{1,0:T(8,128)(2,1)} %get-tuple-element.53), channel_id=1, source_target_pairs={{0,4},{1,5},{2,6},{3,7},{4,0},{5,1},{6,2},{7,3},{8,12},{9,13},{10,... | collective-permute-start | bytes 786440 | tf_op jit(solution)/shard_map/ppermute | solution.py:451
  149.3 14.1 %collective-permute-start.2 = (bf16[512,256]{1,0:T(8,128)(2,1)}, bf16[512,256]{1,0:T(8,128)(2,1)S(1)}, u32[]{:S(2)}, u32[]{:S(2)}) collective-permute-start(bf16[512,256]{1,0:T(8,128)(2,1)} %get-tuple-element.44), channel_id=1, source_target_pairs={{0,4},{1,5},{2,6},{3,7},{4,0},{5,1},{6,2},{7,3},{8,12},{9,13},{10,... | collective-permute-start | bytes 786440 | tf_op jit(solution)/shard_map/ppermute | solution.py:451
  155.6 15.8 %collective-permute-start.11 = (bf16[512,256]{1,0:T(8,128)(2,1)}, bf16[512,256]{1,0:T(8,128)(2,1)S(1)}, u32[]{:S(2)}, u32[]{:S(2)}) collective-permute-start(bf16[512,256]{1,0:T(8,128)(2,1)} %get-tuple-element.56), channel_id=1, source_target_pairs={{0,2},{1,3},{2,4},{3,5},{4,6},{5,7},{6,0},{7,1},{8,10},{9,11},{10,... | collective-permute-start | bytes 786440 | tf_op jit(solution)/shard_map/ppermute | solution.py:451
  156.0 18.6 %collective-permute-start.12 = (bf16[512,256]{1,0:T(8,128)(2,1)}, bf16[512,256]{1,0:T(8,128)(2,1)S(1)}, u32[]{:S(2)}, u32[]{:S(2)}) collective-permute-start(bf16[512,256]{1,0:T(8,128)(2,1)} %get-tuple-element.57), channel_id=1, source_target_pairs={{0,4},{1,5},{2,6},{3,7},{4,0},{5,1},{6,2},{7,3},{8,12},{9,13},{10,... | collective-permute-start | bytes 786440 | tf_op jit(solution)/shard_map/ppermute | solution.py:451
  156.8 18.2 %collective-permute-start.13 = (bf16[512,256]{1,0:T(8,128)(2,1)}, bf16[512,256]{1,0:T(8,128)(2,1)S(1)}, u32[]{:S(2)}, u32[]{:S(2)}) collective-permute-start(bf16[512,256]{1,0:T(8,128)(2,1)} %get-tuple-element.58), channel_id=1, source_target_pairs={{0,6},{1,7},{2,0},{3,1},{4,2},{5,3},{6,4},{7,5},{8,14},{9,15},{10,... | collective-permute-start | bytes 786440 | tf_op jit(solution)/shard_map/ppermute | solution.py:451
  166.4 16.1 %collective-permute-start.4 = (bf16[512,256]{1,0:T(8,128)(2,1)}, bf16[512,256]{1,0:T(8,128)(2,1)S(1)}, u32[]{:S(2)}, u32[]{:S(2)}) collective-permute-start(bf16[512,256]{1,0:T(8,128)(2,1)} %get-tuple-element.47), channel_id=1, source_target_pairs={{0,2},{1,3},{2,4},{3,5},{4,6},{5,7},{6,0},{7,1},{8,10},{9,11},{10,... | collective-permute-start | bytes 786440 | tf_op jit(solution)/shard_map/ppermute | solution.py:451
  167.2 18.7 %collective-permute-start.5 = (bf16[512,256]{1,0:T(8,128)(2,1)}, bf16[512,256]{1,0:T(8,128)(2,1)S(1)}, u32[]{:S(2)}, u32[]{:S(2)}) collective-permute-start(bf16[512,256]{1,0:T(8,128)(2,1)} %get-tuple-element.48), channel_id=1, source_target_pairs={{0,4},{1,5},{2,6},{3,7},{4,0},{5,1},{6,2},{7,3},{8,12},{9,13},{10,... | collective-permute-start | bytes 786440 | tf_op jit(solution)/shard_map/ppermute | solution.py:451
  171.4 14.5 %collective-permute-start.6 = (bf16[512,256]{1,0:T(8,128)(2,1)}, bf16[512,256]{1,0:T(8,128)(2,1)S(1)}, u32[]{:S(2)}, u32[]{:S(2)}) collective-permute-start(bf16[512,256]{1,0:T(8,128)(2,1)} %get-tuple-element.49), channel_id=1, source_target_pairs={{0,6},{1,7},{2,0},{3,1},{4,2},{5,3},{6,4},{7,5},{8,14},{9,15},{10,... | collective-permute-start | bytes 786440 | tf_op jit(solution)/shard_map/ppermute | solution.py:451
  189.3 61.7 %all-to-all-start.2 = ((bf16[32,16,8,256]{3,2,1,0:T(8,128)(2,1)}), bf16[32,16,8,256]{3,2,1,0:T(8,128)(2,1)}, u32[]{:S(2)}, u32[]{:S(2)}) async-start(bf16[32,16,8,256]{3,2,1,0:T(8,128)(2,1)} %bitcast.25), calls=%async_computation.2 | async-start | bytes 4194304 | tf_op jit(solution)/shard_map/all_to_all | solution.py:437
  255.0 92.8 %all-to-all-start.3 = ((bf16[32,16,8,256]{3,2,1,0:T(8,128)(2,1)}), bf16[32,16,8,256]{3,2,1,0:T(8,128)(2,1)}, u32[]{:S(2)}, u32[]{:S(2)}) async-start(bf16[32,16,8,256]{3,2,1,0:T(8,128)(2,1)} %left.3), calls=%async_computation.3 | async-start | bytes 4194304 | tf_op jit(solution)/shard_map/all_to_all | solution.py:437
  265.3 14.2 %collective-permute-start.26 = (bf16[512,256]{1,0:T(8,128)(2,1)}, bf16[512,256]{1,0:T(8,128)(2,1)S(1)}, u32[]{:S(2)}, u32[]{:S(2)}) collective-permute-start(bf16[512,256]{1,0:T(8,128)(2,1)} %get-tuple-element.76), channel_id=1, source_target_pairs={{0,4},{1,5},{2,6},{3,7},{4,0},{5,1},{6,2},{7,3},{8,12},{9,13},{10,... | collective-permute-start | bytes 786440 | tf_op jit(solution)/shard_map/ppermute | solution.py:451
  267.4 12.5 %collective-permute-start.27 = (bf16[512,256]{1,0:T(8,128)(2,1)}, bf16[512,256]{1,0:T(8,128)(2,1)S(1)}, u32[]{:S(2)}, u32[]{:S(2)}) collective-permute-start(bf16[512,256]{1,0:T(8,128)(2,1)} %get-tuple-element.77), channel_id=1, source_target_pairs={{0,6},{1,7},{2,0},{3,1},{4,2},{5,3},{6,4},{7,5},{8,14},{9,15},{10,... | collective-permute-start | bytes 786440 | tf_op jit(solution)/shard_map/ppermute | solution.py:451
  272.0 14.4 %collective-permute-start.15 = (bf16[512,256]{1,0:T(8,128)(2,1)}, bf16[512,256]{1,0:T(8,128)(2,1)S(1)}, u32[]{:S(2)}, u32[]{:S(2)}) collective-permute-start(bf16[512,256]{1,0:T(8,128)(2,1)} %get-tuple-element.67), channel_id=1, source_target_pairs={{0,2},{1,3},{2,4},{3,5},{4,6},{5,7},{6,0},{7,1},{8,10},{9,11},{10,... | collective-permute-start | bytes 786440 | tf_op jit(solution)/shard_map/ppermute | solution.py:451
  272.0 18.8 %collective-permute-start.16 = (bf16[512,256]{1,0:T(8,128)(2,1)}, bf16[512,256]{1,0:T(8,128)(2,1)S(1)}, u32[]{:S(2)}, u32[]{:S(2)}) collective-permute-start(bf16[512,256]{1,0:T(8,128)(2,1)} %get-tuple-element.68), channel_id=1, source_target_pairs={{0,4},{1,5},{2,6},{3,7},{4,0},{5,1},{6,2},{7,3},{8,12},{9,13},{10,... | collective-permute-start | bytes 786440 | tf_op jit(solution)/shard_map/ppermute | solution.py:451
  273.6 17.2 %collective-permute-start.17 = (bf16[512,256]{1,0:T(8,128)(2,1)}, bf16[512,256]{1,0:T(8,128)(2,1)S(1)}, u32[]{:S(2)}, u32[]{:S(2)}) collective-permute-start(bf16[512,256]{1,0:T(8,128)(2,1)} %get-tuple-element.69), channel_id=1, source_target_pairs={{0,6},{1,7},{2,0},{3,1},{4,2},{5,3},{6,4},{7,5},{8,14},{9,15},{10,... | collective-permute-start | bytes 786440 | tf_op jit(solution)/shard_map/ppermute | solution.py:451
  279.5 16.3 %collective-permute-start.14 = (bf16[256,512]{1,0:T(8,128)(2,1)S(1)}, bf16[256,512]{1,0:T(8,128)(2,1)S(1)}, u32[]{:S(2)}, u32[]{:S(2)}) collective-permute-start(bf16[256,512]{1,0:T(8,128)(2,1)S(1)} %copy-done.4), channel_id=1, source_target_pairs={{0,1},{1,0},{2,3},{3,2},{4,5},{5,4},{6,7},{7,6},{8,9},{9,8},{10,11... | collective-permute-start | bytes 786440 | tf_op jit(solution)/shard_map/ppermute | solution.py:447
  282.5 15.2 %collective-permute-start.30 = (bf16[512,256]{1,0:T(8,128)(2,1)}, bf16[512,256]{1,0:T(8,128)(2,1)S(1)}, u32[]{:S(2)}, u32[]{:S(2)}) collective-permute-start(bf16[512,256]{1,0:T(8,128)(2,1)} %get-tuple-element.80), channel_id=1, source_target_pairs={{0,2},{1,3},{2,4},{3,5},{4,6},{5,7},{6,0},{7,1},{8,10},{9,11},{10,... | collective-permute-start | bytes 786440 | tf_op jit(solution)/shard_map/ppermute | solution.py:451
  286.4 12.1 %collective-permute-start.31 = (bf16[512,256]{1,0:T(8,128)(2,1)}, bf16[512,256]{1,0:T(8,128)(2,1)S(1)}, u32[]{:S(2)}, u32[]{:S(2)}) collective-permute-start(bf16[512,256]{1,0:T(8,128)(2,1)} %get-tuple-element.81), channel_id=1, source_target_pairs={{0,6},{1,7},{2,0},{3,1},{4,2},{5,3},{6,4},{7,5},{8,14},{9,15},{10,... | collective-permute-start | bytes 786440 | tf_op jit(solution)/shard_map/ppermute | solution.py:451
  290.8 13.8 %collective-permute-start.32 = (bf16[512,256]{1,0:T(8,128)(2,1)}, bf16[512,256]{1,0:T(8,128)(2,1)S(1)}, u32[]{:S(2)}, u32[]{:S(2)}) collective-permute-start(bf16[512,256]{1,0:T(8,128)(2,1)} %get-tuple-element.79.refs_0_), channel_id=1, source_target_pairs={{0,1},{1,0},{2,3},{3,2},{4,5},{5,4},{6,7},{7,6},{8,9},{9,8},{10,11... | collective-permute-start | bytes 786440 | tf_op jit(solution)/shard_map/ppermute | solution.py:447
  290.9 15.2 %collective-permute-start.28 = (bf16[512,256]{1,0:T(8,128)(2,1)}, bf16[512,256]{1,0:T(8,128)(2,1)S(1)}, u32[]{:S(2)}, u32[]{:S(2)}) collective-permute-start(bf16[512,256]{1,0:T(8,128)(2,1)} %get-tuple-element.78), channel_id=1, source_target_pairs={{0,4},{1,5},{2,6},{3,7},{4,0},{5,1},{6,2},{7,3},{8,12},{9,13},{10,... | collective-permute-start | bytes 786440 | tf_op jit(solution)/shard_map/ppermute | solution.py:451
  295.8 12.2 %collective-permute-start.18 = (bf16[512,256]{1,0:T(8,128)(2,1)}, bf16[512,256]{1,0:T(8,128)(2,1)S(1)}, u32[]{:S(2)}, u32[]{:S(2)}) collective-permute-start(bf16[512,256]{1,0:T(8,128)(2,1)} %get-tuple-element.71), channel_id=1, source_target_pairs={{0,2},{1,3},{2,4},{3,5},{4,6},{5,7},{6,0},{7,1},{8,10},{9,11},{10,... | collective-permute-start | bytes 786440 | tf_op jit(solution)/shard_map/ppermute | solution.py:451
  298.5 14.3 %collective-permute-start.20 = (bf16[512,256]{1,0:T(8,128)(2,1)}, bf16[512,256]{1,0:T(8,128)(2,1)S(1)}, u32[]{:S(2)}, u32[]{:S(2)}) collective-permute-start(bf16[512,256]{1,0:T(8,128)(2,1)} %get-tuple-element.73), channel_id=1, source_target_pairs={{0,4},{1,5},{2,6},{3,7},{4,0},{5,1},{6,2},{7,3},{8,12},{9,13},{10,... | collective-permute-start | bytes 786440 | tf_op jit(solution)/shard_map/ppermute | solution.py:451
  308.0 18.7 %collective-permute-start.29 = (bf16[512,256]{1,0:T(8,128)(2,1)S(1)}, bf16[512,256]{1,0:T(8,128)(2,1)S(1)}, u32[]{:S(2)}, u32[]{:S(2)}) collective-permute-start(bf16[512,256]{1,0:T(8,128)(2,1)S(1)} %collective-permute-done.28.refs_0_), channel_id=1, source_target_pairs={{0,1},{1,0},{2,3},{3,2},{4,5},{5,4},{6,7},{7,6},{8,9},{9,8},{10,11... | collective-permute-start | bytes 786440 | tf_op jit(solution)/shard_map/ppermute | solution.py:447
  308.0 20.7 %collective-permute-start.21 = (bf16[512,256]{1,0:T(8,128)(2,1)}, bf16[512,256]{1,0:T(8,128)(2,1)S(1)}, u32[]{:S(2)}, u32[]{:S(2)}) collective-permute-start(bf16[512,256]{1,0:T(8,128)(2,1)} %get-tuple-element.70.refs_0_), channel_id=1, source_target_pairs={{0,1},{1,0},{2,3},{3,2},{4,5},{5,4},{6,7},{7,6},{8,9},{9,8},{10,11... | collective-permute-start | bytes 786440 | tf_op jit(solution)/shard_map/ppermute | solution.py:447
  312.8 20.6 %collective-permute-start.22 = (bf16[512,256]{1,0:T(8,128)(2,1)S(1)}, bf16[512,256]{1,0:T(8,128)(2,1)S(1)}, u32[]{:S(2)}, u32[]{:S(2)}) collective-permute-start(bf16[512,256]{1,0:T(8,128)(2,1)S(1)} %collective-permute-done.18.refs_1_), channel_id=1, source_target_pairs={{0,1},{1,0},{2,3},{3,2},{4,5},{5,4},{6,7},{7,6},{8,9},{9,8},{10,11... | collective-permute-start | bytes 786440 | tf_op jit(solution)/shard_map/ppermute | solution.py:447
  312.8 26.3 %collective-permute-start.23 = (bf16[512,256]{1,0:T(8,128)(2,1)S(1)}, bf16[512,256]{1,0:T(8,128)(2,1)S(1)}, u32[]{:S(2)}, u32[]{:S(2)}) collective-permute-start(bf16[512,256]{1,0:T(8,128)(2,1)S(1)} %collective-permute-done.19.refs_2_), channel_id=1, source_target_pairs={{0,1},{1,0},{2,3},{3,2},{4,5},{5,4},{6,7},{7,6},{8,9},{9,8},{10,11... | collective-permute-start | bytes 786440 | tf_op jit(solution)/shard_map/ppermute | solution.py:447
  316.6 28.1 %collective-permute-start.24 = (bf16[512,256]{1,0:T(8,128)(2,1)S(1)}, bf16[512,256]{1,0:T(8,128)(2,1)S(1)}, u32[]{:S(2)}, u32[]{:S(2)}) collective-permute-start(bf16[512,256]{1,0:T(8,128)(2,1)S(1)} %collective-permute-done.20.refs_3_), channel_id=1, source_target_pairs={{0,1},{1,0},{2,3},{3,2},{4,5},{5,4},{6,7},{7,6},{8,9},{9,8},{10,11... | collective-permute-start | bytes 786440 | tf_op jit(solution)/shard_map/ppermute | solution.py:447
  (19 other events, 347.9 us)
